TPU v7x, 128 devices: a whole 4x4x4 slice. The times are simulated.
128 devices in a mesh: dp: 8 (over y_lo, x), zero: 16 (over z, y_hi, core).
Axes of the slice: x: 4, y: 4 (y_hi: 2, y_lo: 2; y = y_hi * 2 + y_lo), z: 4, core: 2. Of those that a mesh axis runs over, the one named last changes fastest.
Arguments:
- tokens: bfloat16 [16384, 1024], P(('dp', 'zero')), may hold values from -24 to 24
- cotangent: bfloat16 [16384, 1024], P(('dp', 'zero')), may hold values from -6 to 6
- segments: int32 [128, 128], P(('dp', 'zero')), may hold values from 0 to 3, never falling along the last dimension, each value on 1 to 64 neighbouring positions
- w_qkv: float32 [1024, 3072], P('zero'), may hold values from -0.1875 to 0.1875
- w_out: float32 [1024, 1024], P('zero'), may hold values from -0.75 to 0.75
- w_fc: float32 [1024, 4096], P('zero'), may hold values from -0.1875 to 0.1875
- w_proj: float32 [4096, 1024], P('zero'), may hold values from -0.09375 to 0.09375
- vectors: float32 [12, 1024], P(None, 'zero'), may hold values from -1.2 to 1.6, as said below
- mean_qkv: float32 [1024, 3072], P('zero'), may hold values from -0.6 to 0.6
- mean_out: float32 [1024, 1024], P('zero'), may hold values from -0.6 to 0.6
- mean_fc: float32 [1024, 4096], P('zero'), may hold values from -0.6 to 0.6
- mean_proj: float32 [4096, 1024], P('zero'), may hold values from -0.6 to 0.6
- mean_vectors: float32 [12, 1024], P(None, 'zero'), may hold values from -0.6 to 0.6
- square_qkv: float32 [1024, 3072], P('zero'), may hold values from 1e-05 to 0.001
- square_out: float32 [1024, 1024], P('zero'), may hold values from 1e-05 to 0.001
- square_fc: float32 [1024, 4096], P('zero'), may hold values from 1e-05 to 0.001
- square_proj: float32 [4096, 1024], P('zero'), may hold values from 1e-05 to 0.001
- square_vectors: float32 [12, 1024], P(None, 'zero'), may hold values from 1e-05 to 0.001
Outputs:
- block_out: bfloat16 [16384, 1024], P(('dp', 'zero'))
- input_grad: bfloat16 [16384, 1024], P(('dp', 'zero'))
- grad_qkv: float32 [1024, 3072], P('zero')
- grad_out: float32 [1024, 1024], P('zero')
- grad_fc: float32 [1024, 4096], P('zero')
- grad_proj: float32 [4096, 1024], P('zero')
- grad_vectors: float32 [12, 1024], P(None, 'zero')
- next_qkv: float32 [1024, 3072], P('zero')
- next_out: float32 [1024, 1024], P('zero')
- next_fc: float32 [1024, 4096], P('zero')
- next_proj: float32 [4096, 1024], P('zero')
- next_vectors: float32 [12, 1024], P(None, 'zero')
- next_mean_qkv: float32 [1024, 3072], P('zero')
- next_mean_out: float32 [1024, 1024], P('zero')
- next_mean_fc: float32 [1024, 4096], P('zero')
- next_mean_proj: float32 [4096, 1024], P('zero')
- next_mean_vectors: float32 [12, 1024], P(None, 'zero')
- next_square_qkv: float32 [1024, 3072], P('zero')
- next_square_out: float32 [1024, 1024], P('zero')
- next_square_fc: float32 [1024, 4096], P('zero')
- next_square_proj: float32 [4096, 1024], P('zero')
- next_square_vectors: float32 [12, 1024], P(None, 'zero')
Inputs may be any that keep to these rules, and one draw needn't show every extreme that they name: `segments`: in each row of 128 tokens the segment numbers never fall; each of the 4 documents of a row has 1 to 64 tokens, and one has exactly 64. `vectors`: rows 0 and 5 lie within 0.4 to 1.6; the other rows within -1.2 to 1.2.
All inputs are finite; a program needn't handle non-finite values.
Results may differ from a plain program's by a relative error of at most 0.04.
Values may be sent and summed in bfloat16 or wider, within the bound.
A program may use at most 192 MiB of HBM per device.

v0:
```python
from functools import partial

import jax
import jax.numpy as jnp
from jax import lax
from jax.sharding import PartitionSpec as P

HEADS = 16
SEQ = 128
ADAM_STEP = 3
LANE = 128


eps_norm = 1e-05
beta_first = 0.9
beta_second = 0.999
eps_adam = 1e-08
rate_matrix = 0.02
rate_vector = 0.15
decay_matrix = 0.1


def sent_together(arrays, axis, dim, along):
    widths = [a.shape[along] for a in arrays]
    both = jnp.concatenate(arrays, axis=along)
    result = lax.all_gather(both, axis, axis=dim, tiled=True)
    return tuple(jnp.split(result, [sum(widths[:k]) for k in range(1, len(widths))], axis=along))


def in_one_piece(arrays, axis, dim, along):
    ends, at = ([], 0)
    for a in arrays[:-1]:
        at += a.shape[along]
        ends.append(at)
    both = jnp.concatenate(arrays, axis=along)
    return tuple(
        jnp.split(lax.psum_scatter(both, axis, scatter_dimension=dim, tiled=True), ends, axis=along)
    )


def gelu_tanh(inputs):
    inner = 0.7978845608028654 * (inputs + 0.044715 * inputs * inputs * inputs)
    return 0.5 * inputs * (1.0 + jnp.tanh(inner))


def layer_norm(inputs, gain_row, bias_row):
    average = jnp.mean(inputs, axis=-1, keepdims=True)
    centred = inputs - average
    variance = jnp.mean(centred * centred, axis=-1, keepdims=True)
    return centred * lax.rsqrt(variance + eps_norm) * gain_row + bias_row


def allowed_mask(seg_rows):
    length = seg_rows.shape[1]
    places = lax.iota(jnp.int32, length)
    causal = places[:, None] >= places[None, :]
    same_doc = seg_rows[:, :, None] == seg_rows[:, None, :]
    return jnp.logical_and(same_doc, causal[None])[:, None]


def attend_scores(queries, keys_in, seg_rows):
    scaling = queries.shape[-1] ** (-0.5)
    scores = (
        jnp.einsum("rqhe,rkhe->rhqk", queries, keys_in, preferred_element_type=jnp.float32)
        * scaling
    )
    return (scores, allowed_mask(seg_rows), scaling)


def attention_forward(queries, keys_in, values, seg_rows):
    scores, allowed, scaling = attend_scores(queries, keys_in, seg_rows)
    exponent = jnp.where(allowed, jnp.exp(scores), 0.0)
    log_total = jnp.log(jnp.sum(exponent, axis=-1, keepdims=True))
    attn_weights = jnp.where(allowed, jnp.exp(scores - log_total), 0.0).astype(jnp.bfloat16)
    attended = jnp.einsum(
        "rhqk,rkhe->rqhe", attn_weights, values, preferred_element_type=jnp.float32
    )
    return (attended.astype(jnp.bfloat16), log_total)


def attention_backward(queries, keys_in, values, seg_rows, log_total, grad_att):
    scores, allowed, scaling = attend_scores(queries, keys_in, seg_rows)
    weights_full = jnp.where(allowed, jnp.exp(scores - log_total), 0.0)
    weights_half = weights_full.astype(jnp.bfloat16)
    grad_values = jnp.einsum(
        "rhqk,rqhe->rkhe", weights_half, grad_att, preferred_element_type=jnp.float32
    )
    grad_weights = jnp.einsum(
        "rqhe,rkhe->rhqk", grad_att, values, preferred_element_type=jnp.float32
    )
    row_dot = jnp.sum(weights_full * grad_weights, axis=-1, keepdims=True)
    grad_scores = (weights_full * (grad_weights - row_dot) * scaling).astype(jnp.bfloat16)
    grad_queries = jnp.einsum(
        "rhqk,rkhe->rqhe", grad_scores, keys_in, preferred_element_type=jnp.float32
    )
    grad_keys = jnp.einsum(
        "rhqk,rqhe->rkhe", grad_scores, queries, preferred_element_type=jnp.float32
    )
    return (grad_queries, grad_keys, grad_values)


def block_pass(tokens_in, cot_in, seg_rows, qkv_mat, out_mat, fc_mat, proj_mat, vec_rows):
    count_tok = tokens_in.shape[0]
    width = tokens_in.shape[1]
    head_width = width // HEADS
    row_count = count_tok // SEQ
    split_shape = (row_count, SEQ, HEADS, head_width)
    tokens32 = tokens_in.astype(jnp.float32)
    normed_one = layer_norm(tokens32, vec_rows[0], vec_rows[1]).astype(jnp.bfloat16)
    projected = jnp.dot(normed_one, qkv_mat, preferred_element_type=jnp.float32)
    queries = (projected[:, :width] + vec_rows[2]).astype(jnp.bfloat16).reshape(split_shape)
    keys_in = projected[:, width : 2 * width].astype(jnp.bfloat16).reshape(split_shape)
    values = (projected[:, 2 * width :] + vec_rows[3]).astype(jnp.bfloat16).reshape(split_shape)
    attended, log_total = attention_forward(queries, keys_in, values, seg_rows)
    attended = attended.reshape(count_tok, width)
    middle = tokens32 + jnp.dot(attended, out_mat, preferred_element_type=jnp.float32) + vec_rows[4]
    normed_two = layer_norm(middle, vec_rows[5], vec_rows[6]).astype(jnp.bfloat16)
    fc_bias = vec_rows[8:].reshape(-1)
    hidden_pre = jnp.dot(normed_two, fc_mat, preferred_element_type=jnp.float32) + fc_bias
    hidden = gelu_tanh(hidden_pre).astype(jnp.bfloat16)
    block_out = (
        middle + jnp.dot(hidden, proj_mat, preferred_element_type=jnp.float32) + vec_rows[7]
    ).astype(jnp.bfloat16)
    cot32 = cot_in.astype(jnp.float32)
    grad_proj = jnp.dot(hidden.T, cot_in, preferred_element_type=jnp.float32)
    grad_hidden = jnp.dot(cot_in, proj_mat.T, preferred_element_type=jnp.float32)
    gelu_back = jax.vjp(gelu_tanh, hidden_pre)[1]
    grad_pre = gelu_back(grad_hidden)[0]
    grad_pre_half = grad_pre.astype(jnp.bfloat16)
    grad_fc = jnp.dot(normed_two.T, grad_pre_half, preferred_element_type=jnp.float32)
    grad_normed_two = jnp.dot(grad_pre_half, fc_mat.T, preferred_element_type=jnp.float32)
    norm_two_back = jax.vjp(layer_norm, middle, vec_rows[5], vec_rows[6])[1]
    grad_mid_norm, grad_gain_two, grad_bias_two = norm_two_back(grad_normed_two)
    grad_middle = cot32 + grad_mid_norm
    grad_middle_half = grad_middle.astype(jnp.bfloat16)
    grad_out = jnp.dot(attended.T, grad_middle_half, preferred_element_type=jnp.float32)
    grad_attended = jnp.dot(grad_middle_half, out_mat.T, preferred_element_type=jnp.float32)
    grad_attended = grad_attended.astype(jnp.bfloat16).reshape(split_shape)
    grad_queries, grad_keys, grad_values = attention_backward(
        queries, keys_in, values, seg_rows, log_total, grad_attended
    )
    flat_queries = grad_queries.reshape(count_tok, width)
    flat_keys = grad_keys.reshape(count_tok, width)
    flat_values = grad_values.reshape(count_tok, width)
    grad_projected = jnp.concatenate([flat_queries, flat_keys, flat_values], axis=1).astype(
        jnp.bfloat16
    )
    grad_qkv = jnp.dot(normed_one.T, grad_projected, preferred_element_type=jnp.float32)
    grad_normed_one = jnp.dot(grad_projected, qkv_mat.T, preferred_element_type=jnp.float32)
    norm_one_back = jax.vjp(layer_norm, tokens32, vec_rows[0], vec_rows[1])[1]
    grad_tok_norm, grad_gain_one, grad_bias_one = norm_one_back(grad_normed_one)
    input_grad = (grad_middle + grad_tok_norm).astype(jnp.bfloat16)
    small_rows = jnp.stack(
        [
            grad_gain_one,
            grad_bias_one,
            jnp.sum(flat_queries, axis=0),
            jnp.sum(flat_values, axis=0),
            jnp.sum(grad_middle, axis=0),
            grad_gain_two,
            grad_bias_two,
            jnp.sum(cot32, axis=0),
        ]
    )
    grad_vec = jnp.concatenate([small_rows, jnp.sum(grad_pre, axis=0).reshape(-1, width)], axis=0)
    return (block_out, input_grad, (grad_qkv, grad_out, grad_fc, grad_proj, grad_vec))


def adam_step(weight, gradient, mean_old, square_old, rate, decay):
    mean_new = beta_first * mean_old + (1.0 - beta_first) * gradient
    square_new = beta_second * square_old + (1.0 - beta_second) * gradient * gradient
    mean_hat = mean_new / (1.0 - beta_first**ADAM_STEP)
    square_hat = square_new / (1.0 - beta_second**ADAM_STEP)
    weight_new = weight - rate * (mean_hat / (jnp.sqrt(square_hat) + eps_adam) + decay * weight)
    return (weight_new, mean_new, square_new)


def local(
    tokens,
    cotangent,
    segments,
    w_qkv,
    w_out,
    w_fc,
    w_proj,
    vectors,
    mean_qkv,
    mean_out,
    mean_fc,
    mean_proj,
    mean_vectors,
    square_qkv,
    square_out,
    square_fc,
    square_proj,
    square_vectors,
):
    dp_size = lax.axis_size("dp")
    zero_size = lax.axis_size("zero")
    replicas = dp_size * zero_size
    vec_cols = jnp.pad(vectors.astype(jnp.bfloat16).T, ((0, 0), (0, LANE - vectors.shape[0])))
    qkv_mat, out_mat, fc_mat, vec_cols_all = sent_together(
        (
            w_qkv.astype(jnp.bfloat16),
            w_out.astype(jnp.bfloat16),
            w_fc.astype(jnp.bfloat16),
            vec_cols,
        ),
        "zero",
        0,
        1,
    )
    proj_mat = lax.all_gather(w_proj.astype(jnp.bfloat16), "zero", axis=0, tiled=True)
    vec_rows = vec_cols_all[:, : vectors.shape[0]].T.astype(jnp.float32)
    block_out, input_grad, local_grads = block_pass(
        tokens, cotangent, segments, qkv_mat, out_mat, fc_mat, proj_mat, vec_rows
    )
    grad_vec_cols = jnp.pad(
        local_grads[4].astype(jnp.bfloat16).T, ((0, 0), (0, LANE - vectors.shape[0]))
    )
    joined = jnp.concatenate(
        (
            local_grads[0].astype(jnp.bfloat16),
            local_grads[1].astype(jnp.bfloat16),
            local_grads[2].astype(jnp.bfloat16),
            grad_vec_cols,
        ),
        axis=1,
    )
    scattered = lax.psum_scatter(joined, "zero", scatter_dimension=0, tiled=True)
    proj_scattered = lax.psum_scatter(
        local_grads[3].astype(jnp.bfloat16), "zero", scatter_dimension=0, tiled=True
    )
    summed_joined, summed_proj = lax.psum((scattered, proj_scattered), "dp")
    ends = [w_qkv.shape[1], w_qkv.shape[1] + w_out.shape[1], w_qkv.shape[1] + w_out.shape[1] + w_fc.shape[1]]
    g_qkv, g_out, g_fc, g_vec = jnp.split(summed_joined, ends, axis=1)
    summed = (
        g_qkv.astype(jnp.float32),
        g_out.astype(jnp.float32),
        g_fc.astype(jnp.float32),
        summed_proj.astype(jnp.float32),
        lax.dot_general(
            g_vec[:, : vectors.shape[0]],
            jnp.eye(g_vec.shape[0], dtype=jnp.bfloat16),
            (((0,), (0,)), ((), ())),
            preferred_element_type=jnp.float32,
        ),
    )
    grads = jax.tree.map(partial(jnp.multiply, 1.0 / replicas), summed)
    first = adam_step(w_qkv, grads[0], mean_qkv, square_qkv, rate_matrix, decay_matrix)
    second = adam_step(w_out, grads[1], mean_out, square_out, rate_matrix, decay_matrix)
    third = adam_step(w_fc, grads[2], mean_fc, square_fc, rate_matrix, decay_matrix)
    fourth = adam_step(w_proj, grads[3], mean_proj, square_proj, rate_matrix, decay_matrix)
    fifth = adam_step(vectors, grads[4], mean_vectors, square_vectors, rate_vector, 0.0)
    return (
        block_out,
        input_grad,
        grads[0],
        grads[1],
        grads[2],
        grads[3],
        grads[4],
        first[0],
        second[0],
        third[0],
        fourth[0],
        fifth[0],
        first[1],
        second[1],
        third[1],
        fourth[1],
        fifth[1],
        first[2],
        second[2],
        third[2],
        fourth[2],
        fifth[2],
    )


def solution(mesh):
    placed = (
        P(("dp", "zero"), None),
        P(("dp", "zero"), None),
        P(("dp", "zero"), None),
        P("zero", None),
        P("zero", None),
        P("zero", None),
        P("zero", None),
        P(None, "zero"),
        P("zero", None),
        P("zero", None),
        P("zero", None),
        P("zero", None),
        P(None, "zero"),
        P("zero", None),
        P("zero", None),
        P("zero", None),
        P("zero", None),
        P(None, "zero"),
    )
    return jax.shard_map(
        local,
        mesh=mesh,
        in_specs=placed,
        out_specs=(
            P(("dp", "zero"), None),
            P(("dp", "zero"), None),
            P("zero", None),
            P("zero", None),
            P("zero", None),
            P("zero", None),
            P(None, "zero"),
            P("zero", None),
            P("zero", None),
            P("zero", None),
            P("zero", None),
            P(None, "zero"),
            P("zero", None),
            P("zero", None),
            P("zero", None),
            P("zero", None),
            P(None, "zero"),
            P("zero", None),
            P("zero", None),
            P("zero", None),
            P("zero", None),
            P(None, "zero"),
        ),
        check_vma=False,
    )
```

profile of v0, /device:TPU:4, one launch (start us, length us, event | category | flops | bytes accessed | tf_op | source)
XLA Modules:
  0.0 572.3 jit_solution(10156674104917763068)
XLA Ops:
  7.2 0.0 all-gather.5.cloned.1.call-start
  7.3 2.2 convert_element_type.123
  9.5 0.0 all-gather.3.cloned.1.call-start
  9.6 0.1 copy.90
  9.8 0.1 convert_element_type.110
  9.9 1.1 fusion.46
  11.0 0.0 reduce-scatter.5.cloned.1.call-start
  11.1 0.1 convert_reduce_fusion
  11.2 0.2 fusion.71
  11.4 0.1 fusion.88
  11.5 75.1 %all-gather.5.cloned.1.call-done = bf16[4096,1024]{1,0:T(8,128)(2,1)} async-done(((bf16[256,1024]{1,0:T(8,128)(2,1)}), bf16[4096,1024]{1,0:T(8,128)(2,1)}) %all-gather.5.cloned.1.call-update) | async-done | bytes 8388624 | tf_op jit(solution)/shard_map/all_gather | solution.py:213
  86.6 7.6 %fusion.127 = f32[128,4096]{1,0:T(8,128)} fusion(bf16[128,1024]{1,0:T(8,128)(2,1)S(1)} %copy-done.1, bf16[4096,1024]{1,0:T(8,128)(2,1)} %all-gather.5.cloned.1.call-done), kind=kOutput, calls=%fused_computation.171 | convolution fusion | flops 1073741824 | bytes 10747904 | tf_op jit(solution)/shard_map/dot_general | solution.py:126
  94.2 103.2 %all-gather.3.cloned.1.call-done = bf16[1024,8320]{1,0:T(8,128)(2,1)} async-done(((bf16[64,8320]{1,0:T(8,128)(2,1)}), bf16[1024,8320]{1,0:T(8,128)(2,1)}) %all-gather.3.cloned.1.call-update) | async-done | bytes 17039376 | tf_op jit(solution)/shard_map/all_gather | solution.py:26
  197.4 1.0 convert_bitcast_fusion
  198.4 2.1 slice_reduce_fusion.2
  200.5 0.2 slice.72
  200.7 0.2 copy.79
  200.9 3.9 fusion.10
  204.8 0.1 fusion.73
  204.9 0.2 copy.76
  205.1 0.2 copy.77
  205.3 0.2 copy.75
  205.5 0.4 convolution_multiply_fusion
  205.9 0.5 convolution_convert_fusion.5
  206.4 2.3 fusion.124
  208.7 0.2 multiply_reduce_fusion.3
  208.9 5.6 fusion.119
  214.5 1.3 copy-done.2
  215.8 5.6 convolution_convert_fusion
  221.5 0.2 reduce-scatter.3.cloned.1.call-start
  221.7 0.1 reduce.6
  221.8 6.4 %multiply_reduce_fusion.1 = (bf16[1024]{0:T(1024)(128)(2,1)S(1)}, f32[128]{0:T(128)S(1)}, bf16[1024]{0:T(1024)(128)(2,1)S(1)}, f32[128,1024]{1,0:T(8,128)S(1)}) fusion(f32[128,1024]{1,0:T(8,128)S(1)} %get-tuple-element.72, f32[128]{0:T(128)S(1)} %fusion.99, f32[128]{0:T(128)S(1)} %broadcast_multiply_fusion.1, f32[1024]{0:T(1024)S(1)} %get-tuple-element.29, ...), kind=kOutput, calls=%fused_computation.110 | convolution fusion | flops 1074788224 | bytes 10495488 | tf_op jit(solution)/shard_map/dot_general | solution.py:131
  228.3 0.3 fusion.121
  228.5 2.7 fusion.43
  231.2 0.8 copy.80
  232.1 2.2 fusion.122
  234.2 0.1 stack.25
  234.3 2.3 fusion.128
  236.7 1.3 fusion.33
  238.0 3.1 fusion.123
  241.1 0.1 stack.24
  241.2 3.1 convolution_convert_fusion.4
  244.4 5.2 fusion.110
  249.6 0.3 fusion.70
  250.0 1.0 fusion.107
  251.0 0.1 concatenate.16
  251.1 0.2 copy.84
  251.3 2.2 convolution_convert_fusion.3
  253.5 3.0 copy.85
  256.5 3.2 convolution_convert_fusion.2
  259.7 2.5 convolution_convert_fusion.1
  262.1 6.7 %fusion.3 = bf16[1024,8320]{1,0:T(8,128)(2,1)} fusion(bf16[1024,12]{1,0:T(8,128)(2,1)S(1)} %bitcast.50, bf16[1024,4096]{1,0:T(8,128)(2,1)S(1)} %convolution_convert_fusion.1, bf16[1024,1024]{1,0:T(8,128)(2,1)S(1)} %copy.85, bf16[1024,3072]{1,0:T(8,128)(2,1)S(1)} %convolution_convert_fusion.2), kind=kLoop, calls=%fused_computation.4 | loop fusion | flops 85196800 | bytes 33841152 | tf_op jit(solution)/shard_map/concatenate | solution.py:221
  268.8 0.0 all-reduce.5.cloned.1.call-start
  268.9 52.8 %reduce-scatter.5.cloned.1.call-done = bf16[256,1024]{1,0:T(8,128)(2,1)} async-done(((bf16[4096,1024]{1,0:T(8,128)(2,1)}), bf16[256,1024]{1,0:T(8,128)(2,1)}) %reduce-scatter.5.cloned.1.call-update) | async-done | bytes 524304 | tf_op jit(solution)/shard_map/reduce_scatter | solution.py:231
  321.6 151.3 %reduce-scatter.3.cloned.1.call-done = bf16[64,8320]{1,0:T(8,128)(2,1)} async-done(((bf16[1024,8320]{1,0:T(8,128)(2,1)}), bf16[64,8320]{1,0:T(8,128)(2,1)}) %reduce-scatter.3.cloned.1.call-update) | async-done | bytes 1064976 | tf_op jit(solution)/shard_map/reduce_scatter | solution.py:230
  473.0 5.7 fusion.42
  478.6 73.5 %all-reduce.5.cloned.1.call-done = (bf16[64,8320]{1,0:T(8,128)(2,1)}, bf16[256,1024]{1,0:T(8,128)(2,1)}) async-done(((bf16[64,8320]{1,0:T(8,128)(2,1)}, bf16[256,1024]{1,0:T(8,128)(2,1)}), (bf16[64,8320]{1,0:T(8,128)(2,1)}, bf16[256,1024]{1,0:T(8,128)(2,1)})) %all-reduce.5.cloned.1.call-update) | async-done | bytes 1589264 | tf_op jit(solution)/shard_map/psum | solution.py:234
  552.2 1.6 multiply_subtract_fusion.4
  553.8 2.1 multiply_subtract_fusion.3
  556.0 3.6 multiply_subtract_fusion.2
  559.7 2.6 multiply_subtract_fusion.1
  562.3 0.2 copy-done.13
  562.5 0.5 copy-done.26
  563.1 2.7 multiply_subtract_fusion
  (92 shorter events, 0.5 us)
Async XLA Ops:
  7.2 2.4 copy-start.31
  7.2 2.5 copy-start.16
  7.2 2.5 copy-start.7
  7.2 2.6 copy-start.4
  7.2 79.4 %all-gather.5.cloned.1.call-start = ((), (), s32[]{:S(2)}) async-start(), calls=%async_computation.3 | async-start | bytes 8912896 | tf_op jit(solution)/shard_map/all_gather | solution.py:213
  9.5 187.9 %all-gather.3.cloned.1.call-start = ((), (), s32[]{:S(2)}) async-start(), calls=%async_computation.2 | async-start | bytes 18104320 | tf_op jit(solution)/shard_map/all_gather | solution.py:26
  9.8 1.2 copy-start
  9.9 1.5 copy-start.32
  9.9 76.7 %copy-start.1 = (bf16[128,1024]{1,0:T(8,128)(2,1)S(1)}, bf16[128,1024]{1,0:T(8,128)(2,1)}, u32[]{:S(2)}) copy-start(bf16[128,1024]{1,0:T(8,128)(2,1)} %param.19) | copy-start | bytes 786436
  11.0 310.6 %reduce-scatter.5.cloned.1.call-start = ((), (), s32[]{:S(2)}) async-start(), calls=%async_computation.5 | async-start | bytes 8912896 | tf_op jit(solution)/shard_map/reduce_scatter | solution.py:231
  205.1 1.2 copy-start.17
  205.3 3.4 copy-start.19
  205.5 0.9 copy-start.21
  206.4 2.6 copy-start.23
  206.4 2.5 copy-start.9
  214.5 1.3 copy-start.2
  214.5 7.3 %copy-start.14 = (bf16[128,4096]{1,0:T(8,128)(2,1)}, bf16[128,4096]{1,0:T(8,128)(2,1)S(1)}, u32[]{:S(2)}) copy-start(bf16[128,4096]{1,0:T(8,128)(2,1)S(1)} %get-tuple-element.60) | copy-start | bytes 3145732
  221.5 251.4 %reduce-scatter.3.cloned.1.call-start = ((), (), s32[]{:S(2)}) async-start(), calls=%async_computation.4 | async-start | bytes 18104320 | tf_op jit(solution)/shard_map/reduce_scatter | solution.py:230
  231.2 3.1 copy-start.22
  234.2 3.7 copy-start.20
  236.7 4.5 copy-start.18
  238.0 6.4 %copy-start.28 = (bf16[1,128,16,64]{1,3,2,0:T(8,128)(2,1)S(1)}, bf16[1,128,16,64]{1,3,2,0:T(8,128)(2,1)}, u32[]{:S(2)}) copy-start(bf16[1,128,16,64]{1,3,2,0:T(8,128)(2,1)} %get-tuple-element.68) | copy-start | bytes 786436
  241.1 8.4 %copy-start.29 = (bf16[1,128,16,64]{1,3,2,0:T(8,128)(2,1)}, bf16[1,128,16,64]{1,3,2,0:T(8,128)(2,1)S(1)}, u32[]{:S(2)}) copy-start(bf16[1,128,16,64]{1,3,2,0:T(8,128)(2,1)S(1)} %get-tuple-element.70) | copy-start | bytes 786436
  244.3 5.3 copy-start.30
  249.6 1.7 copy-start.24
  256.5 3.2 copy-start.15
  268.8 204.2 %copy-start.3 = (f32[128,4096]{1,0:T(8,128)S(1)}, f32[128,4096]{1,0:T(8,128)}, u32[]{:S(2)}) copy-start(f32[128,4096]{1,0:T(8,128)} %copy-done.2) | copy-start | bytes 6291460
  268.8 283.4 %all-reduce.5.cloned.1.call-start = ((), (), s32[]{:S(2)}) async-start(), calls=%async_computation.6 | async-start | bytes 3178496 | tf_op jit(solution)/shard_map/psum | solution.py:234
  473.0 79.2 %copy-start.33 = (f32[12,64]{1,0:T(8,128)S(1)}, f32[12,64]{1,0:T(8,128)}, u32[]{:S(2)}) copy-start(f32[12,64]{1,0:T(8,128)} %param.30) | copy-start | bytes 9220
  473.0 79.2 %copy-start.34 = (f32[12,64]{1,0:T(8,128)S(1)}, f32[12,64]{1,0:T(8,128)}, u32[]{:S(2)}) copy-start(f32[12,64]{1,0:T(8,128)} %param.35) | copy-start | bytes 9220
  473.0 80.8 %copy-start.27 = (f32[64,1024]{1,0:T(8,128)S(1)}, f32[64,1024]{1,0:T(8,128)}, u32[]{:S(2)}) copy-start(f32[64,1024]{1,0:T(8,128)} %param.27) | copy-start | bytes 786436
  478.6 77.3 %copy-start.8 = (f32[64,3072]{1,0:T(8,128)S(1)}, f32[64,3072]{1,0:T(8,128)}, u32[]{:S(2)}) copy-start(f32[64,3072]{1,0:T(8,128)} %param.21) | copy-start | bytes 2359300
  552.2 3.7 copy-start.25
  555.9 3.7 copy-start.5
  555.9 3.7 copy-start.10
  556.0 3.7 copy-start.11
  559.6 2.7 copy-start.6
  559.6 2.7 copy-start.12
  559.6 2.9 copy-start.13
  559.7 3.4 copy-start.26
Sparse Core Ops, SparseCore 0:
  11.1 75.4 all-gather.4
  89.1 108.2 all-gather.2
  221.6 99.9 reduce-scatter.4
  325.9 147.0 reduce-scatter.2
  475.6 76.5 all-reduce.4
where the time goes:
time: 575 us; the launch traced here: 572 us
  waiting for transfers between devices  456 us (79%)
  matrix products  65.9 us (11%)
  other arithmetic  25.9 us (5%)
  between operations  14.4 us (3%)
  local copies, waits for them, and re-layouts  9.7 us (2%)
    reduce_scatter x1, waiting for transfers between devices, local(): lax.psum_scatter(joined, 'zero', scatter_dimension=0, tiled=True)  151 us
    all_gather x1, waiting for transfers between devices, sent_together(): result = lax.all_gather(both, axis, axis=dim, tiled=True)  103 us
    all_gather x1, waiting for transfers between devices, local(): lax.all_gather(w_proj.astype(jnp.bfloat16), 'zero', axis=0, tiled=True)  75.1 us
    psum x1, waiting for transfers between devices, local(): summed_joined, summed_proj = lax.psum((scattered, proj_scattered), 'dp')  73.5 us
    reduce_scatter x1, waiting for transfers between devices, local(): lax.psum_scatter(local_grads[3].astype(jnp.bfloat16), 'zero', scatter_dim...  52.8 us
  transfers between devices with their start and end apart: 5, of which 5 were waited for; matrix products, arithmetic and copies ran while one was open for 11% of the time, Pallas kernels for 0%

commit v1 on v0

--- a/solution.py
+++ b/solution.py
@@ -38,6 +38,27 @@
     )
 
 
+def gather_rows(shard):
+    chips = lax.all_gather(shard, "zc", axis=0, tiled=False)
+    both = lax.all_gather(chips, "core", axis=1, tiled=False)
+    return both.reshape((-1,) + shard.shape[1:])
+
+
+def core_major(columns):
+    chips = lax.axis_size("zc")
+    cores = lax.axis_size("core")
+    split = columns.reshape(columns.shape[0], chips, cores, -1)
+    return split.transpose(0, 2, 1, 3).reshape(columns.shape)
+
+
+def scatter_rows(whole):
+    chips = lax.axis_size("zc")
+    cores = lax.axis_size("core")
+    grouped = whole.reshape((cores, chips, whole.shape[0] // (chips * cores)) + whole.shape[1:])
+    on_chip = lax.psum_scatter(grouped, "core", scatter_dimension=0, tiled=False)
+    return lax.psum_scatter(on_chip, "zc", scatter_dimension=0, tiled=False)
+
+
 def gelu_tanh(inputs):
     inner = 0.7978845608028654 * (inputs + 0.044715 * inputs * inputs * inputs)
     return 0.5 * inputs * (1.0 + jnp.tanh(inner))
@@ -99,7 +120,7 @@
     return (grad_queries, grad_keys, grad_values)
 
 
-def block_pass(tokens_in, cot_in, seg_rows, qkv_mat, out_mat, fc_mat, proj_mat, vec_rows):
+def block_pass(tokens_in, cot_in, seg_rows, qkv_mat, out_mat, fc_mat, proj_mat, vec_rows, order):
     count_tok = tokens_in.shape[0]
     width = tokens_in.shape[1]
     head_width = width // HEADS
@@ -122,18 +143,18 @@
         middle + jnp.dot(hidden, proj_mat, preferred_element_type=jnp.float32) + vec_rows[7]
     ).astype(jnp.bfloat16)
     cot32 = cot_in.astype(jnp.float32)
-    grad_proj = jnp.dot(hidden.T, cot_in, preferred_element_type=jnp.float32)
+    grad_proj = jnp.dot(order(hidden).T, cot_in, preferred_element_type=jnp.float32)
     grad_hidden = jnp.dot(cot_in, proj_mat.T, preferred_element_type=jnp.float32)
     gelu_back = jax.vjp(gelu_tanh, hidden_pre)[1]
     grad_pre = gelu_back(grad_hidden)[0]
     grad_pre_half = grad_pre.astype(jnp.bfloat16)
-    grad_fc = jnp.dot(normed_two.T, grad_pre_half, preferred_element_type=jnp.float32)
+    grad_fc = jnp.dot(order(normed_two).T, grad_pre_half, preferred_element_type=jnp.float32)
     grad_normed_two = jnp.dot(grad_pre_half, fc_mat.T, preferred_element_type=jnp.float32)
     norm_two_back = jax.vjp(layer_norm, middle, vec_rows[5], vec_rows[6])[1]
     grad_mid_norm, grad_gain_two, grad_bias_two = norm_two_back(grad_normed_two)
     grad_middle = cot32 + grad_mid_norm
     grad_middle_half = grad_middle.astype(jnp.bfloat16)
-    grad_out = jnp.dot(attended.T, grad_middle_half, preferred_element_type=jnp.float32)
+    grad_out = jnp.dot(order(attended).T, grad_middle_half, preferred_element_type=jnp.float32)
     grad_attended = jnp.dot(grad_middle_half, out_mat.T, preferred_element_type=jnp.float32)
     grad_attended = grad_attended.astype(jnp.bfloat16).reshape(split_shape)
     grad_queries, grad_keys, grad_values = attention_backward(
@@ -145,7 +166,7 @@
     grad_projected = jnp.concatenate([flat_queries, flat_keys, flat_values], axis=1).astype(
         jnp.bfloat16
     )
-    grad_qkv = jnp.dot(normed_one.T, grad_projected, preferred_element_type=jnp.float32)
+    grad_qkv = jnp.dot(order(normed_one).T, grad_projected, preferred_element_type=jnp.float32)
     grad_normed_one = jnp.dot(grad_projected, qkv_mat.T, preferred_element_type=jnp.float32)
     norm_one_back = jax.vjp(layer_norm, tokens32, vec_rows[0], vec_rows[1])[1]
     grad_tok_norm, grad_gain_one, grad_bias_one = norm_one_back(grad_normed_one)
@@ -196,27 +217,31 @@
     square_vectors,
 ):
     dp_size = lax.axis_size("dp")
-    zero_size = lax.axis_size("zero")
+    zero_size = lax.axis_size("zc") * lax.axis_size("core")
     replicas = dp_size * zero_size
     vec_cols = jnp.pad(vectors.astype(jnp.bfloat16).T, ((0, 0), (0, LANE - vectors.shape[0])))
-    qkv_mat, out_mat, fc_mat, vec_cols_all = sent_together(
-        (
-            w_qkv.astype(jnp.bfloat16),
-            w_out.astype(jnp.bfloat16),
-            w_fc.astype(jnp.bfloat16),
-            vec_cols,
+    qkv_mat, out_mat, fc_mat, vec_cols_all = jnp.split(
+        gather_rows(
+            jnp.concatenate(
+                (
+                    w_qkv.astype(jnp.bfloat16),
+                    w_out.astype(jnp.bfloat16),
+                    w_fc.astype(jnp.bfloat16),
+                    vec_cols,
+                ),
+                axis=1,
+            )
         ),
-        "zero",
-        0,
-        1,
-    )
-    proj_mat = lax.all_gather(w_proj.astype(jnp.bfloat16), "zero", axis=0, tiled=True)
+        [w_qkv.shape[1], w_qkv.shape[1] + w_out.shape[1], w_qkv.shape[1] + w_out.shape[1] + w_fc.shape[1]],
+        axis=1,
+    )
+    proj_mat = gather_rows(w_proj.astype(jnp.bfloat16))
     vec_rows = vec_cols_all[:, : vectors.shape[0]].T.astype(jnp.float32)
     block_out, input_grad, local_grads = block_pass(
-        tokens, cotangent, segments, qkv_mat, out_mat, fc_mat, proj_mat, vec_rows
+        tokens, cotangent, segments, qkv_mat, out_mat, fc_mat, proj_mat, vec_rows, core_major
     )
     grad_vec_cols = jnp.pad(
-        local_grads[4].astype(jnp.bfloat16).T, ((0, 0), (0, LANE - vectors.shape[0]))
+        core_major(local_grads[4].astype(jnp.bfloat16)).T, ((0, 0), (0, LANE - vectors.shape[0]))
     )
     joined = jnp.concatenate(
         (
@@ -227,10 +252,8 @@
         ),
         axis=1,
     )
-    scattered = lax.psum_scatter(joined, "zero", scatter_dimension=0, tiled=True)
-    proj_scattered = lax.psum_scatter(
-        local_grads[3].astype(jnp.bfloat16), "zero", scatter_dimension=0, tiled=True
-    )
+    scattered = scatter_rows(joined)
+    proj_scattered = scatter_rows(local_grads[3].astype(jnp.bfloat16))
     summed_joined, summed_proj = lax.psum((scattered, proj_scattered), "dp")
     ends = [w_qkv.shape[1], w_qkv.shape[1] + w_out.shape[1], w_qkv.shape[1] + w_out.shape[1] + w_fc.shape[1]]
     g_qkv, g_out, g_fc, g_vec = jnp.split(summed_joined, ends, axis=1)
@@ -279,53 +302,58 @@
 
 
 def solution(mesh):
+    cores = 2
+    split_mesh = jax.sharding.Mesh(
+        mesh.devices.reshape(mesh.shape["dp"], mesh.shape["zero"] // cores, cores),
+        ("dp", "zc", "core"),
+    )
     placed = (
-        P(("dp", "zero"), None),
-        P(("dp", "zero"), None),
-        P(("dp", "zero"), None),
-        P("zero", None),
-        P("zero", None),
-        P("zero", None),
-        P("zero", None),
-        P(None, "zero"),
-        P("zero", None),
-        P("zero", None),
-        P("zero", None),
-        P("zero", None),
-        P(None, "zero"),
-        P("zero", None),
-        P("zero", None),
-        P("zero", None),
-        P("zero", None),
-        P(None, "zero"),
+        P(("dp", "zc", "core"), None),
+        P(("dp", "zc", "core"), None),
+        P(("dp", "zc", "core"), None),
+        P(("zc", "core"), None),
+        P(("zc", "core"), None),
+        P(("zc", "core"), None),
+        P(("zc", "core"), None),
+        P(None, ("zc", "core")),
+        P(("zc", "core"), None),
+        P(("zc", "core"), None),
+        P(("zc", "core"), None),
+        P(("zc", "core"), None),
+        P(None, ("zc", "core")),
+        P(("zc", "core"), None),
+        P(("zc", "core"), None),
+        P(("zc", "core"), None),
+        P(("zc", "core"), None),
+        P(None, ("zc", "core")),
     )
     return jax.shard_map(
         local,
-        mesh=mesh,
+        mesh=split_mesh,
         in_specs=placed,
         out_specs=(
-            P(("dp", "zero"), None),
-            P(("dp", "zero"), None),
-            P("zero", None),
-            P("zero", None),
-            P("zero", None),
-            P("zero", None),
-            P(None, "zero"),
-            P("zero", None),
-            P("zero", None),
-            P("zero", None),
-            P("zero", None),
-            P(None, "zero"),
-            P("zero", None),
-            P("zero", None),
-            P("zero", None),
-            P("zero", None),
-            P(None, "zero"),
-            P("zero", None),
-            P("zero", None),
-            P("zero", None),
-            P("zero", None),
-            P(None, "zero"),
+            P(("dp", "zc", "core"), None),
+            P(("dp", "zc", "core"), None),
+            P(("zc", "core"), None),
+            P(("zc", "core"), None),
+            P(("zc", "core"), None),
+            P(("zc", "core"), None),
+            P(None, ("zc", "core")),
+            P(("zc", "core"), None),
+            P(("zc", "core"), None),
+            P(("zc", "core"), None),
+            P(("zc", "core"), None),
+            P(None, ("zc", "core")),
+            P(("zc", "core"), None),
+            P(("zc", "core"), None),
+            P(("zc", "core"), None),
+            P(("zc", "core"), None),
+            P(None, ("zc", "core")),
+            P(("zc", "core"), None),
+            P(("zc", "core"), None),
+            P(("zc", "core"), None),
+            P(("zc", "core"), None),
+            P(None, ("zc", "core")),
         ),
         check_vma=False,
     )

time: 575 us -> 671 us (1.17)
  waiting for transfers between devices: 456 us -> 544 us
  local copies, waits for them, and re-layouts: 9.7 us -> 16.5 us
    all_gather x2 -> x4, waiting for transfers between devices: 178 us -> 231 us  [the longest x2 182 us: gather_rows(): chips = lax.all_gather(shard, 'zc', axis=0, tiled=False)]
    reduce_scatter x2 -> x4, waiting for transfers between devices: 204 us -> 239 us  [the longest x2 209 us: scatter_rows(): return lax.psum_scatter(on_chip, 'zc', scatter_dimension=0, tiled=False)]
  transfers between devices with their start and end apart: 5 -> 9, of which waited for: 5 -> 8; matrix products, arithmetic and copies ran while one was open for 11% -> 10% of each run, Pallas kernels for 0% -> 0%
where the time goes in v1:
time: 671 us; the launch traced here: 669 us
  waiting for transfers between devices  544 us (81%)
  matrix products  68 us (10%)
  other arithmetic  25.7 us (4%)
  local copies, waits for them, and re-layouts  16.5 us (2%)
  between operations  14.5 us (2%)
    reduce_scatter x2, waiting for transfers between devices, scatter_rows(): return lax.psum_scatter(on_chip, 'zc', scatter_dimension=0, tiled=False)  209 us
    all_gather x2, waiting for transfers between devices, gather_rows(): chips = lax.all_gather(shard, 'zc', axis=0, tiled=False)  182 us
    psum x1, waiting for transfers between devices, local(): summed_joined, summed_proj = lax.psum((scattered, proj_scattered), 'dp')  73.7 us
    all_gather x2, waiting for transfers between devices, gather_rows(): both = lax.all_gather(chips, 'core', axis=1, tiled=False)  48.9 us
    reduce_scatter x2, waiting for transfers between devices, scatter_rows(): lax.psum_scatter(grouped, 'core', scatter_dimension=0, tiled=False)  29.9 us
  transfers between devices with their start and end apart: 9, of which 8 were waited for; matrix products, arithmetic and copies ran while one was open for 10% of the time, Pallas kernels for 0%

profile of v1, /device:TPU:4, one launch (start us, length us, event | category | flops | bytes accessed | tf_op | source)
XLA Modules:
  0.0 668.9 jit_solution(5591794510100210970)
XLA Ops:
  7.3 2.2 convert_element_type.124
  9.6 0.7 convert_bitcast_fusion.1
  10.3 0.1 copy.81
  10.6 1.0 fusion.46
  11.7 73.3 %all-gather.13.cloned.1.call-done = bf16[2048,1024]{1,0:T(8,128)(2,1)} async-done(((bf16[256,1024]{1,0:T(8,128)(2,1)}), bf16[2048,1024]{1,0:T(8,128)(2,1)}) %all-gather.13.cloned.1.call-update) | async-done | bytes 4194320 | tf_op jit(solution)/shard_map/all_gather | solution.py:42
  85.0 108.4 %all-gather.9.cloned.1.call-done = bf16[512,8320]{1,0:T(8,128)(2,1)} async-done(((bf16[64,8320]{1,0:T(8,128)(2,1)}), bf16[512,8320]{1,0:T(8,128)(2,1)}) %all-gather.9.cloned.1.call-update) | async-done | bytes 8519696 | tf_op jit(solution)/shard_map/all_gather | solution.py:42
  193.5 0.9 copy-done
  194.4 0.1 convert_reduce_fusion
  194.5 0.2 fusion.71
  194.9 20.6 %all-gather.15.cloned.1.call-done = bf16[8,512,1024]{2,1,0:T(8,128)(2,1)} async-done(((bf16[8,256,1024]{2,1,0:T(8,128)(2,1)}), bf16[8,512,1024]{2,1,0:T(8,128)(2,1)}) %all-gather.15.cloned.1.call-update) | async-done | bytes 8388624 | tf_op jit(solution)/shard_map/all_gather | solution.py:43
  215.5 7.5 %fusion.124 = f32[128,4096]{1,0:T(8,128)} fusion(bf16[128,1024]{1,0:T(8,128)(2,1)S(1)} %copy-done.3, bf16[4096,1024]{1,0:T(8,128)(2,1)} %bitcast.97), kind=kOutput, calls=%fused_computation.174 | convolution fusion | flops 1073741824 | bytes 10747904 | tf_op jit(solution)/shard_map/dot_general | solution.py:147
  223.0 28.2 %all-gather.11.cloned.1.call-done = bf16[8,128,8320]{2,1,0:T(8,128)(2,1)} async-done(((bf16[8,64,8320]{2,1,0:T(8,128)(2,1)}), bf16[8,128,8320]{2,1,0:T(8,128)(2,1)}) %all-gather.11.cloned.1.call-update) | async-done | bytes 17039376 | tf_op jit(solution)/shard_map/all_gather | solution.py:43
  251.3 1.0 slice.61
  252.2 0.1 copy.77
  252.4 0.2 fusion.69
  252.7 3.8 fusion.8
  256.6 0.2 copy.57
  256.8 0.2 copy.58
  257.0 0.2 copy.56
  257.2 0.4 convolution_multiply_fusion
  257.6 0.5 convolution_convert_fusion.5
  258.1 2.3 fusion.121
  260.4 0.2 multiply_reduce_fusion.3
  260.6 0.2 add_convert_fusion.1
  260.8 7.8 %fusion.115 = (bf16[4096]{0:T(1024)(128)(2,1)S(1)}, bf16[128,4096]{1,0:T(8,128)(2,1)}, bf16[128,4096]{1,0:T(8,128)(2,1)S(1)}) fusion(f32[128,4096]{1,0:T(8,128)S(1)} %copy-done.9, f32[4096]{0:T(1024)S(1)} %bitcast.150, bf16[128,1024]{1,0:T(8,128)(2,1)S(1)} %add_convert_fusion.1, bf16[1024,8320]{1,0:T(8,128)(2,1)} %bitcast.126), kind=kOutput, calls=%fused_computation.168 | convolution fusion | flops 1088417792 | bytes 12869632 | tf_op jit(solution)/shard_map/dot_general | solution.py:140
  268.6 1.6 reshape.338
  270.2 2.6 copy.71
  272.7 5.6 convolution_convert_fusion
  278.4 0.2 reduce-scatter.5.cloned.1.call-start
  278.7 0.2 copy.64
  278.9 0.4 copy-done.22
  279.3 0.2 copy.67
  279.5 1.7 copy.66
  281.3 6.4 multiply_reduce_fusion.1
  287.8 0.3 fusion.117
  288.1 3.4 fusion.43
  291.6 1.9 copy.60
  293.4 2.2 fusion.118
  295.6 2.4 fusion.125
  298.0 1.3 fusion.33
  299.3 2.8 convolution_convert_fusion.4
  302.1 3.4 fusion.119
  305.5 5.2 fusion.106
  310.8 0.3 fusion.70
  311.1 1.0 fusion.105
  312.5 0.9 copy.69
  313.4 2.2 convolution_convert_fusion.3
  315.5 2.9 copy.70
  318.5 2.9 convolution_convert_fusion.2
  321.4 2.3 convolution_convert_fusion.1
  323.8 6.6 fusion.3
  330.5 0.7 reduce-scatter.11.cloned.1.call-update
  331.2 29.9 %reduce-scatter.5.cloned.1.call-done = bf16[1,8,64,8320]{3,2,1,0:T(8,128)(2,1)} async-done(((bf16[2,8,64,8320]{3,2,1,0:T(8,128)(2,1)}), bf16[1,8,64,8320]{3,2,1,0:T(8,128)(2,1)}) %reduce-scatter.5.cloned.1.call-update) | async-done | bytes 8519696 | tf_op jit(solution)/shard_map/reduce_scatter | solution.py:58
  361.2 89.7 %reduce-scatter.11.cloned.1.call-done = bf16[1,256,1024]{2,1,0:T(8,128)(2,1)} async-done(((bf16[8,256,1024]{2,1,0:T(8,128)(2,1)}), bf16[1,256,1024]{2,1,0:T(8,128)(2,1)}) %reduce-scatter.11.cloned.1.call-update) | async-done | bytes 524304 | tf_op jit(solution)/shard_map/reduce_scatter | solution.py:59
  450.9 118.9 %reduce-scatter.7.cloned.1.call-done = bf16[1,64,8320]{2,1,0:T(8,128)(2,1)} async-done(((bf16[8,64,8320]{2,1,0:T(8,128)(2,1)}), bf16[1,64,8320]{2,1,0:T(8,128)(2,1)}) %reduce-scatter.7.cloned.1.call-update) | async-done | bytes 1064976 | tf_op jit(solution)/shard_map/reduce_scatter | solution.py:59
  570.0 5.5 fusion.42
  575.4 73.7 %all-reduce.5.cloned.1.call-done = (bf16[64,8320]{1,0:T(8,128)(2,1)}, bf16[256,1024]{1,0:T(8,128)(2,1)}) async-done(((bf16[64,8320]{1,0:T(8,128)(2,1)}, bf16[256,1024]{1,0:T(8,128)(2,1)}), (bf16[64,8320]{1,0:T(8,128)(2,1)}, bf16[256,1024]{1,0:T(8,128)(2,1)})) %all-reduce.5.cloned.1.call-update) | async-done | bytes 1589264 | tf_op jit(solution)/shard_map/psum | solution.py:257
  649.1 1.6 multiply_subtract_fusion.4
  650.8 2.0 multiply_subtract_fusion.3
  652.8 3.4 multiply_subtract_fusion.2
  656.3 2.6 multiply_subtract_fusion.1
  658.9 0.2 copy-done.14
  659.2 0.5 copy-done.32
  659.7 2.7 multiply_subtract_fusion
  (134 shorter events, 1.9 us)
Async XLA Ops:
  7.2 3.2 copy-start.17
  7.2 3.2 copy-start.7
  7.2 3.3 copy-start.4
  7.2 77.7 %all-gather.13.cloned.1.call-start = ((), (), s32[]{:S(2)}) async-start(), calls=%async_computation.10 | async-start | bytes 4718592 | tf_op jit(solution)/shard_map/all_gather | solution.py:42
  9.5 183.9 %all-gather.9.cloned.1.call-start = ((), (), s32[]{:S(2)}) async-start(), calls=%async_computation.8 | async-start | bytes 9584640 | tf_op jit(solution)/shard_map/all_gather | solution.py:42
  11.6 203.9 %all-gather.15.cloned.1.call-start = ((), (), s32[]{:S(2)}) async-start(), calls=%async_computation.11 | async-start | bytes 12582912 | tf_op jit(solution)/shard_map/all_gather | solution.py:43
  85.0 166.3 %all-gather.11.cloned.1.call-start = ((), (), s32[]{:S(2)}) async-start(), calls=%async_computation.9 | async-start | bytes 25559040 | tf_op jit(solution)/shard_map/all_gather | solution.py:43
  193.4 0.9 copy-start
  193.5 1.3 copy-start.39
  193.5 22.0 %copy-start.3 = (bf16[128,1024]{1,0:T(8,128)(2,1)S(1)}, bf16[128,1024]{1,0:T(8,128)(2,1)}, u32[]{:S(2)}) copy-start(bf16[128,1024]{1,0:T(8,128)(2,1)} %param.19) | copy-start | bytes 786436
  193.5 137.0 %reduce-scatter.9.cloned.1.call-start = ((), (), s32[]{:S(2)}) async-start(), calls=%async_computation.6 | async-start | bytes 12582912 | tf_op jit(solution)/shard_map/reduce_scatter | solution.py:58
  256.8 1.2 copy-start.25
  257.0 1.1 copy-start.23
  257.2 0.9 copy-start.26
  257.5 2.8 copy-start.19
  258.0 2.7 copy-start.29
  258.1 2.7 copy-start.9
  260.8 7.8 %copy-start.21 = (bf16[128,1024]{1,0:T(8,128)(2,1)}, bf16[128,1024]{1,0:T(8,128)(2,1)S(1)}, u32[]{:S(2)}) copy-start(bf16[128,1024]{1,0:T(8,128)(2,1)S(1)} %add_convert_fusion.1) | copy-start | bytes 786436
  268.6 9.7 %copy-start.1 = (bf16[128,4096]{1,0:T(8,128)(2,1)}, bf16[128,4096]{1,0:T(8,128)(2,1)S(1)}, u32[]{:S(2)}) copy-start(bf16[128,4096]{1,0:T(8,128)(2,1)S(1)} %get-tuple-element.55) | copy-start | bytes 3145732
  278.3 1.0 copy-start.22
  278.4 2.9 copy-start.15
  278.4 82.7 %reduce-scatter.5.cloned.1.call-start = ((), (), s32[]{:S(2)}) async-start(), calls=%async_computation.4 | async-start | bytes 25559040 | tf_op jit(solution)/shard_map/reduce_scatter | solution.py:58
  288.1 5.3 copy-start.20
  291.6 4.1 copy-start.27
  298.0 4.1 copy-start.24
  299.3 6.2 copy-start.35
  302.1 8.6 %copy-start.37 = (bf16[16,64,128]{2,1,0:T(8,128)(2,1)}, bf16[16,64,128]{2,1,0:T(8,128)(2,1)S(1)}, u32[]{:S(2)}) copy-start(bf16[16,64,128]{2,1,0:T(8,128)(2,1)S(1)} %convolution_convert_fusion.4) | copy-start | bytes 786436
  310.7 2.7 copy-start.28
  315.5 2.9 copy-start.36
  318.4 2.9 copy-start.16
  321.4 2.4 copy-start.10
  330.4 120.5 %reduce-scatter.11.cloned.1.call-start = ((), (), s32[]{:S(2)}) async-start(), calls=%async_computation.7 | async-start | bytes 4718592 | tf_op jit(solution)/shard_map/reduce_scatter | solution.py:59
  331.2 238.6 %reduce-scatter.7.cloned.1.call-start = ((), (), s32[]{:S(2)}) async-start(), calls=%async_computation.5 | async-start | bytes 9584640 | tf_op jit(solution)/shard_map/reduce_scatter | solution.py:59
  361.1 208.7 %copy-start.2 = (bf16[128,4096]{1,0:T(8,128)(2,1)S(1)}, bf16[128,4096]{1,0:T(8,128)(2,1)}, u32[]{:S(2)}) copy-start(bf16[128,4096]{1,0:T(8,128)(2,1)} %copy-done.1) | copy-start | bytes 3145732
  361.2 288.0 %all-reduce.5.cloned.1.call-start = ((), (), s32[]{:S(2)}) async-start(), calls=%async_computation.12 | async-start | bytes 3178496 | tf_op jit(solution)/shard_map/psum | solution.py:257
  569.9 79.3 %copy-start.38 = (f32[12,64]{1,0:T(8,128)S(1)}, f32[12,64]{1,0:T(8,128)}, u32[]{:S(2)}) copy-start(f32[12,64]{1,0:T(8,128)} %param.25) | copy-start | bytes 9220
  569.9 79.3 %copy-start.40 = (f32[12,64]{1,0:T(8,128)S(1)}, f32[12,64]{1,0:T(8,128)}, u32[]{:S(2)}) copy-start(f32[12,64]{1,0:T(8,128)} %param.30) | copy-start | bytes 9220
  569.9 79.2 %copy-start.41 = (f32[12,64]{1,0:T(8,128)S(1)}, f32[12,64]{1,0:T(8,128)}, u32[]{:S(2)}) copy-start(f32[12,64]{1,0:T(8,128)} %param.35) | copy-start | bytes 9220
  569.9 80.8 %copy-start.18 = (f32[64,1024]{1,0:T(8,128)S(1)}, f32[64,1024]{1,0:T(8,128)}, u32[]{:S(2)}) copy-start(f32[64,1024]{1,0:T(8,128)} %param.22) | copy-start | bytes 786436
  569.9 80.8 %copy-start.33 = (f32[64,1024]{1,0:T(8,128)S(1)}, f32[64,1024]{1,0:T(8,128)}, u32[]{:S(2)}) copy-start(f32[64,1024]{1,0:T(8,128)} %param.27) | copy-start | bytes 786436
  569.9 80.8 %copy-start.34 = (f32[64,1024]{1,0:T(8,128)S(1)}, f32[64,1024]{1,0:T(8,128)}, u32[]{:S(2)}) copy-start(f32[64,1024]{1,0:T(8,128)} %param.32) | copy-start | bytes 786436
  569.9 82.8 %copy-start.31 = (f32[64,3072]{1,0:T(8,128)S(1)}, f32[64,3072]{1,0:T(8,128)}, u32[]{:S(2)}) copy-start(f32[64,3072]{1,0:T(8,128)} %param.26) | copy-start | bytes 2359300
  575.4 77.4 %copy-start.8 = (f32[64,3072]{1,0:T(8,128)S(1)}, f32[64,3072]{1,0:T(8,128)}, u32[]{:S(2)}) copy-start(f32[64,3072]{1,0:T(8,128)} %param.21) | copy-start | bytes 2359300
  649.1 3.6 copy-start.30
  652.8 3.4 copy-start.5
  652.8 3.4 copy-start.11
  652.8 3.4 copy-start.12
  656.2 2.7 copy-start.6
  656.2 2.7 copy-start.13
  656.3 2.9 copy-start.14
  656.3 3.4 copy-start.32
Sparse Core Ops, SparseCore 0:
  11.0 73.9 all-gather.12
  87.2 106.1 all-gather.8
  195.1 20.3 all-gather.14
  217.0 34.2 all-gather.10
  278.5 20.9 reduce-scatter.8
  330.6 30.5 reduce-scatter.4
  364.9 85.9 reduce-scatter.10
  455.3 114.5 reduce-scatter.6
  572.4 76.6 all-reduce.4

commit v2 on v0

--- a/solution.py
+++ b/solution.py
@@ -122,7 +122,10 @@
         middle + jnp.dot(hidden, proj_mat, preferred_element_type=jnp.float32) + vec_rows[7]
     ).astype(jnp.bfloat16)
     cot32 = cot_in.astype(jnp.float32)
-    grad_proj = jnp.dot(hidden.T, cot_in, preferred_element_type=jnp.float32)
+    grad_proj = jnp.dot(hidden.T, cot_in, preferred_element_type=jnp.float32).astype(jnp.bfloat16)
+    grad_proj, cot_in, hidden_pre, middle = lax.optimization_barrier(
+        (grad_proj, cot_in, hidden_pre, middle)
+    )
     grad_hidden = jnp.dot(cot_in, proj_mat.T, preferred_element_type=jnp.float32)
     gelu_back = jax.vjp(gelu_tanh, hidden_pre)[1]
     grad_pre = gelu_back(grad_hidden)[0]
@@ -199,18 +202,14 @@
     zero_size = lax.axis_size("zero")
     replicas = dp_size * zero_size
     vec_cols = jnp.pad(vectors.astype(jnp.bfloat16).T, ((0, 0), (0, LANE - vectors.shape[0])))
-    qkv_mat, out_mat, fc_mat, vec_cols_all = sent_together(
-        (
-            w_qkv.astype(jnp.bfloat16),
-            w_out.astype(jnp.bfloat16),
-            w_fc.astype(jnp.bfloat16),
-            vec_cols,
-        ),
-        "zero",
-        0,
-        1,
-    )
-    proj_mat = lax.all_gather(w_proj.astype(jnp.bfloat16), "zero", axis=0, tiled=True)
+    first_mats = (w_qkv.astype(jnp.bfloat16), w_out.astype(jnp.bfloat16), w_fc.astype(jnp.bfloat16), vec_cols)
+    first_all = lax.all_gather(jnp.concatenate(first_mats, axis=1), "zero", axis=0, tiled=True)
+    first_all, proj_shard = lax.optimization_barrier((first_all, w_proj.astype(jnp.bfloat16)))
+    proj_mat = lax.all_gather(proj_shard, "zero", axis=0, tiled=True)
+    widths = [m.shape[1] for m in first_mats]
+    qkv_mat, out_mat, fc_mat, vec_cols_all = jnp.split(
+        first_all, [sum(widths[:k]) for k in range(1, len(widths))], axis=1
+    )
     vec_rows = vec_cols_all[:, : vectors.shape[0]].T.astype(jnp.float32)
     block_out, input_grad, local_grads = block_pass(
         tokens, cotangent, segments, qkv_mat, out_mat, fc_mat, proj_mat, vec_rows

time: 575 us -> 556 us (0.967)
  waiting for transfers between devices: 456 us -> 435 us
    all_gather x2, waiting for transfers between devices: 178 us -> 159 us  [the longest x1 112 us: local(): lax.all_gather(jnp.concatenate(first_mats, axis=1), 'zero', axis=0, tiled...]
  transfers between devices with their start and end apart: 5 -> 5, of which waited for: 5 -> 5; matrix products, arithmetic and copies ran while one was open for 11% -> 15% of each run, Pallas kernels for 0% -> 0%
where the time goes in v2:
time: 556 us; the launch traced here: 554 us
  waiting for transfers between devices  435 us (78%)
  matrix products  65.4 us (12%)
  other arithmetic  29.3 us (5%)
  between operations  14.4 us (3%)
  local copies, waits for them, and re-layouts  9.47 us (2%)
    reduce_scatter x1, waiting for transfers between devices, local(): lax.psum_scatter(joined, 'zero', scatter_dimension=0, tiled=True)  152 us
    all_gather x1, waiting for transfers between devices, local(): lax.all_gather(jnp.concatenate(first_mats, axis=1), 'zero', axis=0, tiled...  112 us
    psum x1, waiting for transfers between devices, local(): summed_joined, summed_proj = lax.psum((scattered, proj_scattered), 'dp')  73.5 us
    reduce_scatter x1, waiting for transfers between devices, local(): lax.psum_scatter(local_grads[3].astype(jnp.bfloat16), 'zero', scatter_dim...  50.6 us
    all_gather x1, waiting for transfers between devices, local(): proj_mat = lax.all_gather(proj_shard, 'zero', axis=0, tiled=True)  47.3 us
  transfers between devices with their start and end apart: 5, of which 5 were waited for; matrix products, arithmetic and copies ran while one was open for 15% of the time, Pallas kernels for 0%

profile of v2, /device:TPU:4, one launch (start us, length us, event | category | flops | bytes accessed | tf_op | source)
XLA Modules:
  0.0 553.7 jit_solution(3551963044557908865)
XLA Ops:
  7.2 0.8 convert_bitcast_fusion.1
  8.0 0.1 copy.90
  8.1 1.0 convert_element_type.109
  9.1 1.2 convert_element_type.108
  10.4 1.1 fusion.50
  11.5 0.4 copy-done.6
  11.9 0.9 convert_element_type.112
  12.8 111.8 %all-gather.3.cloned.1.call-done = bf16[1024,8320]{1,0:T(8,128)(2,1)} async-done(((bf16[64,8320]{1,0:T(8,128)(2,1)}), bf16[1024,8320]{1,0:T(8,128)(2,1)}) %all-gather.3.cloned.1.call-update) | async-done | bytes 17039376 | tf_op jit(solution)/shard_map/all_gather | solution.py:206
  124.6 0.1 convert_reduce_fusion
  124.8 0.2 fusion.75
  125.0 0.1 fusion.92
  125.1 1.0 convert_bitcast_fusion
  126.1 0.2 slice.71
  126.3 0.2 copy.79
  126.5 2.1 slice_reduce_fusion.2
  128.6 3.9 fusion.10
  132.5 0.1 fusion.77
  132.6 0.2 copy.76
  132.8 0.2 copy.77
  133.0 0.2 copy.75
  133.2 0.4 convolution_multiply_fusion
  133.6 0.5 convolution_convert_fusion.5
  134.1 0.5 copy-done.15
  134.5 2.3 fusion.128
  136.9 0.2 multiply_reduce_fusion.4
  137.1 4.8 fusion.12
  141.9 5.6 %convolution_convert_fusion.1 = bf16[4096,1024]{1,0:T(8,128)(2,1)} fusion(bf16[128,1024]{1,0:T(8,128)(2,1)S(1)} %copy-done.3, f32[128,4096]{1,0:T(8,128)S(1)} %fusion.12), kind=kOutput, calls=%fused_computation.6 | convolution fusion | flops 1082654720 | bytes 10747904 | tf_op jit(solution)/shard_map/dot_general | solution.py:125
  147.5 0.2 reduce-scatter.3.cloned.1.call-start
  147.8 0.1 reduce_sum.191
  148.0 0.2 multiply_reduce_fusion.3
  148.2 2.9 fusion.37
  151.0 47.3 %all-gather.5.cloned.1.call-done = bf16[4096,1024]{1,0:T(8,128)(2,1)} async-done(((bf16[256,1024]{1,0:T(8,128)(2,1)}), bf16[4096,1024]{1,0:T(8,128)(2,1)}) %all-gather.5.cloned.1.call-update) | async-done | bytes 8388624 | tf_op jit(solution)/shard_map/all_gather | solution.py:208
  198.3 8.5 %fusion.123 = (bf16[4096]{0:T(1024)(128)(2,1)S(1)}, bf16[128,4096]{1,0:T(8,128)(2,1)}) fusion(f32[128,4096]{1,0:T(8,128)S(1)} %fusion.12, bf16[128,1024]{1,0:T(8,128)(2,1)S(1)} %copy-done.3, bf16[4096,1024]{1,0:T(8,128)(2,1)} %all-gather.5.cloned.1.call-done), kind=kOutput, calls=%fused_computation.173 | convolution fusion | flops 1086844928 | bytes 11804672 | tf_op jit(solution)/shard_map/dot_general | solution.py:129
  206.8 7.3 %multiply_reduce_fusion.1 = (bf16[1024]{0:T(1024)(128)(2,1)S(1)}, f32[128]{0:T(128)S(1)}, bf16[1024]{0:T(1024)(128)(2,1)S(1)}, f32[128,1024]{1,0:T(8,128)S(1)}) fusion(f32[128,1024]{1,0:T(8,128)S(1)} %get-tuple-element.32, f32[128]{0:T(128)S(1)} %fusion.103, f32[128]{0:T(128)S(1)} %broadcast_multiply_fusion.1, f32[1024]{0:T(1024)S(1)} %get-tuple-element.41, ...), kind=kOutput, calls=%fused_computation.114 | convolution fusion | flops 1074788224 | bytes 10495488 | tf_op jit(solution)/shard_map/dot_general | solution.py:134
  214.2 0.3 fusion.125
  214.4 2.6 fusion.47
  217.1 0.2 copy.80
  217.3 3.1 fusion.126
  220.4 0.1 stack.25
  220.5 1.3 fusion.131
  221.8 2.9 fusion.127
  224.7 0.1 stack.24
  224.8 2.1 convolution_convert_fusion.4
  227.0 0.7 copy-done.28
  227.7 5.2 fusion.114
  232.9 0.3 fusion.74
  233.2 1.0 fusion.111
  234.3 0.2 copy.84
  234.5 2.2 convolution_convert_fusion.3
  236.7 3.1 copy.85
  239.9 3.1 convolution_convert_fusion.2
  243.0 2.5 convolution_convert_fusion
  245.4 6.6 %fusion.3 = bf16[1024,8320]{1,0:T(8,128)(2,1)} fusion(bf16[1024,12]{1,0:T(8,128)(2,1)S(1)} %bitcast.50, bf16[1024,4096]{1,0:T(8,128)(2,1)S(1)} %convolution_convert_fusion, bf16[1024,1024]{1,0:T(8,128)(2,1)S(1)} %copy.85, bf16[1024,3072]{1,0:T(8,128)(2,1)S(1)} %convolution_convert_fusion.2), kind=kLoop, calls=%fused_computation.4 | loop fusion | flops 85196800 | bytes 33841152 | tf_op jit(solution)/shard_map/concatenate | solution.py:220
  252.2 50.6 %reduce-scatter.5.cloned.1.call-done = bf16[256,1024]{1,0:T(8,128)(2,1)} async-done(((bf16[4096,1024]{1,0:T(8,128)(2,1)}), bf16[256,1024]{1,0:T(8,128)(2,1)}) %reduce-scatter.5.cloned.1.call-update) | async-done | bytes 524304 | tf_op jit(solution)/shard_map/reduce_scatter | solution.py:230
  302.7 151.6 %reduce-scatter.3.cloned.1.call-done = bf16[64,8320]{1,0:T(8,128)(2,1)} async-done(((bf16[1024,8320]{1,0:T(8,128)(2,1)}), bf16[64,8320]{1,0:T(8,128)(2,1)}) %reduce-scatter.3.cloned.1.call-update) | async-done | bytes 1064976 | tf_op jit(solution)/shard_map/reduce_scatter | solution.py:229
  454.4 5.7 %fusion.46 = bf16[128,1024]{1,0:T(8,128)(2,1)} fusion(f32[128,1024]{1,0:T(8,128)S(1)} %get-tuple-element.32, bf16[4096,1024]{1,0:T(8,128)(2,1)} %all-gather.5.cloned.1.call-done, f32[1024]{0:T(1024)S(1)} %get-tuple-element.42, f32[128,4096]{1,0:T(8,128)S(1)} %copy-done.2), kind=kOutput, calls=%fused_computation.60 | convolution fusion | flops 1078853632 | bytes 11276288 | tf_op jit(solution)/shard_map/dot_general | solution.py:122
  460.1 73.5 %all-reduce.5.cloned.1.call-done = (bf16[64,8320]{1,0:T(8,128)(2,1)}, bf16[256,1024]{1,0:T(8,128)(2,1)}) async-done(((bf16[64,8320]{1,0:T(8,128)(2,1)}, bf16[256,1024]{1,0:T(8,128)(2,1)}), (bf16[64,8320]{1,0:T(8,128)(2,1)}, bf16[256,1024]{1,0:T(8,128)(2,1)})) %all-reduce.5.cloned.1.call-update) | async-done | bytes 1589264 | tf_op jit(solution)/shard_map/psum | solution.py:233
  533.6 1.6 multiply_subtract_fusion.4
  535.2 2.1 multiply_subtract_fusion.3
  537.4 3.6 multiply_subtract_fusion.2
  541.1 2.6 multiply_subtract_fusion.1
  543.8 0.2 copy-done.12
  544.0 0.5 copy-done.24
  544.5 2.7 multiply_subtract_fusion
  (92 shorter events, 0.8 us)
Async XLA Ops:
  7.2 3.1 copy-start.4
  7.2 117.4 %all-gather.3.cloned.1.call-start = ((), (), s32[]{:S(2)}) async-start(), calls=%async_computation.2 | async-start | bytes 18104320 | tf_op jit(solution)/shard_map/all_gather | solution.py:206
  10.3 1.6 copy-start.6
  11.4 113.2 %copy-start = (bf16[128,1024]{1,0:T(8,128)(2,1)S(1)}, bf16[128,1024]{1,0:T(8,128)(2,1)}, u32[]{:S(2)}) copy-start(bf16[128,1024]{1,0:T(8,128)(2,1)} %param.18) | copy-start | bytes 786436
  11.4 113.6 %copy-start.30 = (s32[1,128]{1,0:T(1,128)S(1)}, s32[1,128]{1,0:T(1,128)}, u32[]{:S(2)}) copy-start(s32[1,128]{1,0:T(1,128)} %param.20) | copy-start | bytes 1540
  11.5 186.9 %all-gather.5.cloned.1.call-start = ((), (), s32[]{:S(2)}) async-start(), calls=%async_computation.3 | async-start | bytes 8912896 | tf_op jit(solution)/shard_map/all_gather | solution.py:208
  124.6 178.1 %reduce-scatter.5.cloned.1.call-start = ((), (), s32[]{:S(2)}) async-start(), calls=%async_computation.5 | async-start | bytes 8912896 | tf_op jit(solution)/shard_map/reduce_scatter | solution.py:230
  133.0 3.8 copy-start.16
  133.2 3.7 copy-start.18
  133.6 1.0 copy-start.15
  134.0 3.0 copy-start.21
  137.1 4.8 copy-start.3
  141.9 56.5 %copy-start.1 = (f32[128,4096]{1,0:T(8,128)}, f32[128,4096]{1,0:T(8,128)S(1)}, u32[]{:S(2)}) copy-start(f32[128,4096]{1,0:T(8,128)S(1)} %fusion.12) | copy-start | bytes 6291460
  147.5 306.8 %reduce-scatter.3.cloned.1.call-start = ((), (), s32[]{:S(2)}) async-start(), calls=%async_computation.4 | async-start | bytes 18104320 | tf_op jit(solution)/shard_map/reduce_scatter | solution.py:229
  217.1 3.4 copy-start.19
  217.1 4.7 copy-start.17
  217.3 3.1 copy-start.20
  221.8 5.8 %copy-start.26 = (bf16[1,128,16,64]{1,3,2,0:T(8,128)(2,1)S(1)}, bf16[1,128,16,64]{1,3,2,0:T(8,128)(2,1)}, u32[]{:S(2)}) copy-start(bf16[1,128,16,64]{1,3,2,0:T(8,128)(2,1)} %get-tuple-element.80) | copy-start | bytes 786436
  226.9 0.7 copy-start.28
  232.8 1.7 copy-start.22
  236.7 3.1 copy-start.27
  239.9 3.1 copy-start.13
  252.1 202.3 %copy-start.2 = (f32[128,4096]{1,0:T(8,128)S(1)}, f32[128,4096]{1,0:T(8,128)}, u32[]{:S(2)}) copy-start(f32[128,4096]{1,0:T(8,128)} %copy-done.1) | copy-start | bytes 6291460
  252.1 281.5 %all-reduce.5.cloned.1.call-start = ((), (), s32[]{:S(2)}) async-start(), calls=%async_computation.6 | async-start | bytes 3178496 | tf_op jit(solution)/shard_map/psum | solution.py:233
  454.4 79.2 %copy-start.29 = (f32[12,64]{1,0:T(8,128)S(1)}, f32[12,64]{1,0:T(8,128)}, u32[]{:S(2)}) copy-start(f32[12,64]{1,0:T(8,128)} %param.25) | copy-start | bytes 9220
  454.4 79.2 %copy-start.31 = (f32[12,64]{1,0:T(8,128)S(1)}, f32[12,64]{1,0:T(8,128)}, u32[]{:S(2)}) copy-start(f32[12,64]{1,0:T(8,128)} %param.30) | copy-start | bytes 9220
  454.4 79.2 %copy-start.32 = (f32[12,64]{1,0:T(8,128)S(1)}, f32[12,64]{1,0:T(8,128)}, u32[]{:S(2)}) copy-start(f32[12,64]{1,0:T(8,128)} %param.35) | copy-start | bytes 9220
  454.4 80.8 %copy-start.14 = (f32[64,1024]{1,0:T(8,128)S(1)}, f32[64,1024]{1,0:T(8,128)}, u32[]{:S(2)}) copy-start(f32[64,1024]{1,0:T(8,128)} %param.22) | copy-start | bytes 786436
  454.4 80.8 %copy-start.25 = (f32[64,1024]{1,0:T(8,128)S(1)}, f32[64,1024]{1,0:T(8,128)}, u32[]{:S(2)}) copy-start(f32[64,1024]{1,0:T(8,128)} %param.27) | copy-start | bytes 786436
  460.1 77.3 %copy-start.8 = (f32[64,3072]{1,0:T(8,128)S(1)}, f32[64,3072]{1,0:T(8,128)}, u32[]{:S(2)}) copy-start(f32[64,3072]{1,0:T(8,128)} %param.21) | copy-start | bytes 2359300
  533.6 3.8 copy-start.23
  537.4 3.7 copy-start.5
  537.4 3.7 copy-start.9
  537.4 3.7 copy-start.10
  541.1 2.7 copy-start.7
  541.1 2.7 copy-start.11
  541.1 2.9 copy-start.12
  541.1 3.4 copy-start.24
Sparse Core Ops, SparseCore 0:
  11.6 112.9 all-gather.2
  127.6 70.6 all-gather.4
  202.6 100.0 reduce-scatter.4
  306.9 147.3 reduce-scatter.2
  457.0 76.5 all-reduce.4

commit v3 on v2

--- a/solution.py
+++ b/solution.py
@@ -3,6 +3,8 @@
 import jax
 import jax.numpy as jnp
 from jax import lax
+from jax.experimental import pallas as pl
+from jax.experimental.pallas import tpu as pltpu
 from jax.sharding import PartitionSpec as P
 
 HEADS = 16
@@ -36,6 +38,94 @@
     return tuple(
         jnp.split(lax.psum_scatter(both, axis, scatter_dimension=dim, tiled=True), ends, axis=along)
     )
+
+
+def dp_sum_kernel(parts, x_ref, out_ref, recv_one, recv_two, mine, send_one, got_one, send_two, got_two):
+    me = lax.axis_index("dp")
+    shard = lax.axis_index("zero")
+    rows = recv_one.shape[1]
+    barrier = pltpu.get_barrier_semaphore()
+    for k in range(1, parts):
+        pl.semaphore_signal(
+            barrier, inc=1, device_id=(lax.rem(me + k, parts), shard),
+            device_id_type=pl.DeviceIdType.MESH,
+        )
+    pl.semaphore_wait(barrier, parts - 1)
+    first = []
+    for k in range(1, parts):
+        peer = lax.rem(me + k, parts)
+        copy = pltpu.make_async_remote_copy(
+            src_ref=x_ref.at[pl.ds(pl.multiple_of(peer * rows, rows), rows)],
+            dst_ref=recv_one.at[k],
+            send_sem=send_one.at[k],
+            recv_sem=got_one.at[k],
+            device_id=(peer, shard),
+            device_id_type=pl.DeviceIdType.MESH,
+        )
+        copy.start()
+        first.append(copy)
+    total = x_ref[pl.ds(pl.multiple_of(me * rows, rows), rows), :].astype(jnp.float32)
+    for k, copy in enumerate(first, start=1):
+        copy.wait_recv()
+        total = total + recv_one[k].astype(jnp.float32)
+    mine[...] = total.astype(mine.dtype)
+    out_ref[pl.ds(pl.multiple_of(me * rows, rows), rows), :] = mine[...]
+    second = []
+    for k in range(1, parts):
+        peer = lax.rem(me + k, parts)
+        copy = pltpu.make_async_remote_copy(
+            src_ref=mine,
+            dst_ref=recv_two.at[k],
+            send_sem=send_two.at[k],
+            recv_sem=got_two.at[k],
+            device_id=(peer, shard),
+            device_id_type=pl.DeviceIdType.MESH,
+        )
+        copy.start()
+        second.append(copy)
+    for copy in first:
+        copy.wait_send()
+    for k, copy in enumerate(second, start=1):
+        copy.wait_recv()
+        source = lax.rem(me + parts - k, parts)
+        out_ref[pl.ds(pl.multiple_of(source * rows, rows), rows), :] = recv_two[k]
+    for copy in second:
+        copy.wait_send()
+
+
+def dp_sum(packed, parts):
+    rows = packed.shape[0] // parts
+    return pl.pallas_call(
+        partial(dp_sum_kernel, parts),
+        out_shape=jax.ShapeDtypeStruct(packed.shape, packed.dtype),
+        in_specs=[pl.BlockSpec(memory_space=pltpu.VMEM)],
+        out_specs=pl.BlockSpec(memory_space=pltpu.VMEM),
+        scratch_shapes=[
+            pltpu.VMEM((parts, rows, packed.shape[1]), packed.dtype),
+            pltpu.VMEM((parts, rows, packed.shape[1]), packed.dtype),
+            pltpu.VMEM((rows, packed.shape[1]), packed.dtype),
+            pltpu.SemaphoreType.DMA((parts,)),
+            pltpu.SemaphoreType.DMA((parts,)),
+            pltpu.SemaphoreType.DMA((parts,)),
+            pltpu.SemaphoreType.DMA((parts,)),
+        ],
+        compiler_params=pltpu.CompilerParams(collective_id=0, has_side_effects=True),
+    )(packed)
+
+
+def summed_over_dp(arrays):
+    parts = lax.axis_size("dp")
+    flat = [a.reshape(-1, LANE) for a in arrays]
+    count = sum(f.shape[0] for f in flat)
+    step = parts * 16
+    padded = -(-count // step) * step
+    packed = jnp.concatenate(flat + [jnp.zeros((padded - count, LANE), arrays[0].dtype)], axis=0)
+    result = dp_sum(packed, parts)
+    outs, at = [], 0
+    for a, f in zip(arrays, flat):
+        outs.append(result[at : at + f.shape[0]].reshape(a.shape))
+        at += f.shape[0]
+    return outs
 
 
 def gelu_tanh(inputs):
@@ -230,7 +320,7 @@
     proj_scattered = lax.psum_scatter(
         local_grads[3].astype(jnp.bfloat16), "zero", scatter_dimension=0, tiled=True
     )
-    summed_joined, summed_proj = lax.psum((scattered, proj_scattered), "dp")
+    summed_joined, summed_proj = summed_over_dp((scattered, proj_scattered))
     ends = [w_qkv.shape[1], w_qkv.shape[1] + w_out.shape[1], w_qkv.shape[1] + w_out.shape[1] + w_fc.shape[1]]
     g_qkv, g_out, g_fc, g_vec = jnp.split(summed_joined, ends, axis=1)
     summed = (

time: 556 us -> 558 us (level); the launches traced: 554 us -> 550 us
  waiting for transfers between devices: 435 us -> 356 us
  Pallas kernels: 0 us -> 54 us
  local copies, waits for them, and re-layouts: 9.47 us -> 22.4 us
  other arithmetic: 29.3 us -> 39 us
    psum x1 -> x0, waiting for transfers between devices: 73.5 us -> none  [local(): summed_joined, summed_proj = lax.psum((scattered, proj_scattered), 'dp')]
    pallas_call x0 -> x1, Pallas kernels: none -> 54 us  [dp_sum(): pl.pallas_call(partial(dp_sum_kernel, parts), out_shape=jax.ShapeDtypeStr...]
    concatenate x0 -> x1, other arithmetic: none -> 9.12 us  [summed_over_dp(): jnp.concatenate(flat + [jnp.zeros((padded - count, LANE), arrays[0].dtype...]
    reduce_scatter x1, waiting for transfers between devices: 152 us -> 145 us  [local(): lax.psum_scatter(joined, 'zero', scatter_dimension=0, tiled=True)]
    mul x0 -> x3, local copies, waits for them, and re-layouts: none -> 6.49 us  [the longest x1 2.75 us: adam_step(): mean_new = beta_first * mean_old + (1.0 - beta_first) * gradient]
  transfers between devices with their start and end apart: 5 -> 4, of which waited for: 5 -> 4; matrix products, arithmetic and copies ran while one was open for 15% -> 15% of each run, Pallas kernels for 0% -> 0%
where the time goes in v3:
time: 558 us; the launch traced here: 550 us
  waiting for transfers between devices  356 us (64%)
  matrix products  63.6 us (11%)
  Pallas kernels  54 us (10%)
  other arithmetic  39 us (7%)
  local copies, waits for them, and re-layouts  22.4 us (4%)
  between operations  14.9 us (3%)
    reduce_scatter x1, waiting for transfers between devices, local(): lax.psum_scatter(joined, 'zero', scatter_dimension=0, tiled=True)  145 us
    all_gather x1, waiting for transfers between devices, local(): lax.all_gather(jnp.concatenate(first_mats, axis=1), 'zero', axis=0, tiled...  112 us
    pallas_call x1, Pallas kernels, dp_sum(): pl.pallas_call(partial(dp_sum_kernel, parts), out_shape=jax.ShapeDtypeStr...  54 us
    reduce_scatter x1, waiting for transfers between devices, local(): lax.psum_scatter(local_grads[3].astype(jnp.bfloat16), 'zero', scatter_dim...  51.6 us
    all_gather x1, waiting for transfers between devices, local(): proj_mat = lax.all_gather(proj_shard, 'zero', axis=0, tiled=True)  47.7 us
  transfers between devices with their start and end apart: 4, of which 4 were waited for; matrix products, arithmetic and copies ran while one was open for 15% of the time, Pallas kernels for 0%

profile of v3, /device:TPU:4, one launch (start us, length us, event | category | flops | bytes accessed | tf_op | source)
XLA Modules:
  0.0 550.0 jit_solution(11903020414343987750)
XLA Ops:
  7.2 0.8 convert_bitcast_fusion.1
  8.1 1.3 convert_element_type.111
  9.4 1.0 convert_element_type.110
  10.5 1.1 fusion.50
  11.6 0.4 copy-done.6
  12.0 0.9 convert_element_type.113
  12.9 111.8 %all-gather.3.cloned.1.call-done = bf16[1024,8320]{1,0:T(8,128)(2,1)} async-done(((bf16[64,8320]{1,0:T(8,128)(2,1)}), bf16[1024,8320]{1,0:T(8,128)(2,1)}) %all-gather.3.cloned.1.call-update) | async-done | bytes 17039376 | tf_op jit(solution)/shard_map/all_gather | solution.py:296
  124.8 0.2 fusion.72
  125.2 1.0 convert_bitcast_fusion
  126.2 0.2 slice.79
  126.4 2.1 slice_reduce_fusion.2
  128.5 3.9 fusion.10
  132.5 0.2 copy.75
  132.7 0.2 copy.76
  133.1 0.2 copy.79
  133.3 0.4 convolution_multiply_fusion
  133.7 0.5 convolution_convert_fusion.5
  134.2 2.4 fusion.123
  136.6 0.2 multiply_reduce_fusion.4
  136.8 4.8 fusion.12
  141.6 5.6 %convolution_convert_fusion.1 = bf16[4096,1024]{1,0:T(8,128)(2,1)} fusion(bf16[128,1024]{1,0:T(8,128)(2,1)S(1)} %copy-done.4, f32[128,4096]{1,0:T(8,128)S(1)} %fusion.12), kind=kOutput, calls=%fused_computation.6 | convolution fusion | flops 1082654720 | bytes 10747904 | tf_op jit(solution)/shard_map/dot_general | solution.py:215
  147.2 0.2 reduce-scatter.3.cloned.1.call-start
  147.7 0.2 multiply_reduce_fusion.3
  147.9 2.9 fusion.37
  150.7 47.7 %all-gather.5.cloned.1.call-done = bf16[4096,1024]{1,0:T(8,128)(2,1)} async-done(((bf16[256,1024]{1,0:T(8,128)(2,1)}), bf16[4096,1024]{1,0:T(8,128)(2,1)}) %all-gather.5.cloned.1.call-update) | async-done | bytes 8388624 | tf_op jit(solution)/shard_map/all_gather | solution.py:298
  198.4 7.5 %fusion.118 = (bf16[4096]{0:T(1024)(128)(2,1)S(1)}, bf16[128,4096]{1,0:T(8,128)(2,1)S(1)}) fusion(f32[128,4096]{1,0:T(8,128)S(1)} %fusion.12, bf16[128,1024]{1,0:T(8,128)(2,1)S(1)} %copy-done.4, bf16[4096,1024]{1,0:T(8,128)(2,1)} %all-gather.5.cloned.1.call-done), kind=kOutput, calls=%fused_computation.173 | convolution fusion | flops 1086844928 | bytes 11804672 | tf_op jit(solution)/shard_map/dot_general | solution.py:219
  205.9 7.1 %multiply_reduce_fusion.1 = (bf16[1024]{0:T(1024)(128)(2,1)S(1)}, f32[128]{0:T(128)S(1)}, bf16[1024]{0:T(1024)(128)(2,1)S(1)}, f32[128,1024]{1,0:T(8,128)S(1)}) fusion(f32[128,1024]{1,0:T(8,128)S(1)} %get-tuple-element.32, f32[128]{0:T(128)S(1)} %fusion.100, f32[128]{0:T(128)S(1)} %broadcast_multiply_fusion.1, f32[1024]{0:T(1024)S(1)} %get-tuple-element.41, ...), kind=kOutput, calls=%fused_computation.114 | convolution fusion | flops 1074788224 | bytes 10495488 | tf_op jit(solution)/shard_map/dot_general | solution.py:224
  213.1 0.3 fusion.120
  213.4 2.7 fusion.47
  216.3 0.7 copy-done.25
  217.0 3.0 fusion.121
  219.9 1.3 fusion.126
  221.3 3.0 convolution_convert_fusion.4
  224.3 2.1 fusion.122
  226.4 5.2 fusion.111
  231.7 0.3 fusion.71
  232.2 1.0 fusion.108
  233.4 0.2 copy.84
  233.6 2.2 convolution_convert_fusion.3
  235.7 3.1 copy.85
  238.9 3.1 convolution_convert_fusion.2
  242.0 2.5 convolution_convert_fusion
  244.5 6.6 %fusion.3 = bf16[1024,8320]{1,0:T(8,128)(2,1)} fusion(bf16[1024,12]{1,0:T(8,128)(2,1)S(1)} %bitcast.50, bf16[1024,4096]{1,0:T(8,128)(2,1)S(1)} %convolution_convert_fusion, bf16[1024,1024]{1,0:T(8,128)(2,1)S(1)} %copy.85, bf16[1024,3072]{1,0:T(8,128)(2,1)S(1)} %convolution_convert_fusion.2), kind=kLoop, calls=%fused_computation.4 | loop fusion | flops 85196800 | bytes 33841152 | tf_op jit(solution)/shard_map/concatenate | solution.py:310
  251.2 51.6 %reduce-scatter.5.cloned.1.call-done = bf16[256,1024]{1,0:T(8,128)(2,1)} async-done(((bf16[4096,1024]{1,0:T(8,128)(2,1)}), bf16[256,1024]{1,0:T(8,128)(2,1)}) %reduce-scatter.5.cloned.1.call-update) | async-done | bytes 524304 | tf_op jit(solution)/shard_map/reduce_scatter | solution.py:320
  302.8 1.3 reshape.311
  304.1 5.6 %fusion.46 = bf16[128,1024]{1,0:T(8,128)(2,1)} fusion(f32[128,1024]{1,0:T(8,128)S(1)} %get-tuple-element.32, bf16[4096,1024]{1,0:T(8,128)(2,1)} %all-gather.5.cloned.1.call-done, f32[1024]{0:T(1024)S(1)} %get-tuple-element.42, f32[128,4096]{1,0:T(8,128)S(1)} %copy-done.3), kind=kOutput, calls=%fused_computation.61 | convolution fusion | flops 1078853632 | bytes 11276288 | tf_op jit(solution)/shard_map/dot_general | solution.py:212
  309.7 144.8 %reduce-scatter.3.cloned.1.call-done = bf16[64,8320]{1,0:T(8,128)(2,1)} async-done(((bf16[1024,8320]{1,0:T(8,128)(2,1)}), bf16[64,8320]{1,0:T(8,128)(2,1)}) %reduce-scatter.3.cloned.1.call-update) | async-done | bytes 1064976 | tf_op jit(solution)/shard_map/reduce_scatter | solution.py:319
  454.5 2.7 reshape.310
  457.2 9.1 %maximum_maximum_fusion.x_ref = bf16[6272,128]{1,0:T(8,128)(2,1)} fusion(bf16[2048,128]{1,0:T(8,128)(2,1)S(1)} %reshape.311, bf16[4160,128]{1,0:T(8,128)(2,1)S(1)} %reshape.310, bf16[6272]{0:T(1024)(128)(2,1)S(1)} %pad.12.clone), kind=kLoop, calls=%fused_computation.39 | loop fusion | flops 4816896 | bytes 3207424 | tf_op jit(solution)/shard_map/concatenate | solution.py:122
  466.3 54.0 %shard_map.345 = bf16[6272,128]{1,0:T(8,128)(2,1)} custom-call(bf16[6272,128]{1,0:T(8,128)(2,1)} %maximum_maximum_fusion.x_ref), custom_call_target="tpu_custom_call" | custom-call | tf_op jit(solution)/shard_map/pallas_call | solution.py:98
  520.3 1.4 copy-done.1
  521.7 1.8 convert_multiply_fusion
  523.5 1.2 reshape.312
  524.7 1.4 mul.490
  526.1 2.8 mul.533
  528.8 2.4 mul.538
  531.2 3.6 multiply_subtract_fusion.2
  534.9 1.1 multiply_subtract_fusion.3
  536.0 0.5 copy-done.5
  536.6 2.6 multiply_subtract_fusion.1
  539.2 0.8 multiply_subtract_fusion.4
  540.0 0.2 copy-done.15
  540.2 0.3 copy-done.16
  540.6 2.4 multiply_subtract_fusion
  (110 shorter events, 1.8 us)
Async XLA Ops:
  7.2 3.2 copy-start.11
  7.2 117.4 %all-gather.3.cloned.1.call-start = ((), (), s32[]{:S(2)}) async-start(), calls=%async_computation.2 | async-start | bytes 18104320 | tf_op jit(solution)/shard_map/all_gather | solution.py:296
  10.4 1.6 copy-start.6
  11.5 113.2 %copy-start = (bf16[128,1024]{1,0:T(8,128)(2,1)S(1)}, bf16[128,1024]{1,0:T(8,128)(2,1)}, u32[]{:S(2)}) copy-start(bf16[128,1024]{1,0:T(8,128)(2,1)} %param.18) | copy-start | bytes 786436
  11.5 113.6 %copy-start.34 = (s32[1,128]{1,0:T(1,128)S(1)}, s32[1,128]{1,0:T(1,128)}, u32[]{:S(2)}) copy-start(s32[1,128]{1,0:T(1,128)} %param.20) | copy-start | bytes 1540
  11.5 186.9 %all-gather.5.cloned.1.call-start = ((), (), s32[]{:S(2)}) async-start(), calls=%async_computation.3 | async-start | bytes 8912896 | tf_op jit(solution)/shard_map/all_gather | solution.py:298
  124.7 178.2 %reduce-scatter.5.cloned.1.call-start = ((), (), s32[]{:S(2)}) async-start(), calls=%async_computation.5 | async-start | bytes 8912896 | tf_op jit(solution)/shard_map/reduce_scatter | solution.py:320
  132.7 1.4 copy-start.21
  132.9 1.3 copy-start.23
  133.6 2.9 copy-start.20
  134.1 2.6 copy-start.26
  136.8 4.8 copy-start.4
  141.6 56.8 %copy-start.2 = (f32[128,4096]{1,0:T(8,128)}, f32[128,4096]{1,0:T(8,128)S(1)}, u32[]{:S(2)}) copy-start(f32[128,4096]{1,0:T(8,128)S(1)} %fusion.12) | copy-start | bytes 6291460
  147.2 307.3 %reduce-scatter.3.cloned.1.call-start = ((), (), s32[]{:S(2)}) async-start(), calls=%async_computation.4 | async-start | bytes 18104320 | tf_op jit(solution)/shard_map/reduce_scatter | solution.py:319
  205.9 7.2 %copy-start.17 = (bf16[128,4096]{1,0:T(8,128)(2,1)}, bf16[128,4096]{1,0:T(8,128)(2,1)S(1)}, u32[]{:S(2)}) copy-start(bf16[128,4096]{1,0:T(8,128)(2,1)S(1)} %get-tuple-element.69) | copy-start | bytes 3145732
  216.1 3.9 copy-start.22
  216.1 5.2 copy-start.24
  216.3 0.7 copy-start.25
  221.3 5.1 copy-start.30
  226.4 5.3 copy-start.32
  231.7 1.9 copy-start.27
  235.7 3.2 copy-start.31
  238.9 3.1 copy-start.18
  251.1 53.0 %copy-start.3 = (f32[128,4096]{1,0:T(8,128)S(1)}, f32[128,4096]{1,0:T(8,128)}, u32[]{:S(2)}) copy-start(f32[128,4096]{1,0:T(8,128)} %copy-done.2) | copy-start | bytes 6291460
  520.3 1.4 copy-start.1
  521.7 1.8 slice-start
  526.1 13.9 %copy-start.8 = (f32[256,1024]{1,0:T(8,128)}, f32[256,1024]{1,0:T(8,128)S(1)}, u32[]{:S(2)}) copy-start(f32[256,1024]{1,0:T(8,128)S(1)} %mul.490) | copy-start | bytes 3145732
  526.1 5.1 copy-start.12
  531.2 3.7 copy-start.19
  531.2 3.7 copy-start.28
  531.2 3.7 copy-start.29
  531.2 4.8 copy-start.13
  531.2 4.8 copy-start.14
  534.9 1.6 copy-start.5
  536.5 2.7 copy-start.33
  536.5 2.7 copy-start.35
  536.5 2.7 copy-start.36
  536.5 3.5 copy-start.7
  536.5 3.5 copy-start.9
  536.5 3.5 copy-start.10
  536.5 3.7 copy-start.15
  536.5 4.0 copy-start.16
Sparse Core Ops, SparseCore 0:
  11.7 112.9 all-gather.2
  127.7 70.6 all-gather.4
  202.7 100.0 reduce-scatter.4
  307.0 147.4 reduce-scatter.2

commit v4 on v2

--- a/solution.py
+++ b/solution.py
@@ -3,6 +3,8 @@
 import jax
 import jax.numpy as jnp
 from jax import lax
+from jax.experimental import pallas as pl
+from jax.experimental.pallas import tpu as pltpu
 from jax.sharding import PartitionSpec as P
 
 HEADS = 16
@@ -36,6 +38,76 @@
     return tuple(
         jnp.split(lax.psum_scatter(both, axis, scatter_dimension=dim, tiled=True), ends, axis=along)
     )
+
+
+def dp_sum_kernel(parts, count, *refs):
+    x_refs, out_refs = refs[:count], refs[count : 2 * count]
+    recv_one, recv_two = refs[2 * count : 3 * count], refs[3 * count : 4 * count]
+    mine = refs[4 * count : 5 * count]
+    send_one, got_one, send_two, got_two = refs[5 * count :]
+    me = lax.axis_index("dp")
+    shard = lax.axis_index("zero")
+    barrier = pltpu.get_barrier_semaphore()
+    for k in range(1, parts):
+        pl.semaphore_signal(
+            barrier, inc=1, device_id=(lax.rem(me + k, parts), shard),
+            device_id_type=pl.DeviceIdType.MESH,
+        )
+    pl.semaphore_wait(barrier, parts - 1)
+
+    def send(sources, targets, sends, gots, pick):
+        copies = []
+        for k in range(1, parts):
+            peer = lax.rem(me + k, parts)
+            for i in range(count):
+                copy = pltpu.make_async_remote_copy(
+                    src_ref=pick(sources[i], peer),
+                    dst_ref=targets[i].at[k],
+                    send_sem=sends.at[i, k],
+                    recv_sem=gots.at[i, k],
+                    device_id=(peer, shard),
+                    device_id_type=pl.DeviceIdType.MESH,
+                )
+                copy.start()
+                copies.append(copy)
+        return copies
+
+    first = send(x_refs, recv_one, send_one, got_one, lambda ref, peer: ref.at[peer])
+    totals = [x_refs[i][me].astype(jnp.float32) for i in range(count)]
+    for n, copy in enumerate(first):
+        copy.wait_recv()
+        k, i = n // count + 1, n % count
+        totals[i] = totals[i] + recv_one[i][k].astype(jnp.float32)
+    for i in range(count):
+        mine[i][...] = totals[i].astype(mine[i].dtype)
+        out_refs[i][me] = mine[i][...]
+    second = send(mine, recv_two, send_two, got_two, lambda ref, peer: ref)
+    for copy in first:
+        copy.wait_send()
+    for n, copy in enumerate(second):
+        copy.wait_recv()
+        k, i = n // count + 1, n % count
+        out_refs[i][lax.rem(me + parts - k, parts)] = recv_two[i][k]
+    for copy in second:
+        copy.wait_send()
+
+
+def summed_over_dp(arrays):
+    parts = lax.axis_size("dp")
+    count = len(arrays)
+    stacked = [a.reshape((parts, a.shape[0] // parts) + a.shape[1:]) for a in arrays]
+    vmem = pl.BlockSpec(memory_space=pltpu.VMEM)
+    results = pl.pallas_call(
+        partial(dp_sum_kernel, parts, count),
+        out_shape=[jax.ShapeDtypeStruct(s.shape, s.dtype) for s in stacked],
+        in_specs=[vmem] * count,
+        out_specs=[vmem] * count,
+        scratch_shapes=[pltpu.VMEM(s.shape, s.dtype) for s in stacked] * 2
+        + [pltpu.VMEM(s.shape[1:], s.dtype) for s in stacked]
+        + [pltpu.SemaphoreType.DMA((count, parts))] * 4,
+        compiler_params=pltpu.CompilerParams(collective_id=0, has_side_effects=True),
+    )(*stacked)
+    return [r.reshape(a.shape) for r, a in zip(results, arrays)]
 
 
 def gelu_tanh(inputs):
@@ -230,7 +302,7 @@
     proj_scattered = lax.psum_scatter(
         local_grads[3].astype(jnp.bfloat16), "zero", scatter_dimension=0, tiled=True
     )
-    summed_joined, summed_proj = lax.psum((scattered, proj_scattered), "dp")
+    summed_joined, summed_proj = summed_over_dp((scattered, proj_scattered))
     ends = [w_qkv.shape[1], w_qkv.shape[1] + w_out.shape[1], w_qkv.shape[1] + w_out.shape[1] + w_fc.shape[1]]
     g_qkv, g_out, g_fc, g_vec = jnp.split(summed_joined, ends, axis=1)
     summed = (

time: 556 us -> 527 us (0.948)
  waiting for transfers between devices: 435 us -> 354 us
  Pallas kernels: 0 us -> 53.6 us
    psum x1 -> x0, waiting for transfers between devices: 73.5 us -> none  [local(): summed_joined, summed_proj = lax.psum((scattered, proj_scattered), 'dp')]
    pallas_call x0 -> x1, Pallas kernels: none -> 53.6 us  [summed_over_dp(): pl.pallas_call(partial(dp_sum_kernel, parts, count), out_shape=[jax.Shape...]
    reduce_scatter x1, waiting for transfers between devices: 50.6 us -> 43.3 us  [local(): lax.psum_scatter(local_grads[3].astype(jnp.bfloat16), 'zero', scatter_dim...]
  transfers between devices with their start and end apart: 5 -> 4, of which waited for: 5 -> 4; matrix products, arithmetic and copies ran while one was open for 15% -> 16% of each run, Pallas kernels for 0% -> 0%
where the time goes in v4:
time: 527 us
  waiting for transfers between devices  354 us (67%)
  matrix products  64.8 us (12%)
  Pallas kernels  53.6 us (10%)
  other arithmetic  28.1 us (5%)
  between operations  14.4 us (3%)
  local copies, waits for them, and re-layouts  11.1 us (2%)
    reduce_scatter x1, waiting for transfers between devices, local(): lax.psum_scatter(joined, 'zero', scatter_dimension=0, tiled=True)  152 us
    all_gather x1, waiting for transfers between devices, local(): lax.all_gather(jnp.concatenate(first_mats, axis=1), 'zero', axis=0, tiled...  112 us
    pallas_call x1, Pallas kernels, summed_over_dp(): pl.pallas_call(partial(dp_sum_kernel, parts, count), out_shape=[jax.Shape...  53.6 us
    all_gather x1, waiting for transfers between devices, local(): proj_mat = lax.all_gather(proj_shard, 'zero', axis=0, tiled=True)  47.6 us
    reduce_scatter x1, waiting for transfers between devices, local(): lax.psum_scatter(local_grads[3].astype(jnp.bfloat16), 'zero', scatter_dim...  43.3 us
  transfers between devices with their start and end apart: 4, of which 4 were waited for; matrix products, arithmetic and copies ran while one was open for 16% of the time, Pallas kernels for 0%

profile of v4, /device:TPU:4, one launch (start us, length us, event | category | flops | bytes accessed | tf_op | source)
XLA Modules:
  0.0 526.7 jit_solution(9477297659305530715)
XLA Ops:
  7.2 0.8 convert_bitcast_fusion.1
  8.0 0.1 copy.90
  8.1 1.0 convert_element_type.110
  9.1 1.2 convert_element_type.109
  10.4 1.1 fusion.50
  11.5 0.4 copy-done.7
  11.9 0.9 convert_element_type.113
  12.8 111.8 %all-gather.3.cloned.1.call-done = bf16[1024,8320]{1,0:T(8,128)(2,1)} async-done(((bf16[64,8320]{1,0:T(8,128)(2,1)}), bf16[1024,8320]{1,0:T(8,128)(2,1)}) %all-gather.3.cloned.1.call-update) | async-done | bytes 17039376 | tf_op jit(solution)/shard_map/all_gather | solution.py:278
  124.6 0.1 convert_reduce_fusion
  124.8 0.2 fusion.73
  125.0 0.1 fusion.90
  125.1 1.0 convert_bitcast_fusion
  126.1 0.2 slice.71
  126.3 0.2 copy.79
  126.5 2.1 slice_reduce_fusion.2
  128.6 3.9 fusion.10
  132.5 0.1 fusion.75
  132.7 0.2 copy.76
  132.8 0.2 copy.77
  133.0 0.2 copy.75
  133.2 0.4 convolution_multiply_fusion
  133.6 0.5 convolution_convert_fusion.5
  134.1 2.4 fusion.125
  136.5 0.2 multiply_reduce_fusion.4
  136.7 4.8 fusion.12
  141.5 5.6 %convolution_convert_fusion.1 = bf16[4096,1024]{1,0:T(8,128)(2,1)} fusion(bf16[128,1024]{1,0:T(8,128)(2,1)S(1)} %copy-done.3, f32[128,4096]{1,0:T(8,128)S(1)} %fusion.12), kind=kOutput, calls=%fused_computation.6 | convolution fusion | flops 1082654720 | bytes 10747904 | tf_op jit(solution)/shard_map/dot_general | solution.py:197
  147.2 0.2 reduce-scatter.3.cloned.1.call-start
  147.5 0.1 reduce_sum.191
  147.6 0.2 multiply_reduce_fusion.3
  147.8 3.0 fusion.37
  150.8 47.6 %all-gather.5.cloned.1.call-done = bf16[4096,1024]{1,0:T(8,128)(2,1)} async-done(((bf16[256,1024]{1,0:T(8,128)(2,1)}), bf16[4096,1024]{1,0:T(8,128)(2,1)}) %all-gather.5.cloned.1.call-update) | async-done | bytes 8388624 | tf_op jit(solution)/shard_map/all_gather | solution.py:280
  198.3 8.5 %fusion.120 = (bf16[4096]{0:T(1024)(128)(2,1)S(1)}, bf16[128,4096]{1,0:T(8,128)(2,1)}) fusion(f32[128,4096]{1,0:T(8,128)S(1)} %fusion.12, bf16[128,1024]{1,0:T(8,128)(2,1)S(1)} %copy-done.3, bf16[4096,1024]{1,0:T(8,128)(2,1)} %all-gather.5.cloned.1.call-done), kind=kOutput, calls=%fused_computation.173 | convolution fusion | flops 1086844928 | bytes 11804672 | tf_op jit(solution)/shard_map/dot_general | solution.py:201
  206.8 7.3 %multiply_reduce_fusion.1 = (bf16[1024]{0:T(1024)(128)(2,1)S(1)}, f32[128]{0:T(128)S(1)}, bf16[1024]{0:T(1024)(128)(2,1)S(1)}, f32[128,1024]{1,0:T(8,128)S(1)}) fusion(f32[128,1024]{1,0:T(8,128)S(1)} %get-tuple-element.34, f32[128]{0:T(128)S(1)} %fusion.101, f32[128]{0:T(128)S(1)} %broadcast_multiply_fusion.1, f32[1024]{0:T(1024)S(1)} %get-tuple-element.45, ...), kind=kOutput, calls=%fused_computation.114 | convolution fusion | flops 1074788224 | bytes 10495488 | tf_op jit(solution)/shard_map/dot_general | solution.py:206
  214.2 0.3 fusion.122
  214.4 2.6 fusion.47
  217.1 0.2 copy.80
  217.3 3.1 fusion.123
  220.5 1.3 fusion.128
  221.8 2.9 fusion.124
  224.7 0.1 stack.24
  224.8 2.1 convolution_convert_fusion.4
  226.9 0.7 copy-done.31
  227.6 5.2 fusion.112
  232.8 0.3 fusion.72
  233.2 1.0 fusion.109
  234.3 0.2 copy.84
  234.5 2.2 convolution_convert_fusion.3
  236.7 3.1 copy.85
  239.9 3.1 convolution_convert_fusion.2
  243.0 2.5 convolution_convert_fusion
  245.4 6.6 %fusion.3 = bf16[1024,8320]{1,0:T(8,128)(2,1)} fusion(bf16[1024,12]{1,0:T(8,128)(2,1)S(1)} %bitcast.65, bf16[1024,4096]{1,0:T(8,128)(2,1)S(1)} %convolution_convert_fusion, bf16[1024,1024]{1,0:T(8,128)(2,1)S(1)} %copy.85, bf16[1024,3072]{1,0:T(8,128)(2,1)S(1)} %convolution_convert_fusion.2), kind=kLoop, calls=%fused_computation.4 | loop fusion | flops 85196800 | bytes 33841152 | tf_op jit(solution)/shard_map/concatenate | solution.py:292
  252.1 1.6 copy-done.2
  253.7 5.8 %fusion.46 = bf16[128,1024]{1,0:T(8,128)(2,1)} fusion(f32[128,1024]{1,0:T(8,128)S(1)} %get-tuple-element.34, bf16[4096,1024]{1,0:T(8,128)(2,1)} %all-gather.5.cloned.1.call-done, f32[1024]{0:T(1024)S(1)} %get-tuple-element.46, f32[128,4096]{1,0:T(8,128)S(1)} %copy-done.2), kind=kOutput, calls=%fused_computation.60 | convolution fusion | flops 1078853632 | bytes 11276288 | tf_op jit(solution)/shard_map/dot_general | solution.py:194
  259.5 43.3 %reduce-scatter.5.cloned.1.call-done = bf16[256,1024]{1,0:T(8,128)(2,1)} async-done(((bf16[4096,1024]{1,0:T(8,128)(2,1)}), bf16[256,1024]{1,0:T(8,128)(2,1)}) %reduce-scatter.5.cloned.1.call-update) | async-done | bytes 524304 | tf_op jit(solution)/shard_map/reduce_scatter | solution.py:302
  302.7 151.6 %reduce-scatter.3.cloned.1.call-done = bf16[64,8320]{1,0:T(8,128)(2,1)} async-done(((bf16[1024,8320]{1,0:T(8,128)(2,1)}), bf16[64,8320]{1,0:T(8,128)(2,1)}) %reduce-scatter.3.cloned.1.call-update) | async-done | bytes 1064976 | tf_op jit(solution)/shard_map/reduce_scatter | solution.py:301
  454.4 53.6 %shard_map.345 = (bf16[8,8,8320]{2,1,0:T(8,128)(2,1)}, bf16[8,32,1024]{2,1,0:T(8,128)(2,1)}) custom-call(bf16[8,8,8320]{2,1,0:T(8,128)(2,1)} %bitcast.64, bf16[8,32,1024]{2,1,0:T(8,128)(2,1)} %bitcast.80), custom_call_target="tpu_custom_call" | custom-call | tf_op jit(solution)/shard_map/pallas_call | solution.py:100
  508.1 1.6 convert_multiply_fusion
  509.7 0.9 multiply_subtract_fusion.4
  510.6 1.1 multiply_subtract_fusion.3
  511.8 2.1 multiply_subtract_fusion.2
  513.9 0.8 copy-done.11
  514.8 2.6 multiply_subtract_fusion.1
  517.4 0.4 copy-done.13
  517.8 2.3 multiply_subtract_fusion
  (97 shorter events, 0.8 us)
Async XLA Ops:
  7.2 3.1 copy-start.5
  7.2 117.4 %all-gather.3.cloned.1.call-start = ((), (), s32[]{:S(2)}) async-start(), calls=%async_computation.2 | async-start | bytes 18104320 | tf_op jit(solution)/shard_map/all_gather | solution.py:278
  10.3 1.6 copy-start.7
  11.4 113.2 %copy-start = (bf16[128,1024]{1,0:T(8,128)(2,1)S(1)}, bf16[128,1024]{1,0:T(8,128)(2,1)}, u32[]{:S(2)}) copy-start(bf16[128,1024]{1,0:T(8,128)(2,1)} %param.18) | copy-start | bytes 786436
  11.4 113.6 %copy-start.33 = (s32[1,128]{1,0:T(1,128)S(1)}, s32[1,128]{1,0:T(1,128)}, u32[]{:S(2)}) copy-start(s32[1,128]{1,0:T(1,128)} %param.20) | copy-start | bytes 1540
  11.5 186.9 %all-gather.5.cloned.1.call-start = ((), (), s32[]{:S(2)}) async-start(), calls=%async_computation.3 | async-start | bytes 8912896 | tf_op jit(solution)/shard_map/all_gather | solution.py:280
  124.6 178.1 %reduce-scatter.5.cloned.1.call-start = ((), (), s32[]{:S(2)}) async-start(), calls=%async_computation.5 | async-start | bytes 8912896 | tf_op jit(solution)/shard_map/reduce_scatter | solution.py:302
  133.0 1.1 copy-start.17
  133.2 0.9 copy-start.19
  133.6 3.1 copy-start.16
  134.0 2.6 copy-start.22
  136.7 4.8 copy-start.3
  141.5 56.8 %copy-start.1 = (f32[128,4096]{1,0:T(8,128)}, f32[128,4096]{1,0:T(8,128)S(1)}, u32[]{:S(2)}) copy-start(f32[128,4096]{1,0:T(8,128)S(1)} %fusion.12) | copy-start | bytes 6291460
  147.2 307.2 %reduce-scatter.3.cloned.1.call-start = ((), (), s32[]{:S(2)}) async-start(), calls=%async_computation.4 | async-start | bytes 18104320 | tf_op jit(solution)/shard_map/reduce_scatter | solution.py:301
  217.1 3.4 copy-start.20
  217.1 4.7 copy-start.18
  217.3 3.1 copy-start.21
  221.8 5.8 %copy-start.29 = (bf16[1,128,16,64]{1,3,2,0:T(8,128)(2,1)S(1)}, bf16[1,128,16,64]{1,3,2,0:T(8,128)(2,1)}, u32[]{:S(2)}) copy-start(bf16[1,128,16,64]{1,3,2,0:T(8,128)(2,1)} %get-tuple-element.84) | copy-start | bytes 786436
  226.9 0.7 copy-start.31
  232.8 1.7 copy-start.23
  236.7 3.2 copy-start.30
  239.8 3.1 copy-start.14
  252.1 1.6 copy-start.2
  508.0 1.7 copy-start.24
  508.0 1.7 copy-start.32
  508.0 1.7 copy-start.34
  508.0 1.7 copy-start.35
  508.0 2.6 copy-start.15
  508.0 2.6 copy-start.27
  508.0 2.6 copy-start.28
  508.0 3.7 copy-start.9
  508.1 3.7 copy-start.25
  508.1 3.7 copy-start.26
  509.7 7.7 %copy-start.4 = (f32[8,32,1024]{2,1,0:T(8,128)}, f32[8,32,1024]{2,1,0:T(8,128)S(1)}, u32[]{:S(2)}) copy-start(f32[8,32,1024]{2,1,0:T(8,128)S(1)} %get-tuple-element.82) | copy-start | bytes 3145732
  511.8 2.2 copy-start.6
  511.8 2.2 copy-start.10
  511.8 3.0 copy-start.11
  514.8 2.7 copy-start.8
  514.8 2.7 copy-start.12
  514.8 3.0 copy-start.13
Sparse Core Ops, SparseCore 0:
  11.6 112.9 all-gather.2
  127.6 70.6 all-gather.4
  202.6 100.0 reduce-scatter.4
  306.9 147.3 reduce-scatter.2

commit v5 on v4

--- a/solution.py
+++ b/solution.py
@@ -92,7 +92,7 @@
         copy.wait_send()
 
 
-def summed_over_dp(arrays):
+def summed_over_dp(arrays, slot):
     parts = lax.axis_size("dp")
     count = len(arrays)
     stacked = [a.reshape((parts, a.shape[0] // parts) + a.shape[1:]) for a in arrays]
@@ -105,7 +105,7 @@
         scratch_shapes=[pltpu.VMEM(s.shape, s.dtype) for s in stacked] * 2
         + [pltpu.VMEM(s.shape[1:], s.dtype) for s in stacked]
         + [pltpu.SemaphoreType.DMA((count, parts))] * 4,
-        compiler_params=pltpu.CompilerParams(collective_id=0, has_side_effects=True),
+        compiler_params=pltpu.CompilerParams(collective_id=slot, has_side_effects=True),
     )(*stacked)
     return [r.reshape(a.shape) for r, a in zip(results, arrays)]
 
@@ -302,7 +302,8 @@
     proj_scattered = lax.psum_scatter(
         local_grads[3].astype(jnp.bfloat16), "zero", scatter_dimension=0, tiled=True
     )
-    summed_joined, summed_proj = summed_over_dp((scattered, proj_scattered))
+    (summed_proj,) = summed_over_dp((proj_scattered,), 1)
+    (summed_joined,) = summed_over_dp((scattered,), 0)
     ends = [w_qkv.shape[1], w_qkv.shape[1] + w_out.shape[1], w_qkv.shape[1] + w_out.shape[1] + w_fc.shape[1]]
     g_qkv, g_out, g_fc, g_vec = jnp.split(summed_joined, ends, axis=1)
     summed = (

time: 527 us -> 506 us (0.960)
  waiting for transfers between devices: 354 us -> 331 us
    reduce_scatter x1, waiting for transfers between devices: 152 us -> 121 us  [local(): lax.psum_scatter(joined, 'zero', scatter_dimension=0, tiled=True)]
    reduce_scatter x1, waiting for transfers between devices: 43.3 us -> 51.2 us  [local(): lax.psum_scatter(local_grads[3].astype(jnp.bfloat16), 'zero', scatter_dim...]
    pallas_call x1 -> x2, Pallas kernels: 53.6 us -> 50.4 us  [summed_over_dp(): pl.pallas_call(partial(dp_sum_kernel, parts, count), out_shape=[jax.Shape...]
  transfers between devices with their start and end apart: 4 -> 4, of which waited for: 4 -> 4; matrix products, arithmetic and copies ran while one was open for 16% -> 18% of each run, Pallas kernels for 0% -> 4%
where the time goes in v5:
time: 506 us; the launch traced here: 502 us
  waiting for transfers between devices  331 us (65%)
  matrix products  67 us (13%)
  Pallas kernels  50.4 us (10%)
  other arithmetic  29.1 us (6%)
  between operations  14.4 us (3%)
  local copies, waits for them, and re-layouts  10 us (2%)
    reduce_scatter x1, waiting for transfers between devices, local(): lax.psum_scatter(joined, 'zero', scatter_dimension=0, tiled=True)  121 us
    all_gather x1, waiting for transfers between devices, local(): lax.all_gather(jnp.concatenate(first_mats, axis=1), 'zero', axis=0, tiled...  112 us
    reduce_scatter x1, waiting for transfers between devices, local(): lax.psum_scatter(local_grads[3].astype(jnp.bfloat16), 'zero', scatter_dim...  51.2 us
    pallas_call x2, Pallas kernels, summed_over_dp(): pl.pallas_call(partial(dp_sum_kernel, parts, count), out_shape=[jax.Shape...  50.4 us
    all_gather x1, waiting for transfers between devices, local(): proj_mat = lax.all_gather(proj_shard, 'zero', axis=0, tiled=True)  47.6 us
  transfers between devices with their start and end apart: 4, of which 4 were waited for; matrix products, arithmetic and copies ran while one was open for 18% of the time, Pallas kernels for 4%

profile of v5, /device:TPU:4, one launch (start us, length us, event | category | flops | bytes accessed | tf_op | source)
XLA Modules:
  0.0 502.4 jit_solution(5881419920177301128)
XLA Ops:
  7.2 0.8 convert_bitcast_fusion.1
  8.0 0.1 copy.90
  8.1 1.0 convert_element_type.110
  9.1 1.2 convert_element_type.109
  10.4 1.1 fusion.50
  11.5 0.4 copy-done.6
  11.9 0.9 convert_element_type.113
  12.8 111.8 %all-gather.3.cloned.1.call-done = bf16[1024,8320]{1,0:T(8,128)(2,1)} async-done(((bf16[64,8320]{1,0:T(8,128)(2,1)}), bf16[1024,8320]{1,0:T(8,128)(2,1)}) %all-gather.3.cloned.1.call-update) | async-done | bytes 17039376 | tf_op jit(solution)/shard_map/all_gather | solution.py:278
  124.6 0.1 convert_reduce_fusion
  124.8 0.2 fusion.73
  125.0 0.1 fusion.90
  125.1 1.0 convert_bitcast_fusion
  126.1 0.2 slice.71
  126.3 0.2 copy.79
  126.5 2.1 slice_reduce_fusion.2
  128.6 3.9 fusion.10
  132.5 0.1 fusion.75
  132.6 0.2 copy.76
  132.8 0.2 copy.77
  133.0 0.2 copy.75
  133.2 0.4 convolution_multiply_fusion
  133.6 0.5 convolution_convert_fusion.5
  134.1 2.4 fusion.125
  136.5 0.2 multiply_reduce_fusion.4
  136.7 4.8 fusion.12
  141.5 5.6 %convolution_convert_fusion.1 = bf16[4096,1024]{1,0:T(8,128)(2,1)} fusion(bf16[128,1024]{1,0:T(8,128)(2,1)S(1)} %copy-done.4, f32[128,4096]{1,0:T(8,128)S(1)} %fusion.12), kind=kOutput, calls=%fused_computation.6 | convolution fusion | flops 1082654720 | bytes 10747904 | tf_op jit(solution)/shard_map/dot_general | solution.py:197
  147.2 0.2 reduce-scatter.3.cloned.1.call-start
  147.5 0.1 reduce_sum.191
  147.6 0.2 multiply_reduce_fusion.3
  147.8 3.0 fusion.37
  150.8 47.6 %all-gather.5.cloned.1.call-done = bf16[4096,1024]{1,0:T(8,128)(2,1)} async-done(((bf16[256,1024]{1,0:T(8,128)(2,1)}), bf16[4096,1024]{1,0:T(8,128)(2,1)}) %all-gather.5.cloned.1.call-update) | async-done | bytes 8388624 | tf_op jit(solution)/shard_map/all_gather | solution.py:280
  198.3 8.5 %fusion.120 = (bf16[4096]{0:T(1024)(128)(2,1)S(1)}, bf16[128,4096]{1,0:T(8,128)(2,1)}) fusion(f32[128,4096]{1,0:T(8,128)S(1)} %fusion.12, bf16[128,1024]{1,0:T(8,128)(2,1)S(1)} %copy-done.4, bf16[4096,1024]{1,0:T(8,128)(2,1)} %all-gather.5.cloned.1.call-done), kind=kOutput, calls=%fused_computation.173 | convolution fusion | flops 1086844928 | bytes 11804672 | tf_op jit(solution)/shard_map/dot_general | solution.py:201
  206.8 7.3 %multiply_reduce_fusion.1 = (bf16[1024]{0:T(1024)(128)(2,1)S(1)}, f32[128]{0:T(128)S(1)}, bf16[1024]{0:T(1024)(128)(2,1)S(1)}, f32[128,1024]{1,0:T(8,128)S(1)}) fusion(f32[128,1024]{1,0:T(8,128)S(1)} %get-tuple-element.32, f32[128]{0:T(128)S(1)} %fusion.101, f32[128]{0:T(128)S(1)} %broadcast_multiply_fusion.1, f32[1024]{0:T(1024)S(1)} %get-tuple-element.41, ...), kind=kOutput, calls=%fused_computation.114 | convolution fusion | flops 1074788224 | bytes 10495488 | tf_op jit(solution)/shard_map/dot_general | solution.py:206
  214.2 0.3 fusion.122
  214.4 2.6 fusion.47
  217.1 0.2 copy.80
  217.3 3.1 fusion.123
  220.5 1.3 fusion.128
  221.8 2.9 fusion.124
  224.8 2.1 convolution_convert_fusion.4
  226.9 5.2 %fusion.112 = (bf16[1024]{0:T(1024)(128)(2,1)S(1)}, f32[128]{0:T(128)S(1)}, f32[128,1024]{1,0:T(8,128)S(1)}) fusion(f32[1024]{0:T(1024)S(1)} %get-tuple-element.48, f32[128]{0:T(128)S(1)} %broadcast_multiply_fusion.3, bf16[128,1024]{1,0:T(8,128)(2,1)S(1)} %copy-done, bf16[1024,8320]{1,0:T(8,128)(2,1)} %all-gather.3.cloned.1.call-done, ...), kind=kOutput, calls=%fused_computation.172 | convolution fusion | flops 808450944 | bytes 7871488 | tf_op jit(solution)/shard_map/dot_general | solution.py:224
  232.2 0.3 fusion.72
  232.6 1.0 fusion.109
  233.7 0.2 copy.84
  233.9 2.2 convolution_convert_fusion.3
  236.1 3.2 copy.85
  239.3 3.1 convolution_convert_fusion.2
  242.4 2.5 convolution_convert_fusion
  244.8 6.6 %fusion.3 = bf16[1024,8320]{1,0:T(8,128)(2,1)} fusion(bf16[1024,12]{1,0:T(8,128)(2,1)S(1)} %bitcast.69, bf16[1024,4096]{1,0:T(8,128)(2,1)S(1)} %convolution_convert_fusion, bf16[1024,1024]{1,0:T(8,128)(2,1)S(1)} %copy.85, bf16[1024,3072]{1,0:T(8,128)(2,1)S(1)} %convolution_convert_fusion.2), kind=kLoop, calls=%fused_computation.4 | loop fusion | flops 85196800 | bytes 33841152 | tf_op jit(solution)/shard_map/concatenate | solution.py:292
  251.5 51.2 %reduce-scatter.5.cloned.1.call-done = bf16[256,1024]{1,0:T(8,128)(2,1)} async-done(((bf16[4096,1024]{1,0:T(8,128)(2,1)}), bf16[256,1024]{1,0:T(8,128)(2,1)}) %reduce-scatter.5.cloned.1.call-update) | async-done | bytes 524304 | tf_op jit(solution)/shard_map/reduce_scatter | solution.py:302
  302.7 18.2 %shard_map.346 = bf16[8,32,1024]{2,1,0:T(8,128)(2,1)} custom-call(bf16[8,32,1024]{2,1,0:T(8,128)(2,1)} %bitcast.80), custom_call_target="tpu_custom_call" | custom-call | tf_op jit(solution)/shard_map/pallas_call | solution.py:100
  321.0 1.7 convert_multiply_fusion
  322.7 0.5 copy-done.11
  323.2 0.8 copy-done.12
  323.9 2.3 multiply_subtract_fusion
  326.2 0.4 copy-done.2
  326.7 7.2 %fusion.46 = bf16[128,1024]{1,0:T(8,128)(2,1)} fusion(f32[128,1024]{1,0:T(8,128)S(1)} %get-tuple-element.32, bf16[4096,1024]{1,0:T(8,128)(2,1)} %all-gather.5.cloned.1.call-done, f32[1024]{0:T(1024)S(1)} %get-tuple-element.42, f32[128,4096]{1,0:T(8,128)S(1)} %copy-done.2), kind=kOutput, calls=%fused_computation.60 | convolution fusion | flops 1078853632 | bytes 11276288 | tf_op jit(solution)/shard_map/dot_general | solution.py:194
  333.8 120.5 %reduce-scatter.3.cloned.1.call-done = bf16[64,8320]{1,0:T(8,128)(2,1)} async-done(((bf16[1024,8320]{1,0:T(8,128)(2,1)}), bf16[64,8320]{1,0:T(8,128)(2,1)}) %reduce-scatter.3.cloned.1.call-update) | async-done | bytes 1064976 | tf_op jit(solution)/shard_map/reduce_scatter | solution.py:301
  454.4 32.2 %shard_map.345 = bf16[8,8,8320]{2,1,0:T(8,128)(2,1)} custom-call(bf16[8,8,8320]{2,1,0:T(8,128)(2,1)} %bitcast.68), custom_call_target="tpu_custom_call" | custom-call | tf_op jit(solution)/shard_map/pallas_call | solution.py:100
  486.6 1.6 multiply_subtract_fusion.4
  488.2 2.0 multiply_subtract_fusion.3
  490.3 2.1 multiply_subtract_fusion.2
  492.4 0.8 copy-done.14
  493.2 2.6 multiply_subtract_fusion.1
  (98 shorter events, 0.9 us)
Async XLA Ops:
  7.2 3.1 copy-start.8
  7.2 117.4 %all-gather.3.cloned.1.call-start = ((), (), s32[]{:S(2)}) async-start(), calls=%async_computation.2 | async-start | bytes 18104320 | tf_op jit(solution)/shard_map/all_gather | solution.py:278
  10.3 1.6 copy-start.6
  11.4 113.2 %copy-start = (bf16[128,1024]{1,0:T(8,128)(2,1)S(1)}, bf16[128,1024]{1,0:T(8,128)(2,1)}, u32[]{:S(2)}) copy-start(bf16[128,1024]{1,0:T(8,128)(2,1)} %param.18) | copy-start | bytes 786436
  11.4 113.6 %copy-start.33 = (s32[1,128]{1,0:T(1,128)S(1)}, s32[1,128]{1,0:T(1,128)}, u32[]{:S(2)}) copy-start(s32[1,128]{1,0:T(1,128)} %param.20) | copy-start | bytes 1540
  11.5 186.9 %all-gather.5.cloned.1.call-start = ((), (), s32[]{:S(2)}) async-start(), calls=%async_computation.3 | async-start | bytes 8912896 | tf_op jit(solution)/shard_map/all_gather | solution.py:280
  124.6 178.1 %reduce-scatter.5.cloned.1.call-start = ((), (), s32[]{:S(2)}) async-start(), calls=%async_computation.5 | async-start | bytes 8912896 | tf_op jit(solution)/shard_map/reduce_scatter | solution.py:302
  133.0 1.1 copy-start.18
  133.2 0.9 copy-start.20
  133.6 3.1 copy-start.17
  134.0 2.6 copy-start.23
  136.7 4.8 copy-start.4
  141.5 56.8 %copy-start.1 = (f32[128,4096]{1,0:T(8,128)}, f32[128,4096]{1,0:T(8,128)S(1)}, u32[]{:S(2)}) copy-start(f32[128,4096]{1,0:T(8,128)S(1)} %fusion.12) | copy-start | bytes 6291460
  147.2 307.2 %reduce-scatter.3.cloned.1.call-start = ((), (), s32[]{:S(2)}) async-start(), calls=%async_computation.4 | async-start | bytes 18104320 | tf_op jit(solution)/shard_map/reduce_scatter | solution.py:301
  217.1 3.4 copy-start.21
  217.1 4.7 copy-start.19
  217.3 3.1 copy-start.22
  221.8 5.1 %copy-start.29 = (bf16[1,128,16,64]{1,3,2,0:T(8,128)(2,1)S(1)}, bf16[1,128,16,64]{1,3,2,0:T(8,128)(2,1)}, u32[]{:S(2)}) copy-start(bf16[1,128,16,64]{1,3,2,0:T(8,128)(2,1)} %get-tuple-element.80) | copy-start | bytes 786436
  226.9 5.3 %copy-start.31 = (bf16[16,64,128]{2,1,0:T(8,128)(2,1)}, bf16[16,64,128]{2,1,0:T(8,128)(2,1)S(1)}, u32[]{:S(2)}) copy-start(bf16[16,64,128]{2,1,0:T(8,128)(2,1)S(1)} %convolution_convert_fusion.4) | copy-start | bytes 786436
  232.2 1.7 copy-start.24
  236.1 3.2 copy-start.30
  239.3 3.1 copy-start.15
  320.9 1.7 copy-start.7
  321.0 2.2 copy-start.11
  321.0 3.0 copy-start.12
  322.7 3.6 copy-start.5
  323.9 2.7 copy-start.2
  326.6 159.9 %copy-start.32 = (f32[12,64]{1,0:T(8,128)S(1)}, f32[12,64]{1,0:T(8,128)}, u32[]{:S(2)}) copy-start(f32[12,64]{1,0:T(8,128)} %param.25) | copy-start | bytes 9220
  326.7 159.9 %copy-start.34 = (f32[12,64]{1,0:T(8,128)S(1)}, f32[12,64]{1,0:T(8,128)}, u32[]{:S(2)}) copy-start(f32[12,64]{1,0:T(8,128)} %param.30) | copy-start | bytes 9220
  326.7 159.9 %copy-start.35 = (f32[12,64]{1,0:T(8,128)S(1)}, f32[12,64]{1,0:T(8,128)}, u32[]{:S(2)}) copy-start(f32[12,64]{1,0:T(8,128)} %param.35) | copy-start | bytes 9220
  326.7 161.5 %copy-start.27 = (f32[64,1024]{1,0:T(8,128)S(1)}, f32[64,1024]{1,0:T(8,128)}, u32[]{:S(2)}) copy-start(f32[64,1024]{1,0:T(8,128)} %param.27) | copy-start | bytes 786436
  326.7 161.5 %copy-start.28 = (f32[64,1024]{1,0:T(8,128)S(1)}, f32[64,1024]{1,0:T(8,128)}, u32[]{:S(2)}) copy-start(f32[64,1024]{1,0:T(8,128)} %param.32) | copy-start | bytes 786436
  333.8 154.4 %copy-start.16 = (f32[64,1024]{1,0:T(8,128)S(1)}, f32[64,1024]{1,0:T(8,128)}, u32[]{:S(2)}) copy-start(f32[64,1024]{1,0:T(8,128)} %param.22) | copy-start | bytes 786436
  333.8 156.4 %copy-start.10 = (f32[64,3072]{1,0:T(8,128)S(1)}, f32[64,3072]{1,0:T(8,128)}, u32[]{:S(2)}) copy-start(f32[64,3072]{1,0:T(8,128)} %param.21) | copy-start | bytes 2359300
  333.8 156.4 %copy-start.25 = (f32[64,3072]{1,0:T(8,128)S(1)}, f32[64,3072]{1,0:T(8,128)}, u32[]{:S(2)}) copy-start(f32[64,3072]{1,0:T(8,128)} %param.26) | copy-start | bytes 2359300
  333.8 156.4 %copy-start.26 = (f32[64,3072]{1,0:T(8,128)S(1)}, f32[64,3072]{1,0:T(8,128)}, u32[]{:S(2)}) copy-start(f32[64,3072]{1,0:T(8,128)} %param.31) | copy-start | bytes 2359300
  486.5 3.7 copy-start.3
  490.2 2.2 copy-start.9
  490.2 2.2 copy-start.13
  490.2 3.0 copy-start.14
Sparse Core Ops, SparseCore 0:
  11.6 112.9 all-gather.2
  127.6 70.6 all-gather.4
  202.6 100.0 reduce-scatter.4
  306.9 147.3 reduce-scatter.2

commit v6 on v5

--- a/solution.py
+++ b/solution.py
@@ -42,9 +42,9 @@
 
 def dp_sum_kernel(parts, count, *refs):
     x_refs, out_refs = refs[:count], refs[count : 2 * count]
-    recv_one, recv_two = refs[2 * count : 3 * count], refs[3 * count : 4 * count]
-    mine = refs[4 * count : 5 * count]
-    send_one, got_one, send_two, got_two = refs[5 * count :]
+    recv_one = refs[2 * count : 3 * count]
+    mine = refs[3 * count : 4 * count]
+    send_one, got_one, send_two, got_two = refs[4 * count :]
     me = lax.axis_index("dp")
     shard = lax.axis_index("zero")
     barrier = pltpu.get_barrier_semaphore()
@@ -81,13 +81,24 @@
     for i in range(count):
         mine[i][...] = totals[i].astype(mine[i].dtype)
         out_refs[i][me] = mine[i][...]
-    second = send(mine, recv_two, send_two, got_two, lambda ref, peer: ref)
+    second = []
+    for k in range(1, parts):
+        peer = lax.rem(me + k, parts)
+        for i in range(count):
+            copy = pltpu.make_async_remote_copy(
+                src_ref=mine[i],
+                dst_ref=out_refs[i].at[me],
+                send_sem=send_two.at[i, k],
+                recv_sem=got_two.at[i, k],
+                device_id=(peer, shard),
+                device_id_type=pl.DeviceIdType.MESH,
+            )
+            copy.start()
+            second.append(copy)
     for copy in first:
         copy.wait_send()
-    for n, copy in enumerate(second):
+    for copy in second:
         copy.wait_recv()
-        k, i = n // count + 1, n % count
-        out_refs[i][lax.rem(me + parts - k, parts)] = recv_two[i][k]
     for copy in second:
         copy.wait_send()
 
@@ -102,7 +113,7 @@
         out_shape=[jax.ShapeDtypeStruct(s.shape, s.dtype) for s in stacked],
         in_specs=[vmem] * count,
         out_specs=[vmem] * count,
-        scratch_shapes=[pltpu.VMEM(s.shape, s.dtype) for s in stacked] * 2
+        scratch_shapes=[pltpu.VMEM(s.shape, s.dtype) for s in stacked]
         + [pltpu.VMEM(s.shape[1:], s.dtype) for s in stacked]
         + [pltpu.SemaphoreType.DMA((count, parts))] * 4,
         compiler_params=pltpu.CompilerParams(collective_id=slot, has_side_effects=True),

time: 506 us -> 506 us (level)
  no operation moved by 1% of the time
where the time goes in v6:
time: 506 us; the launch traced here: 502 us
  waiting for transfers between devices  331 us (65%)
  matrix products  67 us (13%)
  Pallas kernels  50.4 us (10%)
  other arithmetic  29.1 us (6%)
  between operations  14.4 us (3%)
  local copies, waits for them, and re-layouts  10 us (2%)
    reduce_scatter x1, waiting for transfers between devices, local(): lax.psum_scatter(joined, 'zero', scatter_dimension=0, tiled=True)  121 us
    all_gather x1, waiting for transfers between devices, local(): lax.all_gather(jnp.concatenate(first_mats, axis=1), 'zero', axis=0, tiled...  112 us
    reduce_scatter x1, waiting for transfers between devices, local(): lax.psum_scatter(local_grads[3].astype(jnp.bfloat16), 'zero', scatter_dim...  51.2 us
    pallas_call x2, Pallas kernels, summed_over_dp(): pl.pallas_call(partial(dp_sum_kernel, parts, count), out_shape=[jax.Shape...  50.4 us
    all_gather x1, waiting for transfers between devices, local(): proj_mat = lax.all_gather(proj_shard, 'zero', axis=0, tiled=True)  47.6 us
  transfers between devices with their start and end apart: 4, of which 4 were waited for; matrix products, arithmetic and copies ran while one was open for 18% of the time, Pallas kernels for 4%

profile of v6, /device:TPU:4, one launch (start us, length us, event | category | flops | bytes accessed | tf_op | source)
XLA Modules:
  0.0 502.4 jit_solution(13183887075522422128)
XLA Ops:
  7.2 0.8 convert_bitcast_fusion.1
  8.0 0.1 copy.90
  8.1 1.0 convert_element_type.110
  9.1 1.2 convert_element_type.109
  10.4 1.1 fusion.50
  11.5 0.4 copy-done.6
  11.9 0.9 convert_element_type.113
  12.8 111.8 %all-gather.3.cloned.1.call-done = bf16[1024,8320]{1,0:T(8,128)(2,1)} async-done(((bf16[64,8320]{1,0:T(8,128)(2,1)}), bf16[1024,8320]{1,0:T(8,128)(2,1)}) %all-gather.3.cloned.1.call-update) | async-done | bytes 17039376 | tf_op jit(solution)/shard_map/all_gather | solution.py:289
  124.6 0.1 convert_reduce_fusion
  124.8 0.2 fusion.73
  125.0 0.1 fusion.90
  125.1 1.0 convert_bitcast_fusion
  126.1 0.2 slice.71
  126.3 0.2 copy.79
  126.5 2.1 slice_reduce_fusion.2
  128.6 3.9 fusion.10
  132.5 0.1 fusion.75
  132.6 0.2 copy.76
  132.8 0.2 copy.77
  133.0 0.2 copy.75
  133.2 0.4 convolution_multiply_fusion
  133.6 0.5 convolution_convert_fusion.5
  134.1 2.4 fusion.125
  136.5 0.2 multiply_reduce_fusion.4
  136.7 4.8 fusion.12
  141.5 5.6 %convolution_convert_fusion.1 = bf16[4096,1024]{1,0:T(8,128)(2,1)} fusion(bf16[128,1024]{1,0:T(8,128)(2,1)S(1)} %copy-done.4, f32[128,4096]{1,0:T(8,128)S(1)} %fusion.12), kind=kOutput, calls=%fused_computation.6 | convolution fusion | flops 1082654720 | bytes 10747904 | tf_op jit(solution)/shard_map/dot_general | solution.py:208
  147.2 0.2 reduce-scatter.3.cloned.1.call-start
  147.5 0.1 reduce_sum.191
  147.6 0.2 multiply_reduce_fusion.3
  147.8 3.0 fusion.37
  150.8 47.6 %all-gather.5.cloned.1.call-done = bf16[4096,1024]{1,0:T(8,128)(2,1)} async-done(((bf16[256,1024]{1,0:T(8,128)(2,1)}), bf16[4096,1024]{1,0:T(8,128)(2,1)}) %all-gather.5.cloned.1.call-update) | async-done | bytes 8388624 | tf_op jit(solution)/shard_map/all_gather | solution.py:291
  198.3 8.5 %fusion.120 = (bf16[4096]{0:T(1024)(128)(2,1)S(1)}, bf16[128,4096]{1,0:T(8,128)(2,1)}) fusion(f32[128,4096]{1,0:T(8,128)S(1)} %fusion.12, bf16[128,1024]{1,0:T(8,128)(2,1)S(1)} %copy-done.4, bf16[4096,1024]{1,0:T(8,128)(2,1)} %all-gather.5.cloned.1.call-done), kind=kOutput, calls=%fused_computation.173 | convolution fusion | flops 1086844928 | bytes 11804672 | tf_op jit(solution)/shard_map/dot_general | solution.py:212
  206.8 7.3 %multiply_reduce_fusion.1 = (bf16[1024]{0:T(1024)(128)(2,1)S(1)}, f32[128]{0:T(128)S(1)}, bf16[1024]{0:T(1024)(128)(2,1)S(1)}, f32[128,1024]{1,0:T(8,128)S(1)}) fusion(f32[128,1024]{1,0:T(8,128)S(1)} %get-tuple-element.32, f32[128]{0:T(128)S(1)} %fusion.101, f32[128]{0:T(128)S(1)} %broadcast_multiply_fusion.1, f32[1024]{0:T(1024)S(1)} %get-tuple-element.41, ...), kind=kOutput, calls=%fused_computation.114 | convolution fusion | flops 1074788224 | bytes 10495488 | tf_op jit(solution)/shard_map/dot_general | solution.py:217
  214.2 0.3 fusion.122
  214.4 2.6 fusion.47
  217.1 0.2 copy.80
  217.3 3.1 fusion.123
  220.5 1.3 fusion.128
  221.8 2.9 fusion.124
  224.8 2.1 convolution_convert_fusion.4
  226.9 5.2 %fusion.112 = (bf16[1024]{0:T(1024)(128)(2,1)S(1)}, f32[128]{0:T(128)S(1)}, f32[128,1024]{1,0:T(8,128)S(1)}) fusion(f32[1024]{0:T(1024)S(1)} %get-tuple-element.48, f32[128]{0:T(128)S(1)} %broadcast_multiply_fusion.3, bf16[128,1024]{1,0:T(8,128)(2,1)S(1)} %copy-done, bf16[1024,8320]{1,0:T(8,128)(2,1)} %all-gather.3.cloned.1.call-done, ...), kind=kOutput, calls=%fused_computation.172 | convolution fusion | flops 808450944 | bytes 7871488 | tf_op jit(solution)/shard_map/dot_general | solution.py:235
  232.2 0.3 fusion.72
  232.6 1.0 fusion.109
  233.7 0.2 copy.84
  233.9 2.2 convolution_convert_fusion.3
  236.1 3.2 copy.85
  239.3 3.1 convolution_convert_fusion.2
  242.4 2.5 convolution_convert_fusion
  244.8 6.6 %fusion.3 = bf16[1024,8320]{1,0:T(8,128)(2,1)} fusion(bf16[1024,12]{1,0:T(8,128)(2,1)S(1)} %bitcast.69, bf16[1024,4096]{1,0:T(8,128)(2,1)S(1)} %convolution_convert_fusion, bf16[1024,1024]{1,0:T(8,128)(2,1)S(1)} %copy.85, bf16[1024,3072]{1,0:T(8,128)(2,1)S(1)} %convolution_convert_fusion.2), kind=kLoop, calls=%fused_computation.4 | loop fusion | flops 85196800 | bytes 33841152 | tf_op jit(solution)/shard_map/concatenate | solution.py:303
  251.5 51.2 %reduce-scatter.5.cloned.1.call-done = bf16[256,1024]{1,0:T(8,128)(2,1)} async-done(((bf16[4096,1024]{1,0:T(8,128)(2,1)}), bf16[256,1024]{1,0:T(8,128)(2,1)}) %reduce-scatter.5.cloned.1.call-update) | async-done | bytes 524304 | tf_op jit(solution)/shard_map/reduce_scatter | solution.py:313
  302.7 18.2 %shard_map.346 = bf16[8,32,1024]{2,1,0:T(8,128)(2,1)} custom-call(bf16[8,32,1024]{2,1,0:T(8,128)(2,1)} %bitcast.80), custom_call_target="tpu_custom_call" | custom-call | tf_op jit(solution)/shard_map/pallas_call | solution.py:111
  321.0 1.7 convert_multiply_fusion
  322.7 0.5 copy-done.11
  323.2 0.8 copy-done.12
  323.9 2.3 multiply_subtract_fusion
  326.2 0.4 copy-done.2
  326.7 7.2 %fusion.46 = bf16[128,1024]{1,0:T(8,128)(2,1)} fusion(f32[128,1024]{1,0:T(8,128)S(1)} %get-tuple-element.32, bf16[4096,1024]{1,0:T(8,128)(2,1)} %all-gather.5.cloned.1.call-done, f32[1024]{0:T(1024)S(1)} %get-tuple-element.42, f32[128,4096]{1,0:T(8,128)S(1)} %copy-done.2), kind=kOutput, calls=%fused_computation.60 | convolution fusion | flops 1078853632 | bytes 11276288 | tf_op jit(solution)/shard_map/dot_general | solution.py:205
  333.8 120.5 %reduce-scatter.3.cloned.1.call-done = bf16[64,8320]{1,0:T(8,128)(2,1)} async-done(((bf16[1024,8320]{1,0:T(8,128)(2,1)}), bf16[64,8320]{1,0:T(8,128)(2,1)}) %reduce-scatter.3.cloned.1.call-update) | async-done | bytes 1064976 | tf_op jit(solution)/shard_map/reduce_scatter | solution.py:312
  454.4 32.2 %shard_map.345 = bf16[8,8,8320]{2,1,0:T(8,128)(2,1)} custom-call(bf16[8,8,8320]{2,1,0:T(8,128)(2,1)} %bitcast.68), custom_call_target="tpu_custom_call" | custom-call | tf_op jit(solution)/shard_map/pallas_call | solution.py:111
  486.6 1.6 multiply_subtract_fusion.4
  488.2 2.0 multiply_subtract_fusion.3
  490.2 2.1 multiply_subtract_fusion.2
  492.4 0.8 copy-done.14
  493.2 2.6 multiply_subtract_fusion.1
  (98 shorter events, 0.9 us)
Async XLA Ops:
  7.2 3.1 copy-start.8
  7.2 117.4 %all-gather.3.cloned.1.call-start = ((), (), s32[]{:S(2)}) async-start(), calls=%async_computation.2 | async-start | bytes 18104320 | tf_op jit(solution)/shard_map/all_gather | solution.py:289
  10.3 1.6 copy-start.6
  11.4 113.2 %copy-start = (bf16[128,1024]{1,0:T(8,128)(2,1)S(1)}, bf16[128,1024]{1,0:T(8,128)(2,1)}, u32[]{:S(2)}) copy-start(bf16[128,1024]{1,0:T(8,128)(2,1)} %param.18) | copy-start | bytes 786436
  11.4 113.6 %copy-start.33 = (s32[1,128]{1,0:T(1,128)S(1)}, s32[1,128]{1,0:T(1,128)}, u32[]{:S(2)}) copy-start(s32[1,128]{1,0:T(1,128)} %param.20) | copy-start | bytes 1540
  11.5 186.9 %all-gather.5.cloned.1.call-start = ((), (), s32[]{:S(2)}) async-start(), calls=%async_computation.3 | async-start | bytes 8912896 | tf_op jit(solution)/shard_map/all_gather | solution.py:291
  124.6 178.1 %reduce-scatter.5.cloned.1.call-start = ((), (), s32[]{:S(2)}) async-start(), calls=%async_computation.5 | async-start | bytes 8912896 | tf_op jit(solution)/shard_map/reduce_scatter | solution.py:313
  133.0 1.1 copy-start.18
  133.2 0.9 copy-start.20
  133.6 3.1 copy-start.17
  134.0 2.6 copy-start.23
  136.7 4.8 copy-start.4
  141.5 56.8 %copy-start.1 = (f32[128,4096]{1,0:T(8,128)}, f32[128,4096]{1,0:T(8,128)S(1)}, u32[]{:S(2)}) copy-start(f32[128,4096]{1,0:T(8,128)S(1)} %fusion.12) | copy-start | bytes 6291460
  147.2 307.2 %reduce-scatter.3.cloned.1.call-start = ((), (), s32[]{:S(2)}) async-start(), calls=%async_computation.4 | async-start | bytes 18104320 | tf_op jit(solution)/shard_map/reduce_scatter | solution.py:312
  217.1 3.4 copy-start.21
  217.1 4.7 copy-start.19
  217.3 3.1 copy-start.22
  221.8 5.1 %copy-start.29 = (bf16[1,128,16,64]{1,3,2,0:T(8,128)(2,1)S(1)}, bf16[1,128,16,64]{1,3,2,0:T(8,128)(2,1)}, u32[]{:S(2)}) copy-start(bf16[1,128,16,64]{1,3,2,0:T(8,128)(2,1)} %get-tuple-element.80) | copy-start | bytes 786436
  226.9 5.3 %copy-start.31 = (bf16[16,64,128]{2,1,0:T(8,128)(2,1)}, bf16[16,64,128]{2,1,0:T(8,128)(2,1)S(1)}, u32[]{:S(2)}) copy-start(bf16[16,64,128]{2,1,0:T(8,128)(2,1)S(1)} %convolution_convert_fusion.4) | copy-start | bytes 786436
  232.2 1.7 copy-start.24
  236.1 3.2 copy-start.30
  239.3 3.1 copy-start.15
  320.9 1.7 copy-start.7
  320.9 2.2 copy-start.11
  321.0 3.0 copy-start.12
  322.7 3.6 copy-start.5
  323.9 2.7 copy-start.2
  326.6 159.9 %copy-start.32 = (f32[12,64]{1,0:T(8,128)S(1)}, f32[12,64]{1,0:T(8,128)}, u32[]{:S(2)}) copy-start(f32[12,64]{1,0:T(8,128)} %param.25) | copy-start | bytes 9220
  326.7 159.9 %copy-start.34 = (f32[12,64]{1,0:T(8,128)S(1)}, f32[12,64]{1,0:T(8,128)}, u32[]{:S(2)}) copy-start(f32[12,64]{1,0:T(8,128)} %param.30) | copy-start | bytes 9220
  326.7 159.9 %copy-start.35 = (f32[12,64]{1,0:T(8,128)S(1)}, f32[12,64]{1,0:T(8,128)}, u32[]{:S(2)}) copy-start(f32[12,64]{1,0:T(8,128)} %param.35) | copy-start | bytes 9220
  326.7 161.5 %copy-start.27 = (f32[64,1024]{1,0:T(8,128)S(1)}, f32[64,1024]{1,0:T(8,128)}, u32[]{:S(2)}) copy-start(f32[64,1024]{1,0:T(8,128)} %param.27) | copy-start | bytes 786436
  326.7 161.5 %copy-start.28 = (f32[64,1024]{1,0:T(8,128)S(1)}, f32[64,1024]{1,0:T(8,128)}, u32[]{:S(2)}) copy-start(f32[64,1024]{1,0:T(8,128)} %param.32) | copy-start | bytes 786436
  333.8 154.3 %copy-start.16 = (f32[64,1024]{1,0:T(8,128)S(1)}, f32[64,1024]{1,0:T(8,128)}, u32[]{:S(2)}) copy-start(f32[64,1024]{1,0:T(8,128)} %param.22) | copy-start | bytes 786436
  333.8 156.4 %copy-start.10 = (f32[64,3072]{1,0:T(8,128)S(1)}, f32[64,3072]{1,0:T(8,128)}, u32[]{:S(2)}) copy-start(f32[64,3072]{1,0:T(8,128)} %param.21) | copy-start | bytes 2359300
  333.8 156.4 %copy-start.25 = (f32[64,3072]{1,0:T(8,128)S(1)}, f32[64,3072]{1,0:T(8,128)}, u32[]{:S(2)}) copy-start(f32[64,3072]{1,0:T(8,128)} %param.26) | copy-start | bytes 2359300
  333.8 156.4 %copy-start.26 = (f32[64,3072]{1,0:T(8,128)S(1)}, f32[64,3072]{1,0:T(8,128)}, u32[]{:S(2)}) copy-start(f32[64,3072]{1,0:T(8,128)} %param.31) | copy-start | bytes 2359300
  486.5 3.7 copy-start.3
  490.2 2.2 copy-start.9
  490.2 2.2 copy-start.13
  490.2 3.0 copy-start.14
Sparse Core Ops, SparseCore 0:
  11.6 112.9 all-gather.2
  127.6 70.6 all-gather.4
  202.6 100.0 reduce-scatter.4
  306.9 147.3 reduce-scatter.2

commit v7 on v5

--- a/solution.py
+++ b/solution.py
@@ -108,6 +108,55 @@
         compiler_params=pltpu.CompilerParams(collective_id=slot, has_side_effects=True),
     )(*stacked)
     return [r.reshape(a.shape) for r, a in zip(results, arrays)]
+
+
+def zero_gather_kernel(parts, x_ref, out_ref, own_sem, send_sem, got_sem):
+    me = lax.axis_index("zero")
+    row = lax.axis_index("dp")
+    barrier = pltpu.get_barrier_semaphore()
+    for k in range(1, parts):
+        pl.semaphore_signal(
+            barrier, inc=1, device_id=(row, lax.rem(me + k, parts)),
+            device_id_type=pl.DeviceIdType.MESH,
+        )
+    pl.semaphore_wait(barrier, parts - 1)
+    own = pltpu.make_async_copy(x_ref, out_ref.at[me], own_sem)
+    own.start()
+    copies = []
+    for k in range(1, parts):
+        copy = pltpu.make_async_remote_copy(
+            src_ref=x_ref,
+            dst_ref=out_ref.at[me],
+            send_sem=send_sem.at[k],
+            recv_sem=got_sem.at[k],
+            device_id=(row, lax.rem(me + k, parts)),
+            device_id_type=pl.DeviceIdType.MESH,
+        )
+        copy.start()
+        copies.append(copy)
+    own.wait()
+    for copy in copies:
+        copy.wait_recv()
+    for copy in copies:
+        copy.wait_send()
+
+
+def gathered_over_zero(shard):
+    parts = lax.axis_size("zero")
+    anywhere = pl.BlockSpec(memory_space=pl.ANY)
+    whole = pl.pallas_call(
+        partial(zero_gather_kernel, parts),
+        out_shape=jax.ShapeDtypeStruct((parts,) + shard.shape, shard.dtype),
+        in_specs=[anywhere],
+        out_specs=anywhere,
+        scratch_shapes=[
+            pltpu.SemaphoreType.DMA(()),
+            pltpu.SemaphoreType.DMA((parts,)),
+            pltpu.SemaphoreType.DMA((parts,)),
+        ],
+        compiler_params=pltpu.CompilerParams(collective_id=2, has_side_effects=True),
+    )(shard)
+    return whole.reshape((parts * shard.shape[0],) + shard.shape[1:])
 
 
 def gelu_tanh(inputs):
@@ -276,8 +325,8 @@
     vec_cols = jnp.pad(vectors.astype(jnp.bfloat16).T, ((0, 0), (0, LANE - vectors.shape[0])))
     first_mats = (w_qkv.astype(jnp.bfloat16), w_out.astype(jnp.bfloat16), w_fc.astype(jnp.bfloat16), vec_cols)
     first_all = lax.all_gather(jnp.concatenate(first_mats, axis=1), "zero", axis=0, tiled=True)
-    first_all, proj_shard = lax.optimization_barrier((first_all, w_proj.astype(jnp.bfloat16)))
-    proj_mat = lax.all_gather(proj_shard, "zero", axis=0, tiled=True)
+    proj_mat = gathered_over_zero(w_proj.astype(jnp.bfloat16))
+    first_all, proj_mat = lax.optimization_barrier((first_all, proj_mat))
     widths = [m.shape[1] for m in first_mats]
     qkv_mat, out_mat, fc_mat, vec_cols_all = jnp.split(
         first_all, [sum(widths[:k]) for k in range(1, len(widths))], axis=1

time: 506 us -> 531 us (1.049)
  Pallas kernels: 50.4 us -> 166 us
  waiting for transfers between devices: 331 us -> 240 us
    pallas_call x0 -> x1, Pallas kernels: none -> 115 us  [gathered_over_zero(): pl.pallas_call(partial(zero_gather_kernel, parts), out_shape=jax.ShapeDty...]
    all_gather x1 -> x0, waiting for transfers between devices: 47.6 us -> none  [local(): proj_mat = lax.all_gather(proj_shard, 'zero', axis=0, tiled=True)]
    all_gather x1, waiting for transfers between devices: 112 us -> 77.4 us  [local(): lax.all_gather(jnp.concatenate(first_mats, axis=1), 'zero', axis=0, tiled...]
    reduce_scatter x1, waiting for transfers between devices: 51.2 us -> 34.6 us  [local(): lax.psum_scatter(local_grads[3].astype(jnp.bfloat16), 'zero', scatter_dim...]
    reduce_scatter x1, waiting for transfers between devices: 121 us -> 128 us  [local(): lax.psum_scatter(joined, 'zero', scatter_dimension=0, tiled=True)]
  transfers between devices with their start and end apart: 4 -> 3, of which waited for: 4 -> 3; matrix products, arithmetic and copies ran while one was open for 18% -> 13% of each run, Pallas kernels for 4% -> 25%
where the time goes in v7:
time: 531 us; the launch traced here: 528 us
  waiting for transfers between devices  240 us (45%)
  Pallas kernels  166 us (31%)
  matrix products  67 us (13%)
  other arithmetic  27.6 us (5%)
  between operations  14.4 us (3%)
  local copies, waits for them, and re-layouts  12.4 us (2%)
    reduce_scatter x1, waiting for transfers between devices, local(): lax.psum_scatter(joined, 'zero', scatter_dimension=0, tiled=True)  128 us
    pallas_call x1, Pallas kernels, gathered_over_zero(): pl.pallas_call(partial(zero_gather_kernel, parts), out_shape=jax.ShapeDty...  115 us
    all_gather x1, waiting for transfers between devices, local(): lax.all_gather(jnp.concatenate(first_mats, axis=1), 'zero', axis=0, tiled...  77.4 us
    pallas_call x2, Pallas kernels, summed_over_dp(): pl.pallas_call(partial(dp_sum_kernel, parts, count), out_shape=[jax.Shape...  50.5 us
    reduce_scatter x1, waiting for transfers between devices, local(): lax.psum_scatter(local_grads[3].astype(jnp.bfloat16), 'zero', scatter_dim...  34.6 us
  transfers between devices with their start and end apart: 3, of which 3 were waited for; matrix products, arithmetic and copies ran while one was open for 13% of the time, Pallas kernels for 25%

profile of v7, /device:TPU:4, one launch (start us, length us, event | category | flops | bytes accessed | tf_op | source)
XLA Modules:
  0.0 527.5 jit_solution(10441487572512376575)
XLA Ops:
  7.2 0.8 convert_bitcast_fusion.1
  8.0 0.1 copy.90
  8.1 1.0 convert_element_type.110
  9.1 1.2 convert_element_type.109
  10.4 1.1 fusion.50
  11.6 0.3 copy-done.6
  11.9 0.9 convert_element_type.113.x_ref
  12.8 115.2 %shard_map.345 = bf16[16,256,1024]{2,1,0:T(8,128)(2,1)} custom-call(bf16[256,1024]{1,0:T(8,128)(2,1)} %convert_element_type.113.x_ref), custom_call_target="tpu_custom_call" | custom-call | tf_op jit(solution)/shard_map/pallas_call | solution.py:147
  128.0 0.1 convert_reduce_fusion
  128.1 0.2 fusion.73
  128.4 77.4 %all-gather.2.cloned.1.call-done = bf16[1024,8320]{1,0:T(8,128)(2,1)} async-done(((bf16[64,8320]{1,0:T(8,128)(2,1)}), bf16[1024,8320]{1,0:T(8,128)(2,1)}) %all-gather.2.cloned.1.call-update) | async-done | bytes 17039376 | tf_op jit(solution)/shard_map/all_gather | solution.py:327
  205.8 1.0 convert_bitcast_fusion
  206.8 2.1 slice_reduce_fusion.2
  208.9 0.2 slice.71
  209.1 0.2 copy.79
  209.3 3.9 fusion.10
  213.3 0.1 fusion.75
  213.4 0.2 copy.76
  213.6 0.2 copy.77
  213.7 0.2 copy.75
  213.9 0.4 convolution_multiply_fusion
  214.3 0.5 convolution_convert_fusion.5
  214.8 2.2 fusion.125
  217.1 0.2 multiply_reduce_fusion.4
  217.3 4.8 fusion.12
  222.1 5.6 %convolution_convert_fusion.1 = bf16[4096,1024]{1,0:T(8,128)(2,1)} fusion(bf16[128,1024]{1,0:T(8,128)(2,1)S(1)} %copy-done.4, f32[128,4096]{1,0:T(8,128)S(1)} %fusion.12), kind=kOutput, calls=%fused_computation.6 | convolution fusion | flops 1082654720 | bytes 10747904 | tf_op jit(solution)/shard_map/dot_general | solution.py:246
  227.7 0.2 reduce-scatter.3.cloned.1.call-start
  228.0 8.5 %fusion.120 = (bf16[4096]{0:T(1024)(128)(2,1)S(1)}, bf16[128,4096]{1,0:T(8,128)(2,1)}) fusion(f32[128,4096]{1,0:T(8,128)S(1)} %fusion.12, bf16[128,1024]{1,0:T(8,128)(2,1)S(1)} %copy-done.4, bf16[4096,1024]{1,0:T(8,128)(2,1)} %bitcast.64), kind=kOutput, calls=%fused_computation.173 | convolution fusion | flops 1086844928 | bytes 11804672 | tf_op jit(solution)/shard_map/dot_general | solution.py:250
  236.5 0.1 reduce_sum.191
  236.7 0.2 multiply_reduce_fusion.3
  236.9 7.6 %multiply_reduce_fusion.1 = (bf16[1024]{0:T(1024)(128)(2,1)S(1)}, f32[128]{0:T(128)S(1)}, bf16[1024]{0:T(1024)(128)(2,1)S(1)}, f32[128,1024]{1,0:T(8,128)S(1)}) fusion(f32[128,1024]{1,0:T(8,128)S(1)} %get-tuple-element.32, f32[128]{0:T(128)S(1)} %fusion.101, f32[128]{0:T(128)S(1)} %broadcast_multiply_fusion.1, f32[1024]{0:T(1024)S(1)} %get-tuple-element.41, ...), kind=kOutput, calls=%fused_computation.114 | convolution fusion | flops 1074788224 | bytes 10495488 | tf_op jit(solution)/shard_map/dot_general | solution.py:255
  244.6 0.3 fusion.122
  244.9 3.5 fusion.47
  248.3 1.2 copy.80
  249.5 0.7 copy-done.23
  250.2 1.2 fusion.123
  251.5 2.3 fusion.128
  253.8 1.3 fusion.37
  255.1 2.7 fusion.124
  257.9 2.7 convolution_convert_fusion.4
  260.7 5.9 %fusion.112 = (bf16[1024]{0:T(1024)(128)(2,1)S(1)}, f32[128]{0:T(128)S(1)}, f32[128,1024]{1,0:T(8,128)S(1)}) fusion(f32[1024]{0:T(1024)S(1)} %get-tuple-element.48, f32[128]{0:T(128)S(1)} %broadcast_multiply_fusion.3, bf16[128,1024]{1,0:T(8,128)(2,1)S(1)} %copy-done, bf16[1024,8320]{1,0:T(8,128)(2,1)} %all-gather.2.cloned.1.call-done, ...), kind=kOutput, calls=%fused_computation.172 | convolution fusion | flops 808450944 | bytes 7871488 | tf_op jit(solution)/shard_map/dot_general | solution.py:273
  266.6 0.3 fusion.72
  267.0 1.0 fusion.109
  268.1 0.2 copy.84
  268.3 2.2 convolution_convert_fusion.3
  270.5 2.9 copy.85
  273.4 3.1 convolution_convert_fusion.2
  276.5 2.5 convolution_convert_fusion
  279.0 6.7 %fusion.3 = bf16[1024,8320]{1,0:T(8,128)(2,1)} fusion(bf16[1024,12]{1,0:T(8,128)(2,1)S(1)} %bitcast.72, bf16[1024,4096]{1,0:T(8,128)(2,1)S(1)} %convolution_convert_fusion, bf16[1024,1024]{1,0:T(8,128)(2,1)S(1)} %copy.85, bf16[1024,3072]{1,0:T(8,128)(2,1)S(1)} %convolution_convert_fusion.2), kind=kLoop, calls=%fused_computation.4 | loop fusion | flops 85196800 | bytes 33841152 | tf_op jit(solution)/shard_map/concatenate | solution.py:341
  285.7 1.6 copy-done.2
  287.3 5.9 %fusion.46 = bf16[128,1024]{1,0:T(8,128)(2,1)} fusion(f32[128,1024]{1,0:T(8,128)S(1)} %get-tuple-element.32, bf16[4096,1024]{1,0:T(8,128)(2,1)} %bitcast.65, f32[1024]{0:T(1024)S(1)} %get-tuple-element.42, f32[128,4096]{1,0:T(8,128)S(1)} %copy-done.2), kind=kOutput, calls=%fused_computation.60 | convolution fusion | flops 1078853632 | bytes 11276288 | tf_op jit(solution)/shard_map/dot_general | solution.py:243
  293.2 34.6 %reduce-scatter.5.cloned.1.call-done = bf16[256,1024]{1,0:T(8,128)(2,1)} async-done(((bf16[4096,1024]{1,0:T(8,128)(2,1)}), bf16[256,1024]{1,0:T(8,128)(2,1)}) %reduce-scatter.5.cloned.1.call-update) | async-done | bytes 524304 | tf_op jit(solution)/shard_map/reduce_scatter | solution.py:351
  327.8 18.3 %shard_map.347 = bf16[8,32,1024]{2,1,0:T(8,128)(2,1)} custom-call(bf16[8,32,1024]{2,1,0:T(8,128)(2,1)} %bitcast.83), custom_call_target="tpu_custom_call" | custom-call | tf_op jit(solution)/shard_map/pallas_call | solution.py:100
  346.1 1.7 convert_multiply_fusion
  347.9 0.4 copy-done.11
  348.3 0.6 copy-done.12
  348.9 2.3 multiply_subtract_fusion
  351.3 128.2 %reduce-scatter.3.cloned.1.call-done = bf16[64,8320]{1,0:T(8,128)(2,1)} async-done(((bf16[1024,8320]{1,0:T(8,128)(2,1)}), bf16[64,8320]{1,0:T(8,128)(2,1)}) %reduce-scatter.3.cloned.1.call-update) | async-done | bytes 1064976 | tf_op jit(solution)/shard_map/reduce_scatter | solution.py:350
  479.4 32.2 %shard_map.346 = bf16[8,8,8320]{2,1,0:T(8,128)(2,1)} custom-call(bf16[8,8,8320]{2,1,0:T(8,128)(2,1)} %bitcast.71), custom_call_target="tpu_custom_call" | custom-call | tf_op jit(solution)/shard_map/pallas_call | solution.py:100
  511.7 1.6 multiply_subtract_fusion.4
  513.3 2.0 multiply_subtract_fusion.3
  515.4 2.1 multiply_subtract_fusion.2
  517.5 0.8 copy-done.14
  518.3 2.6 multiply_subtract_fusion.1
  (100 shorter events, 0.9 us)
Async XLA Ops:
  7.2 3.1 copy-start.8
  7.2 198.6 %all-gather.2.cloned.1.call-start = ((), (), s32[]{:S(2)}) async-start(), calls=%async_computation.2 | async-start | bytes 18104320 | tf_op jit(solution)/shard_map/all_gather | solution.py:327
  10.3 1.6 copy-start.6
  11.5 316.3 %reduce-scatter.5.cloned.1.call-start = ((), (), s32[]{:S(2)}) async-start(), calls=%async_computation.4 | async-start | bytes 8912896 | tf_op jit(solution)/shard_map/reduce_scatter | solution.py:351
  12.8 115.2 %copy-start = (bf16[128,1024]{1,0:T(8,128)(2,1)S(1)}, bf16[128,1024]{1,0:T(8,128)(2,1)}, u32[]{:S(2)}) copy-start(bf16[128,1024]{1,0:T(8,128)(2,1)} %param.18) | copy-start | bytes 786436
  12.8 115.6 %copy-start.35 = (s32[1,128]{1,0:T(1,128)S(1)}, s32[1,128]{1,0:T(1,128)}, u32[]{:S(2)}) copy-start(s32[1,128]{1,0:T(1,128)} %param.20) | copy-start | bytes 1540
  213.7 1.1 copy-start.19
  213.9 0.9 copy-start.21
  214.3 2.7 copy-start.17
  214.8 2.5 copy-start.24
  217.3 4.8 copy-start.4
  222.1 6.0 %copy-start.1 = (f32[128,4096]{1,0:T(8,128)}, f32[128,4096]{1,0:T(8,128)S(1)}, u32[]{:S(2)}) copy-start(f32[128,4096]{1,0:T(8,128)S(1)} %fusion.12) | copy-start | bytes 6291460
  227.7 251.7 %reduce-scatter.3.cloned.1.call-start = ((), (), s32[]{:S(2)}) async-start(), calls=%async_computation.3 | async-start | bytes 18104320 | tf_op jit(solution)/shard_map/reduce_scatter | solution.py:350
  244.8 5.4 %copy-start.18 = (f32[16,128,128]{1,2,0:T(8,128)S(1)}, f32[16,128,128]{1,2,0:T(8,128)}, u32[]{:S(2)}) copy-start(f32[16,128,128]{1,2,0:T(8,128)} %copy-done.17) | copy-start | bytes 3145732
  248.3 3.2 copy-start.22
  249.5 0.7 copy-start.23
  251.4 3.7 copy-start.20
  253.8 6.9 %copy-start.30 = (bf16[1,128,16,64]{1,3,2,0:T(8,128)(2,1)S(1)}, bf16[1,128,16,64]{1,3,2,0:T(8,128)(2,1)}, u32[]{:S(2)}) copy-start(bf16[1,128,16,64]{1,3,2,0:T(8,128)(2,1)} %get-tuple-element.80) | copy-start | bytes 786436
  257.8 2.9 copy-start.32
  260.7 5.9 %copy-start.33 = (bf16[16,64,128]{2,1,0:T(8,128)(2,1)}, bf16[16,64,128]{2,1,0:T(8,128)(2,1)S(1)}, u32[]{:S(2)}) copy-start(bf16[16,64,128]{2,1,0:T(8,128)(2,1)S(1)} %convolution_convert_fusion.4) | copy-start | bytes 786436
  266.6 1.7 copy-start.25
  270.5 2.9 copy-start.31
  273.4 3.1 copy-start.15
  285.7 1.6 copy-start.2
  346.1 1.8 copy-start.7
  346.1 2.2 copy-start.11
  346.1 2.8 copy-start.12
  347.9 3.3 copy-start.5
  348.9 164.4 %copy-start.29 = (f32[64,1024]{1,0:T(8,128)S(1)}, f32[64,1024]{1,0:T(8,128)}, u32[]{:S(2)}) copy-start(f32[64,1024]{1,0:T(8,128)} %param.32) | copy-start | bytes 786436
  351.2 160.5 %copy-start.34 = (f32[12,64]{1,0:T(8,128)S(1)}, f32[12,64]{1,0:T(8,128)}, u32[]{:S(2)}) copy-start(f32[12,64]{1,0:T(8,128)} %param.25) | copy-start | bytes 9220
  351.2 160.5 %copy-start.36 = (f32[12,64]{1,0:T(8,128)S(1)}, f32[12,64]{1,0:T(8,128)}, u32[]{:S(2)}) copy-start(f32[12,64]{1,0:T(8,128)} %param.30) | copy-start | bytes 9220
  351.2 160.5 %copy-start.37 = (f32[12,64]{1,0:T(8,128)S(1)}, f32[12,64]{1,0:T(8,128)}, u32[]{:S(2)}) copy-start(f32[12,64]{1,0:T(8,128)} %param.35) | copy-start | bytes 9220
  351.2 162.1 %copy-start.16 = (f32[64,1024]{1,0:T(8,128)S(1)}, f32[64,1024]{1,0:T(8,128)}, u32[]{:S(2)}) copy-start(f32[64,1024]{1,0:T(8,128)} %param.22) | copy-start | bytes 786436
  351.2 162.1 %copy-start.28 = (f32[64,1024]{1,0:T(8,128)S(1)}, f32[64,1024]{1,0:T(8,128)}, u32[]{:S(2)}) copy-start(f32[64,1024]{1,0:T(8,128)} %param.27) | copy-start | bytes 786436
  351.2 164.1 %copy-start.10 = (f32[64,3072]{1,0:T(8,128)S(1)}, f32[64,3072]{1,0:T(8,128)}, u32[]{:S(2)}) copy-start(f32[64,3072]{1,0:T(8,128)} %param.21) | copy-start | bytes 2359300
  351.2 164.1 %copy-start.26 = (f32[64,3072]{1,0:T(8,128)S(1)}, f32[64,3072]{1,0:T(8,128)}, u32[]{:S(2)}) copy-start(f32[64,3072]{1,0:T(8,128)} %param.26) | copy-start | bytes 2359300
  479.4 35.9 %copy-start.27 = (f32[64,3072]{1,0:T(8,128)S(1)}, f32[64,3072]{1,0:T(8,128)}, u32[]{:S(2)}) copy-start(f32[64,3072]{1,0:T(8,128)} %param.31) | copy-start | bytes 2359300
  511.7 3.7 copy-start.3
  515.3 2.2 copy-start.9
  515.3 2.2 copy-start.13
  515.4 3.0 copy-start.14
Sparse Core Ops, SparseCore 0:
  11.7 194.1 all-gather.1
  227.8 99.9 reduce-scatter.4
  332.2 147.2 reduce-scatter.2

commit v8 on v6

--- a/solution.py
+++ b/solution.py
@@ -11,6 +11,7 @@
 SEQ = 128
 ADAM_STEP = 3
 LANE = 128
+CHUNKS = 2
 
 
 eps_norm = 1e-05
@@ -40,7 +41,7 @@
     )
 
 
-def dp_sum_kernel(parts, count, *refs):
+def dp_sum_kernel(parts, count, chunks, *refs):
     x_refs, out_refs = refs[:count], refs[count : 2 * count]
     recv_one = refs[2 * count : 3 * count]
     mine = refs[3 * count : 4 * count]
@@ -55,47 +56,52 @@
         )
     pl.semaphore_wait(barrier, parts - 1)
 
-    def send(sources, targets, sends, gots, pick):
-        copies = []
+    def columns(i, c):
+        width = x_refs[i].shape[-1]
+        cut = (width // LANE // chunks) * LANE
+        start = c * cut
+        return pl.ds(start, width - start if c == chunks - 1 else cut)
+
+    def remote(src, dst, sends, gots, i, c, k):
+        copy = pltpu.make_async_remote_copy(
+            src_ref=src,
+            dst_ref=dst,
+            send_sem=sends.at[i, c, k],
+            recv_sem=gots.at[i, c, k],
+            device_id=(lax.rem(me + k, parts), shard),
+            device_id_type=pl.DeviceIdType.MESH,
+        )
+        copy.start()
+        return copy
+
+    first = {}
+    for c in range(chunks):
         for k in range(1, parts):
             peer = lax.rem(me + k, parts)
             for i in range(count):
-                copy = pltpu.make_async_remote_copy(
-                    src_ref=pick(sources[i], peer),
-                    dst_ref=targets[i].at[k],
-                    send_sem=sends.at[i, k],
-                    recv_sem=gots.at[i, k],
-                    device_id=(peer, shard),
-                    device_id_type=pl.DeviceIdType.MESH,
+                cols = columns(i, c)
+                first[i, c, k] = remote(
+                    x_refs[i].at[peer, :, cols], recv_one[i].at[k, :, cols],
+                    send_one, got_one, i, c, k,
                 )
-                copy.start()
-                copies.append(copy)
-        return copies
-
-    first = send(x_refs, recv_one, send_one, got_one, lambda ref, peer: ref.at[peer])
-    totals = [x_refs[i][me].astype(jnp.float32) for i in range(count)]
-    for n, copy in enumerate(first):
-        copy.wait_recv()
-        k, i = n // count + 1, n % count
-        totals[i] = totals[i] + recv_one[i][k].astype(jnp.float32)
-    for i in range(count):
-        mine[i][...] = totals[i].astype(mine[i].dtype)
-        out_refs[i][me] = mine[i][...]
     second = []
-    for k in range(1, parts):
-        peer = lax.rem(me + k, parts)
+    for c in range(chunks):
         for i in range(count):
-            copy = pltpu.make_async_remote_copy(
-                src_ref=mine[i],
-                dst_ref=out_refs[i].at[me],
-                send_sem=send_two.at[i, k],
-                recv_sem=got_two.at[i, k],
-                device_id=(peer, shard),
-                device_id_type=pl.DeviceIdType.MESH,
-            )
-            copy.start()
-            second.append(copy)
-    for copy in first:
+            cols = columns(i, c)
+            total = x_refs[i][me, :, cols].astype(jnp.float32)
+            for k in range(1, parts):
+                first[i, c, k].wait_recv()
+                total = total + recv_one[i][k, :, cols].astype(jnp.float32)
+            mine[i][:, cols] = total.astype(mine[i].dtype)
+            out_refs[i][me, :, cols] = mine[i][:, cols]
+            for k in range(1, parts):
+                second.append(
+                    remote(
+                        mine[i].at[:, cols], out_refs[i].at[me, :, cols],
+                        send_two, got_two, i, c, k,
+                    )
+                )
+    for copy in first.values():
         copy.wait_send()
     for copy in second:
         copy.wait_recv()
@@ -109,13 +115,13 @@
     stacked = [a.reshape((parts, a.shape[0] // parts) + a.shape[1:]) for a in arrays]
     vmem = pl.BlockSpec(memory_space=pltpu.VMEM)
     results = pl.pallas_call(
-        partial(dp_sum_kernel, parts, count),
+        partial(dp_sum_kernel, parts, count, CHUNKS),
         out_shape=[jax.ShapeDtypeStruct(s.shape, s.dtype) for s in stacked],
         in_specs=[vmem] * count,
         out_specs=[vmem] * count,
         scratch_shapes=[pltpu.VMEM(s.shape, s.dtype) for s in stacked]
         + [pltpu.VMEM(s.shape[1:], s.dtype) for s in stacked]
-        + [pltpu.SemaphoreType.DMA((count, parts))] * 4,
+        + [pltpu.SemaphoreType.DMA((count, CHUNKS, parts))] * 4,
         compiler_params=pltpu.CompilerParams(collective_id=slot, has_side_effects=True),
     )(*stacked)
     return [r.reshape(a.shape) for r, a in zip(results, arrays)]

time: 506 us -> 501 us (level)
  no operation moved by 1% of the time
where the time goes in v8:
time: 501 us; the launch traced here: 500 us
  waiting for transfers between devices  330 us (66%)
  matrix products  67 us (13%)
  Pallas kernels  48.8 us (10%)
  other arithmetic  29.1 us (6%)
  between operations  14.4 us (3%)
  local copies, waits for them, and re-layouts  10 us (2%)
    reduce_scatter x1, waiting for transfers between devices, local(): lax.psum_scatter(joined, 'zero', scatter_dimension=0, tiled=True)  120 us
    all_gather x1, waiting for transfers between devices, local(): lax.all_gather(jnp.concatenate(first_mats, axis=1), 'zero', axis=0, tiled...  112 us
    reduce_scatter x1, waiting for transfers between devices, local(): lax.psum_scatter(local_grads[3].astype(jnp.bfloat16), 'zero', scatter_dim...  51.2 us
    pallas_call x2, Pallas kernels, summed_over_dp(): pl.pallas_call(partial(dp_sum_kernel, parts, count, CHUNKS), out_shape=[j...  48.8 us
    all_gather x1, waiting for transfers between devices, local(): proj_mat = lax.all_gather(proj_shard, 'zero', axis=0, tiled=True)  47.6 us
  transfers between devices with their start and end apart: 4, of which 4 were waited for; matrix products, arithmetic and copies ran while one was open for 18% of the time, Pallas kernels for 4%

profile of v8, /device:TPU:4, one launch (start us, length us, event | category | flops | bytes accessed | tf_op | source)
XLA Modules:
  0.0 500.1 jit_solution(17102242668367388308)
XLA Ops:
  7.2 0.8 convert_bitcast_fusion.1
  8.0 0.1 copy.90
  8.1 1.0 convert_element_type.110
  9.1 1.2 convert_element_type.109
  10.4 1.1 fusion.50
  11.5 0.4 copy-done.6
  11.9 0.9 convert_element_type.113
  12.8 111.8 %all-gather.3.cloned.1.call-done = bf16[1024,8320]{1,0:T(8,128)(2,1)} async-done(((bf16[64,8320]{1,0:T(8,128)(2,1)}), bf16[1024,8320]{1,0:T(8,128)(2,1)}) %all-gather.3.cloned.1.call-update) | async-done | bytes 17039376 | tf_op jit(solution)/shard_map/all_gather | solution.py:295
  124.6 0.1 convert_reduce_fusion
  124.8 0.2 fusion.73
  125.0 0.1 fusion.90
  125.1 1.0 convert_bitcast_fusion
  126.1 0.2 slice.71
  126.3 0.2 copy.79
  126.5 2.1 slice_reduce_fusion.2
  128.6 3.9 fusion.10
  132.5 0.1 fusion.75
  132.6 0.2 copy.76
  132.8 0.2 copy.77
  133.0 0.2 copy.75
  133.2 0.4 convolution_multiply_fusion
  133.6 0.5 convolution_convert_fusion.5
  134.1 2.4 fusion.125
  136.5 0.2 multiply_reduce_fusion.4
  136.7 4.8 fusion.12
  141.5 5.6 %convolution_convert_fusion.1 = bf16[4096,1024]{1,0:T(8,128)(2,1)} fusion(bf16[128,1024]{1,0:T(8,128)(2,1)S(1)} %copy-done.4, f32[128,4096]{1,0:T(8,128)S(1)} %fusion.12), kind=kOutput, calls=%fused_computation.6 | convolution fusion | flops 1082654720 | bytes 10747904 | tf_op jit(solution)/shard_map/dot_general | solution.py:214
  147.2 0.2 reduce-scatter.3.cloned.1.call-start
  147.5 0.1 reduce_sum.191
  147.6 0.2 multiply_reduce_fusion.3
  147.8 3.0 fusion.37
  150.8 47.6 %all-gather.5.cloned.1.call-done = bf16[4096,1024]{1,0:T(8,128)(2,1)} async-done(((bf16[256,1024]{1,0:T(8,128)(2,1)}), bf16[4096,1024]{1,0:T(8,128)(2,1)}) %all-gather.5.cloned.1.call-update) | async-done | bytes 8388624 | tf_op jit(solution)/shard_map/all_gather | solution.py:297
  198.3 8.5 %fusion.120 = (bf16[4096]{0:T(1024)(128)(2,1)S(1)}, bf16[128,4096]{1,0:T(8,128)(2,1)}) fusion(f32[128,4096]{1,0:T(8,128)S(1)} %fusion.12, bf16[128,1024]{1,0:T(8,128)(2,1)S(1)} %copy-done.4, bf16[4096,1024]{1,0:T(8,128)(2,1)} %all-gather.5.cloned.1.call-done), kind=kOutput, calls=%fused_computation.173 | convolution fusion | flops 1086844928 | bytes 11804672 | tf_op jit(solution)/shard_map/dot_general | solution.py:218
  206.8 7.3 %multiply_reduce_fusion.1 = (bf16[1024]{0:T(1024)(128)(2,1)S(1)}, f32[128]{0:T(128)S(1)}, bf16[1024]{0:T(1024)(128)(2,1)S(1)}, f32[128,1024]{1,0:T(8,128)S(1)}) fusion(f32[128,1024]{1,0:T(8,128)S(1)} %get-tuple-element.32, f32[128]{0:T(128)S(1)} %fusion.101, f32[128]{0:T(128)S(1)} %broadcast_multiply_fusion.1, f32[1024]{0:T(1024)S(1)} %get-tuple-element.41, ...), kind=kOutput, calls=%fused_computation.114 | convolution fusion | flops 1074788224 | bytes 10495488 | tf_op jit(solution)/shard_map/dot_general | solution.py:223
  214.2 0.3 fusion.122
  214.4 2.6 fusion.47
  217.1 0.2 copy.80
  217.3 3.1 fusion.123
  220.5 1.3 fusion.128
  221.8 2.9 fusion.124
  224.8 2.1 convolution_convert_fusion.4
  226.9 5.2 %fusion.112 = (bf16[1024]{0:T(1024)(128)(2,1)S(1)}, f32[128]{0:T(128)S(1)}, f32[128,1024]{1,0:T(8,128)S(1)}) fusion(f32[1024]{0:T(1024)S(1)} %get-tuple-element.48, f32[128]{0:T(128)S(1)} %broadcast_multiply_fusion.3, bf16[128,1024]{1,0:T(8,128)(2,1)S(1)} %copy-done, bf16[1024,8320]{1,0:T(8,128)(2,1)} %all-gather.3.cloned.1.call-done, ...), kind=kOutput, calls=%fused_computation.172 | convolution fusion | flops 808450944 | bytes 7871488 | tf_op jit(solution)/shard_map/dot_general | solution.py:241
  232.2 0.3 fusion.72
  232.6 1.0 fusion.109
  233.7 0.2 copy.84
  233.9 2.2 convolution_convert_fusion.3
  236.1 3.2 copy.85
  239.3 3.1 convolution_convert_fusion.2
  242.4 2.5 convolution_convert_fusion
  244.8 6.6 %fusion.3 = bf16[1024,8320]{1,0:T(8,128)(2,1)} fusion(bf16[1024,12]{1,0:T(8,128)(2,1)S(1)} %bitcast.69, bf16[1024,4096]{1,0:T(8,128)(2,1)S(1)} %convolution_convert_fusion, bf16[1024,1024]{1,0:T(8,128)(2,1)S(1)} %copy.85, bf16[1024,3072]{1,0:T(8,128)(2,1)S(1)} %convolution_convert_fusion.2), kind=kLoop, calls=%fused_computation.4 | loop fusion | flops 85196800 | bytes 33841152 | tf_op jit(solution)/shard_map/concatenate | solution.py:309
  251.5 51.2 %reduce-scatter.5.cloned.1.call-done = bf16[256,1024]{1,0:T(8,128)(2,1)} async-done(((bf16[4096,1024]{1,0:T(8,128)(2,1)}), bf16[256,1024]{1,0:T(8,128)(2,1)}) %reduce-scatter.5.cloned.1.call-update) | async-done | bytes 524304 | tf_op jit(solution)/shard_map/reduce_scatter | solution.py:319
  302.7 18.9 %shard_map.346 = bf16[8,32,1024]{2,1,0:T(8,128)(2,1)} custom-call(bf16[8,32,1024]{2,1,0:T(8,128)(2,1)} %bitcast.80), custom_call_target="tpu_custom_call" | custom-call | tf_op jit(solution)/shard_map/pallas_call | solution.py:117
  321.7 1.7 convert_multiply_fusion
  323.4 0.5 copy-done.11
  323.9 0.7 copy-done.12
  324.6 2.3 multiply_subtract_fusion
  326.9 0.4 copy-done.2
  327.3 7.2 %fusion.46 = bf16[128,1024]{1,0:T(8,128)(2,1)} fusion(f32[128,1024]{1,0:T(8,128)S(1)} %get-tuple-element.32, bf16[4096,1024]{1,0:T(8,128)(2,1)} %all-gather.5.cloned.1.call-done, f32[1024]{0:T(1024)S(1)} %get-tuple-element.42, f32[128,4096]{1,0:T(8,128)S(1)} %copy-done.2), kind=kOutput, calls=%fused_computation.60 | convolution fusion | flops 1078853632 | bytes 11276288 | tf_op jit(solution)/shard_map/dot_general | solution.py:211
  334.5 119.8 %reduce-scatter.3.cloned.1.call-done = bf16[64,8320]{1,0:T(8,128)(2,1)} async-done(((bf16[1024,8320]{1,0:T(8,128)(2,1)}), bf16[64,8320]{1,0:T(8,128)(2,1)}) %reduce-scatter.3.cloned.1.call-update) | async-done | bytes 1064976 | tf_op jit(solution)/shard_map/reduce_scatter | solution.py:318
  454.4 29.9 %shard_map.345 = bf16[8,8,8320]{2,1,0:T(8,128)(2,1)} custom-call(bf16[8,8,8320]{2,1,0:T(8,128)(2,1)} %bitcast.68), custom_call_target="tpu_custom_call" | custom-call | tf_op jit(solution)/shard_map/pallas_call | solution.py:117
  484.3 1.6 multiply_subtract_fusion.4
  485.9 2.0 multiply_subtract_fusion.3
  488.0 2.1 multiply_subtract_fusion.2
  490.1 0.8 copy-done.14
  490.9 2.6 multiply_subtract_fusion.1
  (98 shorter events, 0.9 us)
Async XLA Ops:
  7.2 3.1 copy-start.8
  7.2 117.4 %all-gather.3.cloned.1.call-start = ((), (), s32[]{:S(2)}) async-start(), calls=%async_computation.2 | async-start | bytes 18104320 | tf_op jit(solution)/shard_map/all_gather | solution.py:295
  10.3 1.6 copy-start.6
  11.4 113.2 %copy-start = (bf16[128,1024]{1,0:T(8,128)(2,1)S(1)}, bf16[128,1024]{1,0:T(8,128)(2,1)}, u32[]{:S(2)}) copy-start(bf16[128,1024]{1,0:T(8,128)(2,1)} %param.18) | copy-start | bytes 786436
  11.4 113.6 %copy-start.33 = (s32[1,128]{1,0:T(1,128)S(1)}, s32[1,128]{1,0:T(1,128)}, u32[]{:S(2)}) copy-start(s32[1,128]{1,0:T(1,128)} %param.20) | copy-start | bytes 1540
  11.5 186.9 %all-gather.5.cloned.1.call-start = ((), (), s32[]{:S(2)}) async-start(), calls=%async_computation.3 | async-start | bytes 8912896 | tf_op jit(solution)/shard_map/all_gather | solution.py:297
  124.6 178.1 %reduce-scatter.5.cloned.1.call-start = ((), (), s32[]{:S(2)}) async-start(), calls=%async_computation.5 | async-start | bytes 8912896 | tf_op jit(solution)/shard_map/reduce_scatter | solution.py:319
  133.0 1.1 copy-start.18
  133.2 0.9 copy-start.20
  133.6 3.1 copy-start.17
  134.0 2.6 copy-start.23
  136.7 4.8 copy-start.4
  141.5 56.8 %copy-start.1 = (f32[128,4096]{1,0:T(8,128)}, f32[128,4096]{1,0:T(8,128)S(1)}, u32[]{:S(2)}) copy-start(f32[128,4096]{1,0:T(8,128)S(1)} %fusion.12) | copy-start | bytes 6291460
  147.2 307.2 %reduce-scatter.3.cloned.1.call-start = ((), (), s32[]{:S(2)}) async-start(), calls=%async_computation.4 | async-start | bytes 18104320 | tf_op jit(solution)/shard_map/reduce_scatter | solution.py:318
  217.1 3.4 copy-start.21
  217.1 4.7 copy-start.19
  217.3 3.1 copy-start.22
  221.8 5.1 %copy-start.29 = (bf16[1,128,16,64]{1,3,2,0:T(8,128)(2,1)S(1)}, bf16[1,128,16,64]{1,3,2,0:T(8,128)(2,1)}, u32[]{:S(2)}) copy-start(bf16[1,128,16,64]{1,3,2,0:T(8,128)(2,1)} %get-tuple-element.80) | copy-start | bytes 786436
  226.9 5.3 %copy-start.31 = (bf16[16,64,128]{2,1,0:T(8,128)(2,1)}, bf16[16,64,128]{2,1,0:T(8,128)(2,1)S(1)}, u32[]{:S(2)}) copy-start(bf16[16,64,128]{2,1,0:T(8,128)(2,1)S(1)} %convolution_convert_fusion.4) | copy-start | bytes 786436
  232.2 1.7 copy-start.24
  236.1 3.2 copy-start.30
  239.3 3.1 copy-start.15
  321.7 1.7 copy-start.7
  321.7 2.2 copy-start.11
  321.7 2.9 copy-start.12
  323.4 3.5 copy-start.5
  324.6 2.8 copy-start.2
  327.3 156.9 %copy-start.32 = (f32[12,64]{1,0:T(8,128)S(1)}, f32[12,64]{1,0:T(8,128)}, u32[]{:S(2)}) copy-start(f32[12,64]{1,0:T(8,128)} %param.25) | copy-start | bytes 9220
  327.3 156.9 %copy-start.34 = (f32[12,64]{1,0:T(8,128)S(1)}, f32[12,64]{1,0:T(8,128)}, u32[]{:S(2)}) copy-start(f32[12,64]{1,0:T(8,128)} %param.30) | copy-start | bytes 9220
  327.3 156.9 %copy-start.35 = (f32[12,64]{1,0:T(8,128)S(1)}, f32[12,64]{1,0:T(8,128)}, u32[]{:S(2)}) copy-start(f32[12,64]{1,0:T(8,128)} %param.35) | copy-start | bytes 9220
  327.3 158.5 %copy-start.27 = (f32[64,1024]{1,0:T(8,128)S(1)}, f32[64,1024]{1,0:T(8,128)}, u32[]{:S(2)}) copy-start(f32[64,1024]{1,0:T(8,128)} %param.27) | copy-start | bytes 786436
  327.3 158.5 %copy-start.28 = (f32[64,1024]{1,0:T(8,128)S(1)}, f32[64,1024]{1,0:T(8,128)}, u32[]{:S(2)}) copy-start(f32[64,1024]{1,0:T(8,128)} %param.32) | copy-start | bytes 786436
  334.5 151.4 %copy-start.16 = (f32[64,1024]{1,0:T(8,128)S(1)}, f32[64,1024]{1,0:T(8,128)}, u32[]{:S(2)}) copy-start(f32[64,1024]{1,0:T(8,128)} %param.22) | copy-start | bytes 786436
  334.5 153.4 %copy-start.10 = (f32[64,3072]{1,0:T(8,128)S(1)}, f32[64,3072]{1,0:T(8,128)}, u32[]{:S(2)}) copy-start(f32[64,3072]{1,0:T(8,128)} %param.21) | copy-start | bytes 2359300
  334.5 153.4 %copy-start.25 = (f32[64,3072]{1,0:T(8,128)S(1)}, f32[64,3072]{1,0:T(8,128)}, u32[]{:S(2)}) copy-start(f32[64,3072]{1,0:T(8,128)} %param.26) | copy-start | bytes 2359300
  334.5 153.4 %copy-start.26 = (f32[64,3072]{1,0:T(8,128)S(1)}, f32[64,3072]{1,0:T(8,128)}, u32[]{:S(2)}) copy-start(f32[64,3072]{1,0:T(8,128)} %param.31) | copy-start | bytes 2359300
  484.2 3.7 copy-start.3
  487.9 2.2 copy-start.9
  487.9 2.2 copy-start.13
  487.9 3.0 copy-start.14
Sparse Core Ops, SparseCore 0:
  11.6 112.9 all-gather.2
  127.6 70.6 all-gather.4
  202.6 100.0 reduce-scatter.4
  306.9 147.3 reduce-scatter.2

commit v9 on v8

--- a/solution.py
+++ b/solution.py
@@ -11,7 +11,7 @@
 SEQ = 128
 ADAM_STEP = 3
 LANE = 128
-CHUNKS = 2
+CHUNKS = 4
 
 
 eps_norm = 1e-05

time: 501 us -> 502 us (level)
  no operation moved by 1% of the time
where the time goes in v9:
time: 502 us; the launch traced here: 501 us
  waiting for transfers between devices  331 us (66%)
  matrix products  67 us (13%)
  Pallas kernels  48.8 us (10%)
  other arithmetic  29 us (6%)
  between operations  14.4 us (3%)
  local copies, waits for them, and re-layouts  9.97 us (2%)
    reduce_scatter x1, waiting for transfers between devices, local(): lax.psum_scatter(joined, 'zero', scatter_dimension=0, tiled=True)  120 us
    all_gather x1, waiting for transfers between devices, local(): lax.all_gather(jnp.concatenate(first_mats, axis=1), 'zero', axis=0, tiled...  112 us
    reduce_scatter x1, waiting for transfers between devices, local(): lax.psum_scatter(local_grads[3].astype(jnp.bfloat16), 'zero', scatter_dim...  51.2 us
    pallas_call x2, Pallas kernels, summed_over_dp(): pl.pallas_call(partial(dp_sum_kernel, parts, count, CHUNKS), out_shape=[j...  48.8 us
    all_gather x1, waiting for transfers between devices, local(): proj_mat = lax.all_gather(proj_shard, 'zero', axis=0, tiled=True)  47.6 us
  transfers between devices with their start and end apart: 4, of which 4 were waited for; matrix products, arithmetic and copies ran while one was open for 18% of the time, Pallas kernels for 4%

profile of v9, /device:TPU:4, one launch (start us, length us, event | category | flops | bytes accessed | tf_op | source)
XLA Modules:
  0.0 500.7 jit_solution(10716632324737476845)
XLA Ops:
  7.2 0.8 convert_bitcast_fusion.1
  8.0 0.1 copy.90
  8.1 1.0 convert_element_type.110
  9.1 1.2 convert_element_type.109
  10.4 1.1 fusion.50
  11.5 0.4 copy-done.6
  11.9 0.9 convert_element_type.113
  12.8 111.8 %all-gather.3.cloned.1.call-done = bf16[1024,8320]{1,0:T(8,128)(2,1)} async-done(((bf16[64,8320]{1,0:T(8,128)(2,1)}), bf16[1024,8320]{1,0:T(8,128)(2,1)}) %all-gather.3.cloned.1.call-update) | async-done | bytes 17039376 | tf_op jit(solution)/shard_map/all_gather | solution.py:295
  124.6 0.1 convert_reduce_fusion
  124.8 0.2 fusion.73
  125.0 0.1 fusion.90
  125.1 1.0 convert_bitcast_fusion
  126.1 0.2 slice.71
  126.3 0.2 copy.79
  126.5 2.1 slice_reduce_fusion.2
  128.6 3.9 fusion.10
  132.5 0.1 fusion.75
  132.6 0.2 copy.76
  132.8 0.2 copy.77
  133.0 0.2 copy.75
  133.2 0.4 convolution_multiply_fusion
  133.6 0.5 convolution_convert_fusion.5
  134.1 2.4 fusion.125
  136.5 0.2 multiply_reduce_fusion.4
  136.7 4.8 fusion.12
  141.5 5.6 %convolution_convert_fusion.1 = bf16[4096,1024]{1,0:T(8,128)(2,1)} fusion(bf16[128,1024]{1,0:T(8,128)(2,1)S(1)} %copy-done.4, f32[128,4096]{1,0:T(8,128)S(1)} %fusion.12), kind=kOutput, calls=%fused_computation.6 | convolution fusion | flops 1082654720 | bytes 10747904 | tf_op jit(solution)/shard_map/dot_general | solution.py:214
  147.2 0.2 reduce-scatter.3.cloned.1.call-start
  147.5 0.1 reduce_sum.191
  147.6 0.2 multiply_reduce_fusion.3
  147.8 3.0 fusion.37
  150.8 47.6 %all-gather.5.cloned.1.call-done = bf16[4096,1024]{1,0:T(8,128)(2,1)} async-done(((bf16[256,1024]{1,0:T(8,128)(2,1)}), bf16[4096,1024]{1,0:T(8,128)(2,1)}) %all-gather.5.cloned.1.call-update) | async-done | bytes 8388624 | tf_op jit(solution)/shard_map/all_gather | solution.py:297
  198.3 8.5 %fusion.120 = (bf16[4096]{0:T(1024)(128)(2,1)S(1)}, bf16[128,4096]{1,0:T(8,128)(2,1)}) fusion(f32[128,4096]{1,0:T(8,128)S(1)} %fusion.12, bf16[128,1024]{1,0:T(8,128)(2,1)S(1)} %copy-done.4, bf16[4096,1024]{1,0:T(8,128)(2,1)} %all-gather.5.cloned.1.call-done), kind=kOutput, calls=%fused_computation.173 | convolution fusion | flops 1086844928 | bytes 11804672 | tf_op jit(solution)/shard_map/dot_general | solution.py:218
  206.8 7.3 %multiply_reduce_fusion.1 = (bf16[1024]{0:T(1024)(128)(2,1)S(1)}, f32[128]{0:T(128)S(1)}, bf16[1024]{0:T(1024)(128)(2,1)S(1)}, f32[128,1024]{1,0:T(8,128)S(1)}) fusion(f32[128,1024]{1,0:T(8,128)S(1)} %get-tuple-element.32, f32[128]{0:T(128)S(1)} %fusion.101, f32[128]{0:T(128)S(1)} %broadcast_multiply_fusion.1, f32[1024]{0:T(1024)S(1)} %get-tuple-element.41, ...), kind=kOutput, calls=%fused_computation.114 | convolution fusion | flops 1074788224 | bytes 10495488 | tf_op jit(solution)/shard_map/dot_general | solution.py:223
  214.2 0.3 fusion.122
  214.4 2.6 fusion.47
  217.1 0.2 copy.80
  217.3 3.1 fusion.123
  220.5 1.3 fusion.128
  221.8 2.9 fusion.124
  224.8 2.1 convolution_convert_fusion.4
  226.9 5.2 %fusion.112 = (bf16[1024]{0:T(1024)(128)(2,1)S(1)}, f32[128]{0:T(128)S(1)}, f32[128,1024]{1,0:T(8,128)S(1)}) fusion(f32[1024]{0:T(1024)S(1)} %get-tuple-element.48, f32[128]{0:T(128)S(1)} %broadcast_multiply_fusion.3, bf16[128,1024]{1,0:T(8,128)(2,1)S(1)} %copy-done, bf16[1024,8320]{1,0:T(8,128)(2,1)} %all-gather.3.cloned.1.call-done, ...), kind=kOutput, calls=%fused_computation.172 | convolution fusion | flops 808450944 | bytes 7871488 | tf_op jit(solution)/shard_map/dot_general | solution.py:241
  232.2 0.3 fusion.72
  232.6 1.0 fusion.109
  233.7 0.2 copy.84
  233.9 2.2 convolution_convert_fusion.3
  236.1 3.2 copy.85
  239.3 3.1 convolution_convert_fusion.2
  242.4 2.5 convolution_convert_fusion
  244.8 6.6 %fusion.3 = bf16[1024,8320]{1,0:T(8,128)(2,1)} fusion(bf16[1024,12]{1,0:T(8,128)(2,1)S(1)} %bitcast.69, bf16[1024,4096]{1,0:T(8,128)(2,1)S(1)} %convolution_convert_fusion, bf16[1024,1024]{1,0:T(8,128)(2,1)S(1)} %copy.85, bf16[1024,3072]{1,0:T(8,128)(2,1)S(1)} %convolution_convert_fusion.2), kind=kLoop, calls=%fused_computation.4 | loop fusion | flops 85196800 | bytes 33841152 | tf_op jit(solution)/shard_map/concatenate | solution.py:309
  251.5 51.2 %reduce-scatter.5.cloned.1.call-done = bf16[256,1024]{1,0:T(8,128)(2,1)} async-done(((bf16[4096,1024]{1,0:T(8,128)(2,1)}), bf16[256,1024]{1,0:T(8,128)(2,1)}) %reduce-scatter.5.cloned.1.call-update) | async-done | bytes 524304 | tf_op jit(solution)/shard_map/reduce_scatter | solution.py:319
  302.7 18.3 %shard_map.346 = bf16[8,32,1024]{2,1,0:T(8,128)(2,1)} custom-call(bf16[8,32,1024]{2,1,0:T(8,128)(2,1)} %bitcast.80), custom_call_target="tpu_custom_call" | custom-call | tf_op jit(solution)/shard_map/pallas_call | solution.py:117
  321.1 1.6 convert_multiply_fusion
  322.8 0.4 copy-done.11
  323.2 0.6 copy-done.12
  323.8 2.3 multiply_subtract_fusion
  326.1 0.5 copy-done.2
  326.7 7.2 %fusion.46 = bf16[128,1024]{1,0:T(8,128)(2,1)} fusion(f32[128,1024]{1,0:T(8,128)S(1)} %get-tuple-element.32, bf16[4096,1024]{1,0:T(8,128)(2,1)} %all-gather.5.cloned.1.call-done, f32[1024]{0:T(1024)S(1)} %get-tuple-element.42, f32[128,4096]{1,0:T(8,128)S(1)} %copy-done.2), kind=kOutput, calls=%fused_computation.60 | convolution fusion | flops 1078853632 | bytes 11276288 | tf_op jit(solution)/shard_map/dot_general | solution.py:211
  333.9 120.5 %reduce-scatter.3.cloned.1.call-done = bf16[64,8320]{1,0:T(8,128)(2,1)} async-done(((bf16[1024,8320]{1,0:T(8,128)(2,1)}), bf16[64,8320]{1,0:T(8,128)(2,1)}) %reduce-scatter.3.cloned.1.call-update) | async-done | bytes 1064976 | tf_op jit(solution)/shard_map/reduce_scatter | solution.py:318
  454.3 30.5 %shard_map.345 = bf16[8,8,8320]{2,1,0:T(8,128)(2,1)} custom-call(bf16[8,8,8320]{2,1,0:T(8,128)(2,1)} %bitcast.68), custom_call_target="tpu_custom_call" | custom-call | tf_op jit(solution)/shard_map/pallas_call | solution.py:117
  484.9 1.6 multiply_subtract_fusion.4
  486.5 2.0 multiply_subtract_fusion.3
  488.5 2.1 multiply_subtract_fusion.2
  490.7 0.8 copy-done.14
  491.5 2.6 multiply_subtract_fusion.1
  (98 shorter events, 0.9 us)
Async XLA Ops:
  7.2 3.1 copy-start.8
  7.2 117.4 %all-gather.3.cloned.1.call-start = ((), (), s32[]{:S(2)}) async-start(), calls=%async_computation.2 | async-start | bytes 18104320 | tf_op jit(solution)/shard_map/all_gather | solution.py:295
  10.3 1.6 copy-start.6
  11.4 113.2 %copy-start = (bf16[128,1024]{1,0:T(8,128)(2,1)S(1)}, bf16[128,1024]{1,0:T(8,128)(2,1)}, u32[]{:S(2)}) copy-start(bf16[128,1024]{1,0:T(8,128)(2,1)} %param.18) | copy-start | bytes 786436
  11.4 113.6 %copy-start.33 = (s32[1,128]{1,0:T(1,128)S(1)}, s32[1,128]{1,0:T(1,128)}, u32[]{:S(2)}) copy-start(s32[1,128]{1,0:T(1,128)} %param.20) | copy-start | bytes 1540
  11.5 186.9 %all-gather.5.cloned.1.call-start = ((), (), s32[]{:S(2)}) async-start(), calls=%async_computation.3 | async-start | bytes 8912896 | tf_op jit(solution)/shard_map/all_gather | solution.py:297
  124.6 178.1 %reduce-scatter.5.cloned.1.call-start = ((), (), s32[]{:S(2)}) async-start(), calls=%async_computation.5 | async-start | bytes 8912896 | tf_op jit(solution)/shard_map/reduce_scatter | solution.py:319
  133.0 1.1 copy-start.18
  133.2 0.9 copy-start.20
  133.6 3.1 copy-start.17
  134.0 2.6 copy-start.23
  136.7 4.8 copy-start.4
  141.5 56.8 %copy-start.1 = (f32[128,4096]{1,0:T(8,128)}, f32[128,4096]{1,0:T(8,128)S(1)}, u32[]{:S(2)}) copy-start(f32[128,4096]{1,0:T(8,128)S(1)} %fusion.12) | copy-start | bytes 6291460
  147.2 307.2 %reduce-scatter.3.cloned.1.call-start = ((), (), s32[]{:S(2)}) async-start(), calls=%async_computation.4 | async-start | bytes 18104320 | tf_op jit(solution)/shard_map/reduce_scatter | solution.py:318
  217.1 3.4 copy-start.21
  217.1 4.7 copy-start.19
  217.3 3.1 copy-start.22
  221.8 5.1 %copy-start.29 = (bf16[1,128,16,64]{1,3,2,0:T(8,128)(2,1)S(1)}, bf16[1,128,16,64]{1,3,2,0:T(8,128)(2,1)}, u32[]{:S(2)}) copy-start(bf16[1,128,16,64]{1,3,2,0:T(8,128)(2,1)} %get-tuple-element.80) | copy-start | bytes 786436
  226.9 5.3 %copy-start.31 = (bf16[16,64,128]{2,1,0:T(8,128)(2,1)}, bf16[16,64,128]{2,1,0:T(8,128)(2,1)S(1)}, u32[]{:S(2)}) copy-start(bf16[16,64,128]{2,1,0:T(8,128)(2,1)S(1)} %convolution_convert_fusion.4) | copy-start | bytes 786436
  232.2 1.7 copy-start.24
  236.1 3.2 copy-start.30
  239.3 3.1 copy-start.15
  321.1 1.7 copy-start.7
  321.1 2.1 copy-start.11
  321.1 2.7 copy-start.12
  322.8 3.4 copy-start.5
  323.8 2.9 copy-start.2
  326.7 158.2 %copy-start.32 = (f32[12,64]{1,0:T(8,128)S(1)}, f32[12,64]{1,0:T(8,128)}, u32[]{:S(2)}) copy-start(f32[12,64]{1,0:T(8,128)} %param.25) | copy-start | bytes 9220
  326.7 158.2 %copy-start.34 = (f32[12,64]{1,0:T(8,128)S(1)}, f32[12,64]{1,0:T(8,128)}, u32[]{:S(2)}) copy-start(f32[12,64]{1,0:T(8,128)} %param.30) | copy-start | bytes 9220
  326.7 158.2 %copy-start.35 = (f32[12,64]{1,0:T(8,128)S(1)}, f32[12,64]{1,0:T(8,128)}, u32[]{:S(2)}) copy-start(f32[12,64]{1,0:T(8,128)} %param.35) | copy-start | bytes 9220
  326.7 159.8 %copy-start.27 = (f32[64,1024]{1,0:T(8,128)S(1)}, f32[64,1024]{1,0:T(8,128)}, u32[]{:S(2)}) copy-start(f32[64,1024]{1,0:T(8,128)} %param.27) | copy-start | bytes 786436
  326.7 159.8 %copy-start.28 = (f32[64,1024]{1,0:T(8,128)S(1)}, f32[64,1024]{1,0:T(8,128)}, u32[]{:S(2)}) copy-start(f32[64,1024]{1,0:T(8,128)} %param.32) | copy-start | bytes 786436
  333.8 152.6 %copy-start.16 = (f32[64,1024]{1,0:T(8,128)S(1)}, f32[64,1024]{1,0:T(8,128)}, u32[]{:S(2)}) copy-start(f32[64,1024]{1,0:T(8,128)} %param.22) | copy-start | bytes 786436
  333.8 154.6 %copy-start.10 = (f32[64,3072]{1,0:T(8,128)S(1)}, f32[64,3072]{1,0:T(8,128)}, u32[]{:S(2)}) copy-start(f32[64,3072]{1,0:T(8,128)} %param.21) | copy-start | bytes 2359300
  333.9 154.6 %copy-start.25 = (f32[64,3072]{1,0:T(8,128)S(1)}, f32[64,3072]{1,0:T(8,128)}, u32[]{:S(2)}) copy-start(f32[64,3072]{1,0:T(8,128)} %param.26) | copy-start | bytes 2359300
  333.9 154.6 %copy-start.26 = (f32[64,3072]{1,0:T(8,128)S(1)}, f32[64,3072]{1,0:T(8,128)}, u32[]{:S(2)}) copy-start(f32[64,3072]{1,0:T(8,128)} %param.31) | copy-start | bytes 2359300
  484.8 3.7 copy-start.3
  488.5 2.2 copy-start.9
  488.5 2.2 copy-start.13
  488.5 3.0 copy-start.14
Sparse Core Ops, SparseCore 0:
  11.6 112.9 all-gather.2
  127.6 70.6 all-gather.4
  202.6 100.0 reduce-scatter.4
  306.9 147.3 reduce-scatter.2

commit v10 on v9

--- a/solution.py
+++ b/solution.py
@@ -11,7 +11,7 @@
 SEQ = 128
 ADAM_STEP = 3
 LANE = 128
-CHUNKS = 4
+CHUNKS = 3
 
 
 eps_norm = 1e-05

time: 502 us -> 501 us (level)
  no operation moved by 1% of the time
where the time goes in v10:
time: 501 us; the launch traced here: 500 us
  waiting for transfers between devices  330 us (66%)
  matrix products  67 us (13%)
  Pallas kernels  49.2 us (10%)
  other arithmetic  29 us (6%)
  between operations  14.4 us (3%)
  local copies, waits for them, and re-layouts  9.97 us (2%)
    reduce_scatter x1, waiting for transfers between devices, local(): lax.psum_scatter(joined, 'zero', scatter_dimension=0, tiled=True)  120 us
    all_gather x1, waiting for transfers between devices, local(): lax.all_gather(jnp.concatenate(first_mats, axis=1), 'zero', axis=0, tiled...  112 us
    reduce_scatter x1, waiting for transfers between devices, local(): lax.psum_scatter(local_grads[3].astype(jnp.bfloat16), 'zero', scatter_dim...  51.2 us
    pallas_call x2, Pallas kernels, summed_over_dp(): pl.pallas_call(partial(dp_sum_kernel, parts, count, CHUNKS), out_shape=[j...  49.2 us
    all_gather x1, waiting for transfers between devices, local(): proj_mat = lax.all_gather(proj_shard, 'zero', axis=0, tiled=True)  47.6 us
  transfers between devices with their start and end apart: 4, of which 4 were waited for; matrix products, arithmetic and copies ran while one was open for 18% of the time, Pallas kernels for 4%

profile of v10, /device:TPU:4, one launch (start us, length us, event | category | flops | bytes accessed | tf_op | source)
XLA Modules:
  0.0 500.4 jit_solution(636034884683385167)
XLA Ops:
  7.2 0.8 convert_bitcast_fusion.1
  8.0 0.1 copy.90
  8.1 1.0 convert_element_type.110
  9.1 1.2 convert_element_type.109
  10.4 1.1 fusion.50
  11.5 0.4 copy-done.6
  11.9 0.9 convert_element_type.113
  12.8 111.8 %all-gather.3.cloned.1.call-done = bf16[1024,8320]{1,0:T(8,128)(2,1)} async-done(((bf16[64,8320]{1,0:T(8,128)(2,1)}), bf16[1024,8320]{1,0:T(8,128)(2,1)}) %all-gather.3.cloned.1.call-update) | async-done | bytes 17039376 | tf_op jit(solution)/shard_map/all_gather | solution.py:295
  124.6 0.1 convert_reduce_fusion
  124.8 0.2 fusion.73
  125.0 0.1 fusion.90
  125.1 1.0 convert_bitcast_fusion
  126.1 0.2 slice.71
  126.3 0.2 copy.79
  126.5 2.1 slice_reduce_fusion.2
  128.6 3.9 fusion.10
  132.5 0.1 fusion.75
  132.6 0.2 copy.76
  132.8 0.2 copy.77
  133.0 0.2 copy.75
  133.2 0.4 convolution_multiply_fusion
  133.6 0.5 convolution_convert_fusion.5
  134.1 2.4 fusion.125
  136.5 0.2 multiply_reduce_fusion.4
  136.7 4.8 fusion.12
  141.5 5.6 %convolution_convert_fusion.1 = bf16[4096,1024]{1,0:T(8,128)(2,1)} fusion(bf16[128,1024]{1,0:T(8,128)(2,1)S(1)} %copy-done.4, f32[128,4096]{1,0:T(8,128)S(1)} %fusion.12), kind=kOutput, calls=%fused_computation.6 | convolution fusion | flops 1082654720 | bytes 10747904 | tf_op jit(solution)/shard_map/dot_general | solution.py:214
  147.2 0.2 reduce-scatter.3.cloned.1.call-start
  147.5 0.1 reduce_sum.191
  147.6 0.2 multiply_reduce_fusion.3
  147.8 3.0 fusion.37
  150.8 47.6 %all-gather.5.cloned.1.call-done = bf16[4096,1024]{1,0:T(8,128)(2,1)} async-done(((bf16[256,1024]{1,0:T(8,128)(2,1)}), bf16[4096,1024]{1,0:T(8,128)(2,1)}) %all-gather.5.cloned.1.call-update) | async-done | bytes 8388624 | tf_op jit(solution)/shard_map/all_gather | solution.py:297
  198.3 8.5 %fusion.120 = (bf16[4096]{0:T(1024)(128)(2,1)S(1)}, bf16[128,4096]{1,0:T(8,128)(2,1)}) fusion(f32[128,4096]{1,0:T(8,128)S(1)} %fusion.12, bf16[128,1024]{1,0:T(8,128)(2,1)S(1)} %copy-done.4, bf16[4096,1024]{1,0:T(8,128)(2,1)} %all-gather.5.cloned.1.call-done), kind=kOutput, calls=%fused_computation.173 | convolution fusion | flops 1086844928 | bytes 11804672 | tf_op jit(solution)/shard_map/dot_general | solution.py:218
  206.8 7.3 %multiply_reduce_fusion.1 = (bf16[1024]{0:T(1024)(128)(2,1)S(1)}, f32[128]{0:T(128)S(1)}, bf16[1024]{0:T(1024)(128)(2,1)S(1)}, f32[128,1024]{1,0:T(8,128)S(1)}) fusion(f32[128,1024]{1,0:T(8,128)S(1)} %get-tuple-element.32, f32[128]{0:T(128)S(1)} %fusion.101, f32[128]{0:T(128)S(1)} %broadcast_multiply_fusion.1, f32[1024]{0:T(1024)S(1)} %get-tuple-element.41, ...), kind=kOutput, calls=%fused_computation.114 | convolution fusion | flops 1074788224 | bytes 10495488 | tf_op jit(solution)/shard_map/dot_general | solution.py:223
  214.2 0.3 fusion.122
  214.4 2.6 fusion.47
  217.1 0.2 copy.80
  217.3 3.1 fusion.123
  220.5 1.3 fusion.128
  221.8 2.9 fusion.124
  224.8 2.1 convolution_convert_fusion.4
  226.9 5.2 %fusion.112 = (bf16[1024]{0:T(1024)(128)(2,1)S(1)}, f32[128]{0:T(128)S(1)}, f32[128,1024]{1,0:T(8,128)S(1)}) fusion(f32[1024]{0:T(1024)S(1)} %get-tuple-element.48, f32[128]{0:T(128)S(1)} %broadcast_multiply_fusion.3, bf16[128,1024]{1,0:T(8,128)(2,1)S(1)} %copy-done, bf16[1024,8320]{1,0:T(8,128)(2,1)} %all-gather.3.cloned.1.call-done, ...), kind=kOutput, calls=%fused_computation.172 | convolution fusion | flops 808450944 | bytes 7871488 | tf_op jit(solution)/shard_map/dot_general | solution.py:241
  232.2 0.3 fusion.72
  232.6 1.0 fusion.109
  233.7 0.2 copy.84
  233.9 2.2 convolution_convert_fusion.3
  236.1 3.2 copy.85
  239.3 3.1 convolution_convert_fusion.2
  242.4 2.5 convolution_convert_fusion
  244.8 6.6 %fusion.3 = bf16[1024,8320]{1,0:T(8,128)(2,1)} fusion(bf16[1024,12]{1,0:T(8,128)(2,1)S(1)} %bitcast.69, bf16[1024,4096]{1,0:T(8,128)(2,1)S(1)} %convolution_convert_fusion, bf16[1024,1024]{1,0:T(8,128)(2,1)S(1)} %copy.85, bf16[1024,3072]{1,0:T(8,128)(2,1)S(1)} %convolution_convert_fusion.2), kind=kLoop, calls=%fused_computation.4 | loop fusion | flops 85196800 | bytes 33841152 | tf_op jit(solution)/shard_map/concatenate | solution.py:309
  251.5 51.2 %reduce-scatter.5.cloned.1.call-done = bf16[256,1024]{1,0:T(8,128)(2,1)} async-done(((bf16[4096,1024]{1,0:T(8,128)(2,1)}), bf16[256,1024]{1,0:T(8,128)(2,1)}) %reduce-scatter.5.cloned.1.call-update) | async-done | bytes 524304 | tf_op jit(solution)/shard_map/reduce_scatter | solution.py:319
  302.7 19.0 %shard_map.346 = bf16[8,32,1024]{2,1,0:T(8,128)(2,1)} custom-call(bf16[8,32,1024]{2,1,0:T(8,128)(2,1)} %bitcast.80), custom_call_target="tpu_custom_call" | custom-call | tf_op jit(solution)/shard_map/pallas_call | solution.py:117
  321.8 1.6 convert_multiply_fusion
  323.5 0.4 copy-done.11
  323.9 0.6 copy-done.12
  324.5 2.3 multiply_subtract_fusion
  326.8 0.5 copy-done.2
  327.4 7.2 %fusion.46 = bf16[128,1024]{1,0:T(8,128)(2,1)} fusion(f32[128,1024]{1,0:T(8,128)S(1)} %get-tuple-element.32, bf16[4096,1024]{1,0:T(8,128)(2,1)} %all-gather.5.cloned.1.call-done, f32[1024]{0:T(1024)S(1)} %get-tuple-element.42, f32[128,4096]{1,0:T(8,128)S(1)} %copy-done.2), kind=kOutput, calls=%fused_computation.60 | convolution fusion | flops 1078853632 | bytes 11276288 | tf_op jit(solution)/shard_map/dot_general | solution.py:211
  334.6 119.8 %reduce-scatter.3.cloned.1.call-done = bf16[64,8320]{1,0:T(8,128)(2,1)} async-done(((bf16[1024,8320]{1,0:T(8,128)(2,1)}), bf16[64,8320]{1,0:T(8,128)(2,1)}) %reduce-scatter.3.cloned.1.call-update) | async-done | bytes 1064976 | tf_op jit(solution)/shard_map/reduce_scatter | solution.py:318
  454.4 30.2 %shard_map.345 = bf16[8,8,8320]{2,1,0:T(8,128)(2,1)} custom-call(bf16[8,8,8320]{2,1,0:T(8,128)(2,1)} %bitcast.68), custom_call_target="tpu_custom_call" | custom-call | tf_op jit(solution)/shard_map/pallas_call | solution.py:117
  484.6 1.6 multiply_subtract_fusion.4
  486.2 2.0 multiply_subtract_fusion.3
  488.2 2.1 multiply_subtract_fusion.2
  490.4 0.8 copy-done.14
  491.2 2.6 multiply_subtract_fusion.1
  (98 shorter events, 0.9 us)
Async XLA Ops:
  7.2 3.1 copy-start.8
  7.2 117.4 %all-gather.3.cloned.1.call-start = ((), (), s32[]{:S(2)}) async-start(), calls=%async_computation.2 | async-start | bytes 18104320 | tf_op jit(solution)/shard_map/all_gather | solution.py:295
  10.3 1.6 copy-start.6
  11.4 113.2 %copy-start = (bf16[128,1024]{1,0:T(8,128)(2,1)S(1)}, bf16[128,1024]{1,0:T(8,128)(2,1)}, u32[]{:S(2)}) copy-start(bf16[128,1024]{1,0:T(8,128)(2,1)} %param.18) | copy-start | bytes 786436
  11.4 113.6 %copy-start.33 = (s32[1,128]{1,0:T(1,128)S(1)}, s32[1,128]{1,0:T(1,128)}, u32[]{:S(2)}) copy-start(s32[1,128]{1,0:T(1,128)} %param.20) | copy-start | bytes 1540
  11.5 186.9 %all-gather.5.cloned.1.call-start = ((), (), s32[]{:S(2)}) async-start(), calls=%async_computation.3 | async-start | bytes 8912896 | tf_op jit(solution)/shard_map/all_gather | solution.py:297
  124.6 178.1 %reduce-scatter.5.cloned.1.call-start = ((), (), s32[]{:S(2)}) async-start(), calls=%async_computation.5 | async-start | bytes 8912896 | tf_op jit(solution)/shard_map/reduce_scatter | solution.py:319
  133.0 1.1 copy-start.18
  133.2 0.9 copy-start.20
  133.6 3.1 copy-start.17
  134.0 2.6 copy-start.23
  136.7 4.8 copy-start.4
  141.5 56.8 %copy-start.1 = (f32[128,4096]{1,0:T(8,128)}, f32[128,4096]{1,0:T(8,128)S(1)}, u32[]{:S(2)}) copy-start(f32[128,4096]{1,0:T(8,128)S(1)} %fusion.12) | copy-start | bytes 6291460
  147.2 307.2 %reduce-scatter.3.cloned.1.call-start = ((), (), s32[]{:S(2)}) async-start(), calls=%async_computation.4 | async-start | bytes 18104320 | tf_op jit(solution)/shard_map/reduce_scatter | solution.py:318
  217.1 3.4 copy-start.21
  217.1 4.7 copy-start.19
  217.3 3.1 copy-start.22
  221.8 5.1 %copy-start.29 = (bf16[1,128,16,64]{1,3,2,0:T(8,128)(2,1)S(1)}, bf16[1,128,16,64]{1,3,2,0:T(8,128)(2,1)}, u32[]{:S(2)}) copy-start(bf16[1,128,16,64]{1,3,2,0:T(8,128)(2,1)} %get-tuple-element.80) | copy-start | bytes 786436
  226.9 5.3 %copy-start.31 = (bf16[16,64,128]{2,1,0:T(8,128)(2,1)}, bf16[16,64,128]{2,1,0:T(8,128)(2,1)S(1)}, u32[]{:S(2)}) copy-start(bf16[16,64,128]{2,1,0:T(8,128)(2,1)S(1)} %convolution_convert_fusion.4) | copy-start | bytes 786436
  232.2 1.7 copy-start.24
  236.1 3.2 copy-start.30
  239.3 3.1 copy-start.15
  321.8 1.7 copy-start.7
  321.8 2.1 copy-start.11
  321.8 2.7 copy-start.12
  323.5 3.4 copy-start.5
  324.5 2.9 copy-start.2
  327.4 157.2 %copy-start.32 = (f32[12,64]{1,0:T(8,128)S(1)}, f32[12,64]{1,0:T(8,128)}, u32[]{:S(2)}) copy-start(f32[12,64]{1,0:T(8,128)} %param.25) | copy-start | bytes 9220
  327.4 157.2 %copy-start.34 = (f32[12,64]{1,0:T(8,128)S(1)}, f32[12,64]{1,0:T(8,128)}, u32[]{:S(2)}) copy-start(f32[12,64]{1,0:T(8,128)} %param.30) | copy-start | bytes 9220
  327.4 157.2 %copy-start.35 = (f32[12,64]{1,0:T(8,128)S(1)}, f32[12,64]{1,0:T(8,128)}, u32[]{:S(2)}) copy-start(f32[12,64]{1,0:T(8,128)} %param.35) | copy-start | bytes 9220
  327.4 158.8 %copy-start.27 = (f32[64,1024]{1,0:T(8,128)S(1)}, f32[64,1024]{1,0:T(8,128)}, u32[]{:S(2)}) copy-start(f32[64,1024]{1,0:T(8,128)} %param.27) | copy-start | bytes 786436
  327.4 158.8 %copy-start.28 = (f32[64,1024]{1,0:T(8,128)S(1)}, f32[64,1024]{1,0:T(8,128)}, u32[]{:S(2)}) copy-start(f32[64,1024]{1,0:T(8,128)} %param.32) | copy-start | bytes 786436
  334.5 151.6 %copy-start.16 = (f32[64,1024]{1,0:T(8,128)S(1)}, f32[64,1024]{1,0:T(8,128)}, u32[]{:S(2)}) copy-start(f32[64,1024]{1,0:T(8,128)} %param.22) | copy-start | bytes 786436
  334.6 153.6 %copy-start.10 = (f32[64,3072]{1,0:T(8,128)S(1)}, f32[64,3072]{1,0:T(8,128)}, u32[]{:S(2)}) copy-start(f32[64,3072]{1,0:T(8,128)} %param.21) | copy-start | bytes 2359300
  334.6 153.6 %copy-start.25 = (f32[64,3072]{1,0:T(8,128)S(1)}, f32[64,3072]{1,0:T(8,128)}, u32[]{:S(2)}) copy-start(f32[64,3072]{1,0:T(8,128)} %param.26) | copy-start | bytes 2359300
  334.6 153.6 %copy-start.26 = (f32[64,3072]{1,0:T(8,128)S(1)}, f32[64,3072]{1,0:T(8,128)}, u32[]{:S(2)}) copy-start(f32[64,3072]{1,0:T(8,128)} %param.31) | copy-start | bytes 2359300
  484.5 3.7 copy-start.3
  488.2 2.2 copy-start.9
  488.2 2.2 copy-start.13
  488.2 3.0 copy-start.14
Sparse Core Ops, SparseCore 0:
  11.6 112.9 all-gather.2
  127.6 70.6 all-gather.4
  202.6 100.0 reduce-scatter.4
  306.9 147.3 reduce-scatter.2
